TPU v7x, 32 devices: a whole 2x2x4 slice. The times are simulated.
32 devices in a mesh: groups: 2 (over x), row: 8 (over z, y), col: 2 (over core).
Axes of the slice: x: 2, y: 2, z: 4, core: 2. Of those that a mesh axis runs over, the one named last changes fastest.
Arguments:
- features: bfloat16 [32, 8, 256, 1024], P(('groups', 'row'), 'col'), parts along dimension 0, may hold values from -6 to 6
- assignment: int32 [32, 8], P(('groups', 'row'), 'col'), parts along dimension 0, may hold values from -1 to 7, as said below
- w_reduce: bfloat16 [1024, 512], replicated, may hold values from -0.1875 to 0.1875
- w_expand: bfloat16 [512, 2048], replicated, may hold values from -0.25 to 0.25
- w_short: bfloat16 [1024, 2048], replicated, may hold values from -0.1875 to 0.1875
- w_branch: bfloat16 [2048, 256], replicated, may hold values from -0.125 to 0.125
- w_dilated: bfloat16 [9, 256, 256], replicated, may hold values from -0.125 to 0.125
Outputs:
- branch_out: bfloat16 [512, 128, 256], P(('groups', 'row'), 'col'), parts along dimension 0
There are 2 independent parts, one for each index of `groups`. A program takes and returns all parts, laid end to end along the dimension named above; an argument that names none is the same for every part. Nothing has to cross between parts.
Inputs may be any that keep to these rules, and one draw needn't show every extreme that they name: `assignment`: A value v >= 0 means the tile has tissue and is handled in slot v % 4 by the worker of the same column index whose row index is the holder's row index XOR (v // 4): the holder itself for v < 4, else its partner. Each worker handles exactly 4 tiles, one in each slot, the holder's own tissue tiles included. In every column index some device's tiles are all tissue, so that it hands 4 tiles to its partner, and that partner holds none.
All inputs are finite; a program needn't handle non-finite values.
Results may differ from a plain program's by a relative error of at most 0.0061.
Values may be sent and summed in bfloat16 or wider, within the bound.
No kernel may reach another device: no remote copies, remote signals or barrier semaphores. Data moves between devices by JAX's collectives and lax.ppermute only.
A program may use at most 64 MiB of HBM per device.

v0:
```python
import jax
import jax.numpy as jnp
from jax import lax
from jax.sharding import PartitionSpec as P

TILE = 16
RR = 18
RC = 15


def extended_2(cells, sides, width):
    for axis, dim in sides:
        count = lax.axis_size(axis)
        ends = count - 1
        head = lax.slice_in_dim(cells, 0, width, axis=dim)
        tail = lax.slice_in_dim(cells, cells.shape[dim] - width, cells.shape[dim], axis=dim)
        cells = jnp.concatenate(
            [
                lax.ppermute(tail, axis, [(i, (i + 1) % count) for i in range(ends)]),
                cells,
                lax.ppermute(head, axis, [((i + 1) % count, i) for i in range(ends)]),
            ],
            axis=dim,
        )
    return cells


def trunk(rows_in, w_reduce, w_expand, w_short, w_branch):
    hidden = jax.nn.relu(jnp.dot(rows_in, w_reduce, preferred_element_type=jnp.float32)).astype(
        jnp.bfloat16
    )
    summed = jnp.dot(hidden, w_expand, preferred_element_type=jnp.float32) + jnp.dot(
        rows_in, w_short, preferred_element_type=jnp.float32
    )
    block_out = jax.nn.relu(summed).astype(jnp.bfloat16)
    return jax.nn.relu(jnp.dot(block_out, w_branch, preferred_element_type=jnp.float32)).astype(
        jnp.bfloat16
    )


def shards(features, assignment, w_reduce, w_expand, w_short, w_branch, w_dilated):
    tile_rows, tile_cols, pixels, channels = features.shape
    tile_count = tile_rows * tile_cols
    branch_width = w_branch.shape[1]
    flat_in = features.reshape(tile_count, pixels * channels)
    tile_codes = assignment.reshape(tile_count)
    tissue = tile_codes >= 0
    reduced = trunk(
        flat_in.reshape(tile_count * pixels, channels), w_reduce, w_expand, w_short, w_branch
    )
    reduced = reduced.reshape(tile_count, pixels * branch_width)
    reduced = jnp.where(tissue[:, None], reduced, jnp.zeros_like(reduced))
    height = tile_rows * TILE
    width = tile_cols * TILE
    feature_grid = (
        reduced.reshape(tile_rows, tile_cols, TILE, TILE, branch_width)
        .transpose(0, 2, 1, 3, 4)
        .reshape(height, width, branch_width)
    )
    extended = extended_2(feature_grid, (("row", 0),), RR)
    extended = extended_2(extended, (("col", 1),), RC)
    col_margin = (extended.shape[1] - width) // 2
    windows = []
    for down_tap in range(3):
        for side_tap in range(3):
            col_start = col_margin - RC + side_tap * RC
            window = extended[down_tap * RR : down_tap * RR + height, col_start : col_start + width]
            windows.append(window.reshape(height * width, branch_width))
    stacked = jnp.concatenate(windows, axis=1)
    summed = jnp.dot(
        stacked,
        w_dilated.reshape(9 * branch_width, branch_width),
        preferred_element_type=jnp.float32,
    )
    return jax.nn.relu(summed).astype(jnp.bfloat16).reshape(height, width, branch_width)


def solution(mesh):
    in_specs = (
        P(("groups", "row"), "col", None, None),
        P(("groups", "row"), "col"),
        P(),
        P(),
        P(),
        P(),
        P(),
    )
    out_specs = P(("groups", "row"), "col", None)
    return jax.shard_map(shards, mesh=mesh, in_specs=in_specs, out_specs=out_specs, check_vma=False)
```

profile of v0, /device:TPU:9, one launch (start us, length us, event | category | flops | bytes accessed | tf_op | source)
XLA Modules:
  0.0 79.6 jit_solution(9862306816485134618)
XLA Ops:
  0.0 0.8 %broadcast_compare_fusion = pred[2,4]{1,0:T(4,128)(4,1)S(1)} fusion(s32[2,4]{1,0:T(2,128)} %param.8), kind=kLoop, calls=%fused_computation.27 | loop fusion | flops 8 | bytes 40 | tf_op jit(solution)/shard_map/ge | solution.py:47
  0.8 0.8 copy-done
  1.6 12.0 %fusion.7 = f32[2048,2048]{1,0:T(8,128)} fusion(bf16[512,2048]{1,0:T(8,128)(2,1)S(1)} %copy-done, bf16[2048,1024]{1,0:T(8,128)(2,1)} %bitcast.39, bf16[1024,512]{1,0:T(8,128)(2,1)} %param.9), kind=kOutput, calls=%fused_computation.14 | convolution fusion | flops 6444548096 | bytes 24117248 | tf_op jit(solution)/shard_map/dot_general | solution.py:32
  13.6 19.7 %fusion.6 = bf16[2048,256]{1,0:T(8,128)(2,1)S(1)} fusion(bf16[2048,256]{1,0:T(8,128)(2,1)} %param.12, f32[2048,2048]{1,0:T(8,128)} %fusion.7, bf16[2048,1024]{1,0:T(8,128)(2,1)} %bitcast.40, bf16[1024,2048]{1,0:T(8,128)(2,1)} %param.11), kind=kOutput, calls=%fused_computation.10 | convolution fusion | flops 10751049728 | bytes 27262976 | tf_op jit(solution)/shard_map/dot_general | solution.py:36
  33.2 0.1 copy_select_fusion
  33.4 0.1 fusion.12
  33.5 3.1 %collective-permute-start = (bf16[18,64,256]{2,1,0:T(8,128)(2,1)S(1)}, bf16[18,64,256]{2,1,0:T(8,128)(2,1)S(1)}, u32[]{:S(2)}, u32[]{:S(2)}) collective-permute-start(bf16[18,64,256]{2,1,0:T(8,128)(2,1)S(1)} %get-tuple-element.17), channel_id=1, source_target_pairs={{0,2},{2,4},{4,6},{6,8},{8,10},{10,12},{12,14},{1,3},{3,5},{5,7},{... | collective-permute-start | bytes 1769480 | tf_op jit(solution)/shard_map/ppermute | solution.py:19
  36.6 3.1 %collective-permute-start.1 = (bf16[18,64,256]{2,1,0:T(8,128)(2,1)S(1)}, bf16[18,64,256]{2,1,0:T(8,128)(2,1)S(1)}, u32[]{:S(2)}, u32[]{:S(2)}) collective-permute-start(bf16[18,64,256]{2,1,0:T(8,128)(2,1)S(1)} %get-tuple-element.18), channel_id=1, source_target_pairs={{2,0},{4,2},{6,4},{8,6},{10,8},{12,10},{14,12},{3,1},{5,3},{7,5},{... | collective-permute-start | bytes 1769480 | tf_op jit(solution)/shard_map/ppermute | solution.py:21
  39.7 21.6 %collective-permute-done = bf16[18,64,256]{2,1,0:T(8,128)(2,1)S(1)} collective-permute-done((bf16[18,64,256]{2,1,0:T(8,128)(2,1)S(1)}, bf16[18,64,256]{2,1,0:T(8,128)(2,1)S(1)}, u32[]{:S(2)}, u32[]{:S(2)}) %collective-permute-start) | collective-permute-done | bytes 589856 | tf_op jit(solution)/shard_map/ppermute | solution.py:19
  61.3 2.9 %collective-permute-done.1 = bf16[18,64,256]{2,1,0:T(8,128)(2,1)S(1)} collective-permute-done((bf16[18,64,256]{2,1,0:T(8,128)(2,1)S(1)}, bf16[18,64,256]{2,1,0:T(8,128)(2,1)S(1)}, u32[]{:S(2)}, u32[]{:S(2)}) %collective-permute-start.1) | collective-permute-done | bytes 589856 | tf_op jit(solution)/shard_map/ppermute | solution.py:21
  64.2 0.2 pad_maximum_fusion.3
  64.4 0.2 copy.10
  64.6 1.3 %collective-permute-start.2 = (bf16[68,15,256]{2,0,1:T(8,128)(2,1)S(1)}, bf16[68,15,256]{2,0,1:T(8,128)(2,1)S(1)}, u32[]{:S(2)}, u32[]{:S(2)}) collective-permute-start(bf16[68,15,256]{2,0,1:T(8,128)(2,1)S(1)} %copy.10), channel_id=1, source_target_pairs={{0,1},{2,3},{4,5},{6,7},{8,9},{10,11},{12,13},{14,15},{16,17},{18,... | collective-permute-start | bytes 1566728 | tf_op jit(solution)/shard_map/ppermute | solution.py:19
  65.9 0.2 copy.12
  66.1 3.1 %collective-permute-start.3 = (bf16[68,15,256]{2,0,1:T(8,128)(2,1)S(1)}, bf16[68,15,256]{2,0,1:T(8,128)(2,1)S(1)}, u32[]{:S(2)}, u32[]{:S(2)}) collective-permute-start(bf16[68,15,256]{2,0,1:T(8,128)(2,1)S(1)} %copy.12), channel_id=1, source_target_pairs={{1,0},{3,2},{5,4},{7,6},{9,8},{11,10},{13,12},{15,14},{17,16},{19,... | collective-permute-start | bytes 1566728 | tf_op jit(solution)/shard_map/ppermute | solution.py:21
  69.2 0.2 pad_maximum_fusion.1
  69.4 0.1 copy.11
  69.5 1.2 %collective-permute-done.3 = bf16[68,15,256]{2,0,1:T(8,128)(2,1)S(1)} collective-permute-done((bf16[68,15,256]{2,0,1:T(8,128)(2,1)S(1)}, bf16[68,15,256]{2,0,1:T(8,128)(2,1)S(1)}, u32[]{:S(2)}, u32[]{:S(2)}) %collective-permute-start.3) | collective-permute-done | bytes 522272 | tf_op jit(solution)/shard_map/ppermute | solution.py:21
  70.7 0.1 copy.13
  70.8 1.9 %pad_maximum_fusion = (bf16[68,79,256]{2,1,0:T(8,128)(2,1)S(1)}, bf16[68,79,256]{2,1,0:T(8,128)(2,1)S(1)}) fusion(bf16[68,15,256]{2,1,0:T(8,128)(2,1)S(1)} %copy.13, bf16[18,64,256]{2,1,0:T(8,128)(2,1)S(1)} %collective-permute-done.1, bf16[32,64,256]{2,1,0:T(8,128)(2,1)S(1)} %bitcast.28, bf16[18,64,256]{2,1,0:T(8,128)(2,1)S(1)} %collective-permute-done, ...), kind=kLoop, calls=%fused_computation.6 | loop fusion | flops 22003712 | bytes 8773632 | tf_op jit(solution)/shard_map/concatenate | solution.py:17
  72.7 1.5 %fusion.10 = (bf16[32,64,256]{2,1,0:T(8,128)(2,1)S(1)}, bf16[32,64,256]{2,1,0:T(8,128)(2,1)S(1)}, bf16[32,64,256]{2,1,0:T(8,128)(2,1)S(1)}, bf16[32,64,256]{2,1,...) fusion(bf16[68,79,256]{2,1,0:T(8,128)(2,1)S(1)} %get-tuple-element.11, ...), kind=kLoop, calls=%fused_computation.30 | loop fusion | bytes 12582912 | tf_op jit(solution)/shard_map/slice | solution.py:67
  74.3 0.1 constant_dynamic-update-slice_fusion.7
  74.9 0.9 %copy-done.1 = bf16[9,256,256]{2,1,0:T(8,128)(2,1)S(1)} copy-done((bf16[9,256,256]{2,1,0:T(8,128)(2,1)S(1)}, bf16[9,256,256]{2,1,0:T(8,128)(2,1)}, u32[]{:S(2)}) %copy-start.1) | copy-done | bytes 1179672
  75.9 3.7 %fusion.5 = bf16[2048,256]{1,0:T(8,128)(2,1)} fusion(bf16[2048,2304]{1,0:T(8,128)(2,1)S(1)} %constant_dynamic-update-slice_fusion, bf16[2304,256]{1,0:T(8,128)(2,1)S(1)} %bitcast.41), kind=kOutput, calls=%fused_computation.9 | convolution fusion | flops 2416967680 | bytes 11665408 | tf_op jit(solution)/shard_map/dot_general | solution.py:70
  (11 shorter events, 0.6 us)
Async XLA Ops:
  0.0 1.6 %copy-start = (bf16[512,2048]{1,0:T(8,128)(2,1)S(1)}, bf16[512,2048]{1,0:T(8,128)(2,1)}, u32[]{:S(2)}) copy-start(bf16[512,2048]{1,0:T(8,128)(2,1)} %param.10) | copy-start | bytes 6291460
  33.5 27.8 %collective-permute-start = (bf16[18,64,256]{2,1,0:T(8,128)(2,1)S(1)}, bf16[18,64,256]{2,1,0:T(8,128)(2,1)S(1)}, u32[]{:S(2)}, u32[]{:S(2)}) collective-permute-start(bf16[18,64,256]{2,1,0:T(8,128)(2,1)S(1)} %get-tuple-element.17), channel_id=1, source_target_pairs={{0,2},{2,4},{4,6},{6,8},{8,10},{10,12},{12,14},{1,3},{3,5},{5,7},{... | collective-permute-start | bytes 1769480 | tf_op jit(solution)/shard_map/ppermute | solution.py:19
  36.6 27.5 %collective-permute-start.1 = (bf16[18,64,256]{2,1,0:T(8,128)(2,1)S(1)}, bf16[18,64,256]{2,1,0:T(8,128)(2,1)S(1)}, u32[]{:S(2)}, u32[]{:S(2)}) collective-permute-start(bf16[18,64,256]{2,1,0:T(8,128)(2,1)S(1)} %get-tuple-element.18), channel_id=1, source_target_pairs={{2,0},{4,2},{6,4},{8,6},{10,8},{12,10},{14,12},{3,1},{5,3},{7,5},{... | collective-permute-start | bytes 1769480 | tf_op jit(solution)/shard_map/ppermute | solution.py:21
  64.6 4.8 %collective-permute-start.2 = (bf16[68,15,256]{2,0,1:T(8,128)(2,1)S(1)}, bf16[68,15,256]{2,0,1:T(8,128)(2,1)S(1)}, u32[]{:S(2)}, u32[]{:S(2)}) collective-permute-start(bf16[68,15,256]{2,0,1:T(8,128)(2,1)S(1)} %copy.10), channel_id=1, source_target_pairs={{0,1},{2,3},{4,5},{6,7},{8,9},{10,11},{12,13},{14,15},{16,17},{18,... | collective-permute-start | bytes 1566728 | tf_op jit(solution)/shard_map/ppermute | solution.py:19
  66.1 4.6 %collective-permute-start.3 = (bf16[68,15,256]{2,0,1:T(8,128)(2,1)S(1)}, bf16[68,15,256]{2,0,1:T(8,128)(2,1)S(1)}, u32[]{:S(2)}, u32[]{:S(2)}) collective-permute-start(bf16[68,15,256]{2,0,1:T(8,128)(2,1)S(1)} %copy.12), channel_id=1, source_target_pairs={{1,0},{3,2},{5,4},{7,6},{9,8},{11,10},{13,12},{15,14},{17,16},{19,... | collective-permute-start | bytes 1566728 | tf_op jit(solution)/shard_map/ppermute | solution.py:21
  74.6 1.3 %copy-start.1 = (bf16[9,256,256]{2,1,0:T(8,128)(2,1)S(1)}, bf16[9,256,256]{2,1,0:T(8,128)(2,1)}, u32[]{:S(2)}) copy-start(bf16[9,256,256]{2,1,0:T(8,128)(2,1)} %param.13) | copy-start | bytes 3538948
where the time goes:
time: 79.8 us; the launch traced here: 79.6 us
  matrix products  35.3 us (44%)
  waiting for transfers between devices  25.7 us (32%)
  starting transfers between devices  10.6 us (13%)
  local copies, waits for them, and re-layouts  4.53 us (6%)
  other arithmetic  3.25 us (4%)
    ppermute x2, waiting for transfers between devices, extended_2(): lax.ppermute(tail, axis, [(i, (i + 1) % count) for i in range(ends)])  21.6 us
    dot_general x1, matrix products, trunk(): jnp.dot(block_out, w_branch, preferred_element_type=jnp.float32)  19.7 us
    dot_general x1, matrix products, trunk(): jnp.dot(hidden, w_expand, preferred_element_type=jnp.float32)  12 us
    ppermute x2, starting transfers between devices, extended_2(): lax.ppermute(head, axis, [((i + 1) % count, i) for i in range(ends)])  6.15 us
    ppermute x2, starting transfers between devices, extended_2(): lax.ppermute(tail, axis, [(i, (i + 1) % count) for i in range(ends)])  4.42 us
    ppermute x2, waiting for transfers between devices, extended_2(): lax.ppermute(head, axis, [((i + 1) % count, i) for i in range(ends)])  4.12 us
    dot_general x1, matrix products, shards(): jnp.dot(stacked, w_dilated.reshape(9 * branch_width, branch_width), prefe...  3.69 us
    unnamed x12, local copies, waits for them, and re-layouts  2.29 us
  transfers between devices with their start and end apart: 4, of which 3 were waited for; matrix products, arithmetic and copies ran while one was open for 1% of the time, Pallas kernels for 0%

commit v1 on v0

v1 whole, which is shorter than its diff:
```python
import functools

import jax
import jax.numpy as jnp
from jax import lax
from jax.experimental import pallas as pl
from jax.experimental.pallas import tpu as pltpu
from jax.sharding import PartitionSpec as P


TILE = 16
RR = 18
RC = 15
F32 = jnp.float32
BF16 = jnp.bfloat16
VM = pl.BlockSpec(memory_space=pltpu.VMEM)
SM = pl.BlockSpec(memory_space=pltpu.SMEM)
HBM = pl.BlockSpec(memory_space=pltpu.MemorySpace.HBM)
MIB = 1 << 20
TRUNK_MIB = 16


def params(mib):
    return pltpu.CompilerParams(vmem_limit_bytes=mib * MIB)


def cost(flops, nbytes):
    return pl.CostEstimate(flops=int(flops), bytes_accessed=int(nbytes), transcendentals=0)


def pieces_of(cols, top, tile_rows):
    found = []
    for tr in range(tile_rows):
        first, last = tr * TILE, (tr + 1) * TILE
        lo, hi = (first, min(last, RR)) if top else (max(first, RR), last)
        if hi > lo:
            found += [(tr, tc, lo - first, hi - lo) for tc in cols]
    return found


def trunk_rows(x, wr, we, ws, wb, ready):
    block = 512
    ready(0)
    hidden = jnp.maximum(jnp.dot(x, wr[...], preferred_element_type=F32), 0).astype(BF16)
    total = None
    for k, at in enumerate(range(0, we.shape[1], block)):
        ready(1 + k)
        summed = jnp.dot(hidden, we[:, at : at + block], preferred_element_type=F32)
        summed = summed + jnp.dot(x, ws[:, at : at + block], preferred_element_type=F32)
        block_out = jnp.maximum(summed, 0).astype(BF16)
        term = jnp.dot(block_out, wb[at : at + block, :], preferred_element_type=F32)
        total = term if total is None else total + term
    return jnp.maximum(total, 0)


def put_rows(reduced, pieces, cols, row_base, flags, out):
    at = 0
    for tr, tc, first, count in pieces:
        part = reduced[at : at + count * TILE]
        part = jnp.where(flags[tr, tc] >= 0, part, 0.0).astype(BF16)
        where = cols.index(tc) * TILE
        start = tr * TILE + first - row_base
        out[start : start + count, where : where + TILE, :] = part.reshape(count, TILE, part.shape[-1])
        at += count * TILE


def first_chunk(chunks, cols, flags, feats, wr_h, we_h, ws_h, wb_h, out, xs, wr, we, ws, wb, sems):
    block = 512
    copies = []

    def go(src, dst):
        copy = pltpu.make_async_copy(src, dst, sems.at[len(copies)])
        copy.start()
        copies.append(copy)

    at = 0
    spans = []
    for pieces in chunks:
        start = len(copies)
        for tr, tc, first, count in pieces:
            go(feats.at[tr, tc, pl.ds(first * TILE, count * TILE), :], xs.at[pl.ds(at, count * TILE), :])
            at += count * TILE
        spans.append((start, len(copies)))
        if len(spans) == 1:
            groups = [[len(copies)]]
            go(wr_h, wr)
            for k in range(0, we.shape[1], block):
                groups.append([len(copies) + j for j in range(3)])
                go(we_h.at[:, pl.ds(k, block)], we.at[:, pl.ds(k, block)])
                go(ws_h.at[:, pl.ds(k, block)], ws.at[:, pl.ds(k, block)])
                go(wb_h.at[pl.ds(k, block), :], wb.at[pl.ds(k, block), :])

    def ready(k):
        for j in groups[k]:
            copies[j].wait()

    for j in range(*spans[0]):
        copies[j].wait()
    rows = sum(p[3] for p in chunks[0]) * TILE
    reduced = trunk_rows(xs[0:rows, :], wr, we, ws, wb, ready)
    put_rows(reduced, chunks[0], cols, 0, flags, out)
    for span in spans[1:]:
        for j in range(*span):
            copies[j].wait()


def later_chunk(pieces, cols, at, top, flags, xs, wr, we, ws, wb, *refs):
    out = refs[-1]
    rows = sum(p[3] for p in pieces) * TILE
    reduced = trunk_rows(xs[at : at + rows, :], wr, we, ws, wb, lambda k: None)
    base = 0 if top else out_base(out)
    put_rows(reduced, pieces, cols, base, flags, out)
    if not top:
        head = refs[0]
        out[0 : RR - base, :, :] = head[base:RR, :, :]


def out_base(out):
    return 2 * TILE - out.shape[0]


def conv_kernel(flags, w, te, be, tm, bm, hte, hbe, htm, hbm_, xs, out, ext):
    rows, width = out.shape[0], out.shape[1]
    br = w.shape[1]
    base = rows - RR
    n_edge = te.shape[1] // 2

    def lay(at, count, src_e, src_m, first):
        ext[at : at + count, TILE : TILE + n_edge, :] = src_e[first : first + count, 0:n_edge, :]
        ext[at : at + count, TILE + n_edge : TILE + width - n_edge, :] = src_m[first : first + count, :, :]
        ext[at : at + count, TILE + width - n_edge : TILE + width, :] = src_e[first : first + count, n_edge:, :]

    lay(0, RR, hte, htm, 0)
    lay(RR, RR, te, tm, 0)
    lay(2 * RR, rows - RR, be, bm, RR - base)
    lay(RR + rows, RR, hbe, hbm_, 0)

    zero = jnp.zeros((rows + 2 * RR, TILE, br), BF16)
    for side, at in ((0, 0), (1, TILE + width)):
        @pl.when(flags[side] != 0)
        def _():
            ext[0:RR, at : at + TILE, :] = xs[0:RR]
            ext[RR : 2 * RR, at : at + TILE, :] = xs[RR : 2 * RR]
            ext[2 * RR : RR + rows, at : at + TILE, :] = xs[2 * RR + RR - base : 3 * RR]
            ext[RR + rows :, at : at + TILE, :] = xs[3 * RR : 4 * RR]

        @pl.when(flags[side] == 0)
        def _():
            ext[:, at : at + TILE, :] = zero

    step = 8
    for r in range(0, rows, step):
        total = None
        for a in range(3):
            for b in range(3):
                left = TILE - RC + b * RC
                window = ext[r + a * RR : r + a * RR + step, left : left + width, :]
                term = jnp.dot(window.reshape(step * width, br), w[3 * a + b], preferred_element_type=F32)
                total = term if total is None else total + term
        out[r : r + step] = jnp.maximum(total, 0).astype(BF16).reshape(step, width, br)


def shards(features, assignment, w_reduce, w_expand, w_short, w_branch, w_dilated):
    tile_rows, tile_cols, _, channels = features.shape
    mid, cout, br = w_reduce.shape[1], w_expand.shape[1], w_branch.shape[1]
    height, width = tile_rows * TILE, tile_cols * TILE
    edge = [0, tile_cols - 1]
    middle = list(range(1, tile_cols - 1))
    sets = [(edge, True), (edge, False), (middle, True), (middle, False)]
    chunks = [pieces_of(cols, top, tile_rows) for cols, top in sets]
    sizes = [sum(p[3] for p in c) * TILE for c in chunks]
    starts = [sum(sizes[:i]) for i in range(len(sizes))]
    per_row = 2 * (channels * mid + mid * cout + channels * cout + cout * br)
    n_copies = sum(len(c) for c in chunks) + 1 + 3 * (cout // 512)

    def grid_of(cols):
        return jax.ShapeDtypeStruct((RR, len(cols) * TILE, br), BF16)

    te, xs, wr, we, ws, wb = pl.pallas_call(
        functools.partial(first_chunk, chunks, edge),
        out_shape=[
            grid_of(edge),
            jax.ShapeDtypeStruct((sum(sizes), channels), BF16),
            jax.ShapeDtypeStruct(w_reduce.shape, BF16),
            jax.ShapeDtypeStruct(w_expand.shape, BF16),
            jax.ShapeDtypeStruct(w_short.shape, BF16),
            jax.ShapeDtypeStruct(w_branch.shape, BF16),
        ],
        in_specs=[SM] + [HBM] * 5,
        out_specs=[VM] * 6,
        scratch_shapes=[pltpu.SemaphoreType.DMA((n_copies,))],
        compiler_params=params(TRUNK_MIB),
        cost_estimate=cost(per_row * sizes[0], 12 * MIB),
        name="trunk_first",
    )(
        assignment,
        *[
            pltpu.with_memory_space_constraint(v, pltpu.MemorySpace.HBM)
            for v in (features, w_reduce, w_expand, w_short, w_branch)
        ],
    )

    def later(i, *extra):
        cols, top = sets[i]
        return pl.pallas_call(
            functools.partial(later_chunk, chunks[i], cols, starts[i], top),
            out_shape=grid_of(cols),
            in_specs=[SM] + [VM] * (5 + len(extra)),
            out_specs=VM,
            compiler_params=params(TRUNK_MIB),
            cost_estimate=cost(per_row * sizes[i], MIB),
        )(assignment, xs, wr, we, ws, wb, *extra)

    rows_n = lax.axis_size("row")
    up = [(i + 1, i) for i in range(rows_n - 1)]
    down = [(i, i + 1) for i in range(rows_n - 1)]

    hbe = lax.ppermute(te, "row", up)
    be = later(1, te)
    hte = lax.ppermute(be, "row", down)
    tm = later(2)
    hbm_ = lax.ppermute(tm, "row", up)
    bm = later(3, tm)
    htm = lax.ppermute(bm, "row", down)

    cols_n = lax.axis_size("col")
    me = lax.axis_index("col")
    half = len(edge) * TILE // 2
    mine = jnp.concatenate([hte, te, be, hbe], axis=0)
    sent = jnp.where(me == 0, mine[:, half:], mine[:, :half])
    xside = lax.ppermute(sent, "col", [(0, 1), (1, 0)])
    flags = jnp.stack([me > 0, me < cols_n - 1]).astype(jnp.int32)

    return pl.pallas_call(
        conv_kernel,
        out_shape=jax.ShapeDtypeStruct((height, width, br), BF16),
        in_specs=[SM] + [VM] * 10,
        out_specs=VM,
        scratch_shapes=[pltpu.VMEM((height + 2 * RR, width + 2 * TILE, br), BF16)],
        compiler_params=params(24),
        cost_estimate=cost(2 * height * width * 9 * br * br, 6 * MIB),
        name="dilated",
    )(flags, w_dilated, te, be, tm, bm, hte, hbe, htm, hbm_, xside)


def solution(mesh):
    in_specs = (
        P(("groups", "row"), "col", None, None),
        P(("groups", "row"), "col"),
        P(),
        P(),
        P(),
        P(),
        P(),
    )
    out_specs = P(("groups", "row"), "col", None)

    return jax.shard_map(shards, mesh=mesh, in_specs=in_specs, out_specs=out_specs, check_vma=False)
```

time: 79.8 us -> 64.3 us (0.81)
  matrix products: 35.3 us -> 0 us
  Pallas kernels: 0 us -> 29.7 us
  waiting for transfers between devices: 25.7 us -> 11.9 us
  local copies, waits for them, and re-layouts: 4.53 us -> 7.9 us
  starting transfers between devices: 10.6 us -> 12.9 us
  other arithmetic: 3.25 us -> 1.1 us
    dot_general x3 -> x0, matrix products: 35.3 us -> none  [the longest x1 19.7 us: trunk(): jnp.dot(block_out, w_branch, preferred_element_type=jnp.float32)]
    pallas_call x0 -> x5, Pallas kernels: none -> 29.7 us  [the longest x3 15.2 us: later(): pl.pallas_call(functools.partial(later_chunk, chunks[i], cols, starts[i],...]
    ppermute x4 -> x5, waiting for transfers between devices: 25.7 us -> 11.9 us  [the longest x1 9.9 us: shards(): htm = lax.ppermute(bm, 'row', down)]
    unnamed x12 -> x28, local copies, waits for them, and re-layouts: 2.29 us -> 7.9 us
    ppermute x4 -> x5, starting transfers between devices: 10.6 us -> 12.9 us  [the longest x1 4.05 us: shards(): htm = lax.ppermute(bm, 'row', down)]
    concatenate x3 -> x1, other arithmetic: 2.27 us -> 0.15 us  [shards(): mine = jnp.concatenate([hte, te, be, hbe], axis=0)]
    slice x4 -> x0, local copies, waits for them, and re-layouts: 1.95 us -> none  [the longest x1 1.5 us: shards(): extended[down_tap * RR:down_tap * RR + height, col_start:col_start + width]]
    ge x1 -> x0, other arithmetic: 0.83 us -> none  [shards(): tissue = tile_codes >= 0]
  transfers between devices with their start and end apart: 4 -> 5, of which waited for: 3 -> 2; matrix products, arithmetic and copies ran while one was open for 1% -> 0% of each run, Pallas kernels for 0% -> 24%
where the time goes in v1:
time: 64.3 us; the launch traced here: 63.7 us
  Pallas kernels  29.7 us (46%)
  starting transfers between devices  12.9 us (20%)
  waiting for transfers between devices  11.9 us (19%)
  local copies, waits for them, and re-layouts  7.9 us (12%)
  other arithmetic  1.1 us (2%)
    pallas_call x3, Pallas kernels, later(): pl.pallas_call(functools.partial(later_chunk, chunks[i], cols, starts[i],...  15.2 us
    ppermute x1, waiting for transfers between devices, shards(): htm = lax.ppermute(bm, 'row', down)  9.9 us
    pallas_call x1, Pallas kernels, shards(): pl.pallas_call(functools.partial(first_chunk, chunks, edge), out_shape=[g...  9.64 us
    unnamed x28, local copies, waits for them, and re-layouts  7.9 us
    pallas_call x1, Pallas kernels, shards(): pl.pallas_call(conv_kernel, out_shape=jax.ShapeDtypeStruct((height, width...  4.89 us
    ppermute x1, starting transfers between devices, shards(): htm = lax.ppermute(bm, 'row', down)  4.05 us
    ppermute x1, starting transfers between devices, shards(): hbe = lax.ppermute(te, 'row', up)  3.04 us
    ppermute x1, starting transfers between devices, shards(): hte = lax.ppermute(be, 'row', down)  2.43 us
  transfers between devices with their start and end apart: 5, of which 2 were waited for; matrix products, arithmetic and copies ran while one was open for 0% of the time, Pallas kernels for 24%

profile of v1, /device:TPU:9, one launch (start us, length us, event | category | flops | bytes accessed | tf_op | source)
XLA Modules:
  0.0 63.7 jit_solution(995630177774774376)
XLA Ops:
  0.0 0.7 %copy-done.1 = s32[2,4]{1,0:T(2,128)S(1)} copy-done((s32[2,4]{1,0:T(2,128)S(1)}, s32[2,4]{1,0:T(2,128)}, u32[]{:S(2)}) %copy-start.1) | copy-done | bytes 56
  0.7 9.6 %trunk_first.1 = (bf16[18,32,256]{2,1,0:T(8,128)(2,1)S(1)}, bf16[2048,1024]{1,0:T(8,128)(2,1)S(1)}, bf16[1024,512]{1,0:T(8,128)(2,1)S(1)}, bf16[512,2048]{1,0:T(...) custom-call(s32[2,4]{1,0:T(2,128)S(1)} %copy-done.1, bf16[2,4,256,1024]{3,2,1,0:T(8,128)(2,1)} %feats.1, ...), custom_call_target="tpu_custom_call" | custom-call | flops 4831838208 | bytes 12582912 | tf_op jit(solution)/shard_map/trunk_first/pallas_call | solution.py:179
  10.4 0.0 copy-start.12
  10.4 3.0 %collective-permute-start.1 = (bf16[18,32,256]{2,1,0:T(8,128)(2,1)S(1)}, bf16[18,32,256]{2,1,0:T(8,128)(2,1)S(1)}, u32[]{:S(2)}, u32[]{:S(2)}) collective-permute-start(bf16[18,32,256]{2,1,0:T(8,128)(2,1)S(1)} %get-tuple-element.11.refs_0_.te), channel_id=1, source_target_pairs={{2,0},{4,2},{6,4},{8,6},{10,8},{12,10},{14,12},{3,1},{5,3},{7,5},{... | collective-permute-start | bytes 884744 | tf_op jit(solution)/shard_map/ppermute | solution.py:218
  13.4 0.0 copy-start.2
  13.4 4.7 %shard_map.73.be = bf16[18,32,256]{2,1,0:T(8,128)(2,1)S(1)} custom-call(s32[2,4]{1,0:T(2,128)S(1)} %copy-done.1, bf16[2048,1024]{1,0:T(8,128)(2,1)S(1)} %get-tuple-element.12.xs, bf16[1024,512]{1,0:T(8,128)(2,1)S(1)} %get-tuple-element.13.wr, bf16[512,2048]{1,0:T(8,128)(2,1)S(1)} %get-tuple-element.14.we, bf16[1024,2048]{1,0:T(8,128)(2,1)S(1)} %get-tuple-element.15.ws, ...), custom_call_target="tpu_custom_call" | custom-call | flops 3758096384 | bytes 1048576 | tf_op jit(solution)/shard_map/pallas_call | solution.py:205
  18.2 2.4 %collective-permute-start = (bf16[18,32,256]{2,1,0:T(8,128)(2,1)S(1)}, bf16[18,32,256]{2,1,0:T(8,128)(2,1)S(1)}, u32[]{:S(2)}, u32[]{:S(2)}) collective-permute-start(bf16[18,32,256]{2,1,0:T(8,128)(2,1)S(1)} %shard_map.73.be), channel_id=1, source_target_pairs={{0,2},{2,4},{4,6},{6,8},{8,10},{10,12},{12,14},{1,3},{3,5},{5,7},{... | collective-permute-start | bytes 884744 | tf_op jit(solution)/shard_map/ppermute | solution.py:220
  20.7 2.2 %copy-done.4 = bf16[2048,1024]{1,0:T(8,128)(2,1)S(1)} copy-done((bf16[2048,1024]{1,0:T(8,128)(2,1)S(1)}, bf16[2048,1024]{1,0:T(8,128)(2,1)}, u32[]{:S(2)}) %copy-start.4) | copy-done | bytes 4194328
  22.8 2.2 %copy-done.7 = bf16[1024,2048]{1,0:T(8,128)(2,1)S(1)} copy-done((bf16[1024,2048]{1,0:T(8,128)(2,1)S(1)}, bf16[1024,2048]{1,0:T(8,128)(2,1)}, u32[]{:S(2)}) %copy-start.7) | copy-done | bytes 4194328
  25.0 1.6 %copy-done.9 = bf16[512,2048]{1,0:T(8,128)(2,1)S(1)} copy-done((bf16[512,2048]{1,0:T(8,128)(2,1)S(1)}, bf16[512,2048]{1,0:T(8,128)(2,1)}, u32[]{:S(2)}) %copy-start.9) | copy-done | bytes 2097176
  26.6 1.2 %copy-done.13 = bf16[2048,256]{1,0:T(8,128)(2,1)S(1)} copy-done((bf16[2048,256]{1,0:T(8,128)(2,1)S(1)}, bf16[2048,256]{1,0:T(8,128)(2,1)}, u32[]{:S(2)}) %copy-start.13) | copy-done | bytes 1048600
  27.8 5.8 %shard_map.74.refs_0_.tm = bf16[18,32,256]{2,1,0:T(8,128)(2,1)S(1)} custom-call(s32[2,4]{1,0:T(2,128)S(1)} %copy-done.2, bf16[2048,1024]{1,0:T(8,128)(2,1)S(1)} %copy-done.4, bf16[1024,512]{1,0:T(8,128)(2,1)S(1)} %get-tuple-element.13.wr, bf16[512,2048]{1,0:T(8,128)(2,1)S(1)} %copy-done.9, bf16[1024,2048]{1,0:T(8,128)(2,1)S(1)} %copy-done.7, ...), custom_call_target="tpu_custom_call" | custom-call | flops 4831838208 | bytes 1048576 | tf_op jit(solution)/shard_map/pallas_call | solution.py:205
  33.6 0.0 collective-permute-done.hte
  33.6 0.0 collective-permute-done.1.hbe
  33.6 0.2 pad_maximum_fusion
  33.8 0.9 %slice_select_fusion = bf16[72,16,256]{2,1,0:T(8,128)(2,1)} fusion(bf16[72,32,256]{2,1,0:T(8,128)(2,1)S(1)} %pad_maximum_fusion, pred[]{:T(512)S(6)} %eq.3), kind=kLoop, calls=%fused_computation.1 | loop fusion | flops 294912 | bytes 1769473 | tf_op jit(solution)/shard_map/jit(_where)/select_n | solution.py:230
  34.7 1.2 %collective-permute-start.4 = (bf16[72,16,256]{2,1,0:T(8,128)(2,1)}, bf16[72,16,256]{2,1,0:T(8,128)(2,1)S(1)}, u32[]{:S(2)}, u32[]{:S(2)}) collective-permute-start(bf16[72,16,256]{2,1,0:T(8,128)(2,1)} %slice_select_fusion), channel_id=1, source_target_pairs={{0,1},{1,0},{2,3},{3,2},{4,5},{5,4},{6,7},{7,6},{8,9},{9,8},{10,11... | collective-permute-start | bytes 1769480 | tf_op jit(solution)/shard_map/ppermute | solution.py:231
  35.9 4.7 %shard_map.75.bm = bf16[18,32,256]{2,1,0:T(8,128)(2,1)S(1)} custom-call(s32[2,4]{1,0:T(2,128)S(1)} %copy-done.2, bf16[2048,1024]{1,0:T(8,128)(2,1)S(1)} %copy-done.5, bf16[1024,512]{1,0:T(8,128)(2,1)S(1)} %copy-done.11, bf16[512,2048]{1,0:T(8,128)(2,1)S(1)} %copy-done.9, bf16[1024,2048]{1,0:T(8,128)(2,1)S(1)} %copy-done.7, bf16[2048,256]{1,0:T(8,128)(2,1)S(1)} %copy-done.13, ...), custom_call_target="tpu_custom_call" | custom-call | flops 3758096384 | bytes 1048576 | tf_op jit(solution)/shard_map/pallas_call | solution.py:205
  40.6 4.1 %collective-permute-start.2 = (bf16[18,32,256]{2,1,0:T(8,128)(2,1)S(1)}, bf16[18,32,256]{2,1,0:T(8,128)(2,1)}, u32[]{:S(2)}, u32[]{:S(2)}) collective-permute-start(bf16[18,32,256]{2,1,0:T(8,128)(2,1)S(1)} %shard_map.75.bm), channel_id=1, source_target_pairs={{0,2},{2,4},{4,6},{6,8},{8,10},{10,12},{12,14},{1,3},{3,5},{5,7},{... | collective-permute-start | bytes 884744 | tf_op jit(solution)/shard_map/ppermute | solution.py:224
  44.7 2.1 %collective-permute-start.3 = (bf16[18,32,256]{2,1,0:T(8,128)(2,1)S(1)}, bf16[18,32,256]{2,1,0:T(8,128)(2,1)}, u32[]{:S(2)}, u32[]{:S(2)}) collective-permute-start(bf16[18,32,256]{2,1,0:T(8,128)(2,1)S(1)} %shard_map.74.refs_0_.tm), channel_id=1, source_target_pairs={{2,0},{4,2},{6,4},{8,6},{10,8},{12,10},{14,12},{3,1},{5,3},{7,5},{... | collective-permute-start | bytes 884744 | tf_op jit(solution)/shard_map/ppermute | solution.py:222
  46.8 0.1 add_convert_fusion.flags
  46.9 9.9 %collective-permute-done.2.htm = bf16[18,32,256]{2,1,0:T(8,128)(2,1)} collective-permute-done((bf16[18,32,256]{2,1,0:T(8,128)(2,1)S(1)}, bf16[18,32,256]{2,1,0:T(8,128)(2,1)}, u32[]{:S(2)}, u32[]{:S(2)}) %collective-permute-start.2) | collective-permute-done | bytes 294944 | tf_op jit(solution)/shard_map/ppermute | solution.py:224
  56.8 2.0 %collective-permute-done.3.hbm_ = bf16[18,32,256]{2,1,0:T(8,128)(2,1)} collective-permute-done((bf16[18,32,256]{2,1,0:T(8,128)(2,1)S(1)}, bf16[18,32,256]{2,1,0:T(8,128)(2,1)}, u32[]{:S(2)}, u32[]{:S(2)}) %collective-permute-start.3) | collective-permute-done | bytes 294944 | tf_op jit(solution)/shard_map/ppermute | solution.py:222
  58.8 4.9 %dilated.1 = bf16[32,64,256]{2,1,0:T(8,128)(2,1)} custom-call(s32[2]{0:T(128)S(1)} %add_convert_fusion.flags, bf16[9,256,256]{2,1,0:T(8,128)(2,1)S(1)} %copy-done, bf16[18,32,256]{2,1,0:T(8,128)(2,1)S(1)} %get-tuple-element.11.refs_0_.te, bf16[18,32,256]{2,1,0:T(8,128)(2,1)S(1)} %shard_map.73.be, bf16[18,32,256]{2,1,0:T(8,128)(2,1)S(1)} %shard_map.74.refs_0_.tm, ...), custom_call_target="tpu_custom_call" | custom-call | flops 2415919104 | bytes 6291456 | tf_op jit(solution)/shard_map/dilated/pallas_call | solution.py:234
  (22 shorter events, 0.0 us)
Async XLA Ops:
  0.0 0.7 %copy-start.1 = (s32[2,4]{1,0:T(2,128)S(1)}, s32[2,4]{1,0:T(2,128)}, u32[]{:S(2)}) copy-start(s32[2,4]{1,0:T(2,128)} %flags.7) | copy-start | bytes 100
  10.3 7.8 %copy-start.3 = (bf16[2048,1024]{1,0:T(8,128)(2,1)}, bf16[2048,1024]{1,0:T(8,128)(2,1)S(1)}, u32[]{:S(2)}) copy-start(bf16[2048,1024]{1,0:T(8,128)(2,1)S(1)} %get-tuple-element.12.xs) | copy-start | bytes 12582916
  10.3 7.8 %copy-start.6 = (bf16[1024,2048]{1,0:T(8,128)(2,1)}, bf16[1024,2048]{1,0:T(8,128)(2,1)S(1)}, u32[]{:S(2)}) copy-start(bf16[1024,2048]{1,0:T(8,128)(2,1)S(1)} %get-tuple-element.15.ws) | copy-start | bytes 12582916
  10.3 7.8 %copy-start.8 = (bf16[512,2048]{1,0:T(8,128)(2,1)}, bf16[512,2048]{1,0:T(8,128)(2,1)S(1)}, u32[]{:S(2)}) copy-start(bf16[512,2048]{1,0:T(8,128)(2,1)S(1)} %get-tuple-element.14.we) | copy-start | bytes 6291460
  10.4 7.8 %copy-start.12 = (bf16[2048,256]{1,0:T(8,128)(2,1)}, bf16[2048,256]{1,0:T(8,128)(2,1)S(1)}, u32[]{:S(2)}) copy-start(bf16[2048,256]{1,0:T(8,128)(2,1)S(1)} %get-tuple-element.16.wb) | copy-start | bytes 3145732
  10.4 10.3 %copy-start.10 = (bf16[1024,512]{1,0:T(8,128)(2,1)}, bf16[1024,512]{1,0:T(8,128)(2,1)S(1)}, u32[]{:S(2)}) copy-start(bf16[1024,512]{1,0:T(8,128)(2,1)S(1)} %get-tuple-element.13.wr) | copy-start | bytes 3145732
  10.4 23.2 %collective-permute-start.1 = (bf16[18,32,256]{2,1,0:T(8,128)(2,1)S(1)}, bf16[18,32,256]{2,1,0:T(8,128)(2,1)S(1)}, u32[]{:S(2)}, u32[]{:S(2)}) collective-permute-start(bf16[18,32,256]{2,1,0:T(8,128)(2,1)S(1)} %get-tuple-element.11.refs_0_.te), channel_id=1, source_target_pairs={{2,0},{4,2},{6,4},{8,6},{10,8},{12,10},{14,12},{3,1},{5,3},{7,5},{... | collective-permute-start | bytes 884744 | tf_op jit(solution)/shard_map/ppermute | solution.py:218
  13.4 7.2 %copy-start.2 = (s32[2,4]{1,0:T(2,128)S(1)}, s32[2,4]{1,0:T(2,128)}, u32[]{:S(2)}) copy-start(s32[2,4]{1,0:T(2,128)} %flags.7) | copy-start | bytes 100
  18.2 15.4 %collective-permute-start = (bf16[18,32,256]{2,1,0:T(8,128)(2,1)S(1)}, bf16[18,32,256]{2,1,0:T(8,128)(2,1)S(1)}, u32[]{:S(2)}, u32[]{:S(2)}) collective-permute-start(bf16[18,32,256]{2,1,0:T(8,128)(2,1)S(1)} %shard_map.73.be), channel_id=1, source_target_pairs={{0,2},{2,4},{4,6},{6,8},{8,10},{10,12},{12,14},{1,3},{3,5},{5,7},{... | collective-permute-start | bytes 884744 | tf_op jit(solution)/shard_map/ppermute | solution.py:220
  20.6 2.2 %copy-start.4 = (bf16[2048,1024]{1,0:T(8,128)(2,1)S(1)}, bf16[2048,1024]{1,0:T(8,128)(2,1)}, u32[]{:S(2)}) copy-start(bf16[2048,1024]{1,0:T(8,128)(2,1)} %copy-done.3) | copy-start | bytes 12582916
  22.8 2.2 %copy-start.7 = (bf16[1024,2048]{1,0:T(8,128)(2,1)S(1)}, bf16[1024,2048]{1,0:T(8,128)(2,1)}, u32[]{:S(2)}) copy-start(bf16[1024,2048]{1,0:T(8,128)(2,1)} %copy-done.6) | copy-start | bytes 12582916
  25.0 1.6 %copy-start.9 = (bf16[512,2048]{1,0:T(8,128)(2,1)S(1)}, bf16[512,2048]{1,0:T(8,128)(2,1)}, u32[]{:S(2)}) copy-start(bf16[512,2048]{1,0:T(8,128)(2,1)} %copy-done.8) | copy-start | bytes 6291460
  26.6 1.2 %copy-start.13 = (bf16[2048,256]{1,0:T(8,128)(2,1)S(1)}, bf16[2048,256]{1,0:T(8,128)(2,1)}, u32[]{:S(2)}) copy-start(bf16[2048,256]{1,0:T(8,128)(2,1)} %copy-done.12) | copy-start | bytes 3145732
  27.8 8.1 %copy-start.5 = (bf16[2048,1024]{1,0:T(8,128)(2,1)S(1)}, bf16[2048,1024]{1,0:T(8,128)(2,1)}, u32[]{:S(2)}) copy-start(bf16[2048,1024]{1,0:T(8,128)(2,1)} %copy-done.3) | copy-start | bytes 12582916
  33.8 2.1 %copy-start.11 = (bf16[1024,512]{1,0:T(8,128)(2,1)S(1)}, bf16[1024,512]{1,0:T(8,128)(2,1)}, u32[]{:S(2)}) copy-start(bf16[1024,512]{1,0:T(8,128)(2,1)} %copy-done.10) | copy-start | bytes 3145732
  34.7 24.1 %copy-start = (bf16[9,256,256]{2,1,0:T(8,128)(2,1)S(1)}, bf16[9,256,256]{2,1,0:T(8,128)(2,1)}, u32[]{:S(2)}) copy-start(bf16[9,256,256]{2,1,0:T(8,128)(2,1)} %w.1) | copy-start | bytes 3538948
  34.7 24.1 %collective-permute-start.4 = (bf16[72,16,256]{2,1,0:T(8,128)(2,1)}, bf16[72,16,256]{2,1,0:T(8,128)(2,1)S(1)}, u32[]{:S(2)}, u32[]{:S(2)}) collective-permute-start(bf16[72,16,256]{2,1,0:T(8,128)(2,1)} %slice_select_fusion), channel_id=1, source_target_pairs={{0,1},{1,0},{2,3},{3,2},{4,5},{5,4},{6,7},{7,6},{8,9},{9,8},{10,11... | collective-permute-start | bytes 1769480 | tf_op jit(solution)/shard_map/ppermute | solution.py:231
  40.6 16.2 %collective-permute-start.2 = (bf16[18,32,256]{2,1,0:T(8,128)(2,1)S(1)}, bf16[18,32,256]{2,1,0:T(8,128)(2,1)}, u32[]{:S(2)}, u32[]{:S(2)}) collective-permute-start(bf16[18,32,256]{2,1,0:T(8,128)(2,1)S(1)} %shard_map.75.bm), channel_id=1, source_target_pairs={{0,2},{2,4},{4,6},{6,8},{8,10},{10,12},{12,14},{1,3},{3,5},{5,7},{... | collective-permute-start | bytes 884744 | tf_op jit(solution)/shard_map/ppermute | solution.py:224
  44.7 14.1 %collective-permute-start.3 = (bf16[18,32,256]{2,1,0:T(8,128)(2,1)S(1)}, bf16[18,32,256]{2,1,0:T(8,128)(2,1)}, u32[]{:S(2)}, u32[]{:S(2)}) collective-permute-start(bf16[18,32,256]{2,1,0:T(8,128)(2,1)S(1)} %shard_map.74.refs_0_.tm), channel_id=1, source_target_pairs={{2,0},{4,2},{6,4},{8,6},{10,8},{12,10},{14,12},{3,1},{5,3},{7,5},{... | collective-permute-start | bytes 884744 | tf_op jit(solution)/shard_map/ppermute | solution.py:222

commit v2 on v0

v2 whole, which is shorter than its diff:
```python
import functools

import jax
import jax.numpy as jnp
from jax import lax
from jax.experimental import pallas as pl
from jax.experimental.pallas import tpu as pltpu
from jax.sharding import PartitionSpec as P


TILE = 16
RR = 18
RC = 15
BLOCK = 512
F32 = jnp.float32
BF16 = jnp.bfloat16
VM = pl.BlockSpec(memory_space=pltpu.VMEM)
SM = pl.BlockSpec(memory_space=pltpu.SMEM)
HBM = pl.BlockSpec(memory_space=pltpu.MemorySpace.HBM)
MIB = 1 << 20
TRUNK_MIB = 16
CONV_MIB = 24


def params(mib):
    return pltpu.CompilerParams(vmem_limit_bytes=mib * MIB)


def cost(flops, nbytes):
    return pl.CostEstimate(flops=int(flops), bytes_accessed=int(nbytes), transcendentals=0)


def in_hbm(value):
    return pltpu.with_memory_space_constraint(value, pltpu.MemorySpace.HBM)


def near_is_top():
    return lax.rem(lax.axis_index("row"), 2)


def columns_of(chunk):
    return chunk[0]


def span(chunk, height):
    return (RR if chunk[1] else height - RR) * TILE


def sources(chunk, top):
    rest = (RR - TILE) * TILE
    pixels = TILE * TILE
    for j, col in enumerate(chunk[0]):
        if chunk[1]:
            at = j * (pixels + rest)
            yield 1 - top, col, 0, pixels, at
            yield top, col, (1 - top) * (pixels - rest), rest, at + pixels
        else:
            yield top, col, top * rest, pixels - rest, j * (pixels - rest)


def trunk_rows(x, wr, we, ws, wb, ready=lambda k: None):
    ready(0)
    hidden = jnp.maximum(jnp.dot(x, wr[...], preferred_element_type=F32), 0).astype(BF16)
    total = None
    for k, at in enumerate(range(0, we.shape[1], BLOCK)):
        ready(1 + k)
        summed = jnp.dot(hidden, we[:, at : at + BLOCK], preferred_element_type=F32)
        summed = summed + jnp.dot(x, ws[:, at : at + BLOCK], preferred_element_type=F32)
        block_out = jnp.maximum(summed, 0).astype(BF16)
        term = jnp.dot(block_out, wb[at : at + BLOCK, :], preferred_element_type=F32)
        total = term if total is None else total + term
    return jnp.maximum(total, 0)


def put_column(part, chunk, col, j, top, flags, out):
    width = part.shape[-1]
    where = pl.ds(j * TILE, TILE)
    own = flags[top, col] >= 0
    if chunk[1]:
        pixels = TILE * TILE
        full = jnp.where(flags[1 - top, col] >= 0, part[:pixels], 0.0).astype(BF16)
        rest = jnp.where(own, part[pixels:], 0.0).astype(BF16)
        out[pl.ds((1 - top) * (RR - TILE), TILE), where, :] = full.reshape(TILE, TILE, width)
        out[pl.ds(top * TILE, RR - TILE), where, :] = rest.reshape(RR - TILE, TILE, width)
    else:
        rows = part.shape[0] // TILE
        part = jnp.where(own, part, 0.0).astype(BF16)
        out[pl.ds(top * (RR - rows), rows), where, :] = part.reshape(rows, TILE, width)


def first_chunk(chunks, height, asg, feats, wr_h, we_h, ws_h, wb_h, out, xs, wr, we, ws, wb, flags, sems):
    top = near_is_top()
    steps = [[]]
    steps[0].append((asg, flags))
    at = 0
    later = []
    for i, chunk in enumerate(chunks):
        moves = [
            (feats.at[tr, col, pl.ds(first, count), :], xs.at[pl.ds(at + row, count), :])
            for tr, col, first, count, row in sources(chunk, top)
        ]
        at += span(chunk, height) * len(columns_of(chunk))
        if i == 0:
            steps[0] += moves
        else:
            later.append(moves)
    steps[0].append((wr_h, wr))
    for k in range(0, we.shape[1], BLOCK):
        cols = pl.ds(k, BLOCK)
        steps.append(
            [(ws_h.at[:, cols], ws.at[:, cols]), (we_h.at[:, cols], we.at[:, cols]), (wb_h.at[cols, :], wb.at[cols, :])]
        )
    n_weights = len(steps)
    steps += later
    copies = []
    used = 0
    for step in steps:
        copies.append([pltpu.make_async_copy(src, dst, sems.at[used + j]) for j, (src, dst) in enumerate(step)])
        used += len(step)

    def begin(k):
        if k < len(copies):
            for copy in copies[k]:
                copy.start()

    def ready(k):
        for copy in copies[k]:
            copy.wait()
        begin(k + 2)

    begin(0)
    begin(1)
    ready(0)
    per = span(chunks[0], height)
    cols = columns_of(chunks[0])
    reduced = trunk_rows(xs[0 : per * len(cols), :], wr, we, ws, wb, lambda k: ready(k) if k else None)
    for j, col in enumerate(cols):
        put_column(reduced[j * per : (j + 1) * per], chunks[0], col, j, top, flags, out)
    for k in range(n_weights, len(copies)):
        ready(k)


def later_chunk(chunk, at, height, flags, xs, wr, we, ws, wb, *refs):
    out = refs[-1]
    top = near_is_top()
    per = span(chunk, height)
    cols = columns_of(chunk)

    def busy(col):
        own = flags[top, col] >= 0
        if chunk[1]:
            own = own | (flags[1 - top, col] >= 0)
        return own

    active = [busy(col) for col in cols]
    every = functools.reduce(lambda a, b: a & b, active)
    zero = jnp.zeros((span(chunk, height), out.shape[-1]), F32)

    @pl.when(every)
    def _():
        reduced = trunk_rows(xs[at : at + per * len(cols), :], wr, we, ws, wb)
        for j, col in enumerate(cols):
            put_column(reduced[j * per : (j + 1) * per], chunk, col, j, top, flags, out)

    if len(cols) == 1:
        @pl.when(jnp.logical_not(every))
        def _():
            put_column(zero, chunk, cols[0], 0, top, flags, out)
    else:
        for j, col in enumerate(cols):
            @pl.when(jnp.logical_not(active[j]))
            def _():
                put_column(zero, chunk, col, j, top, flags, out)

        one = cols[0]
        step = cols[1] - cols[0]

        @pl.loop(0, len(cols))
        def _(j):
            col = one + j * step
            mine = flags[top, col] >= 0
            if chunk[1]:
                mine = mine | (flags[1 - top, col] >= 0)

            @pl.when(mine & jnp.logical_not(every))
            def _():
                rows = pl.ds(pl.multiple_of(at + j * per, TILE), per)
                put_column(trunk_rows(xs[rows, :], wr, we, ws, wb), chunk, col, j, top, flags, out)

    if not chunk[1]:
        near = refs[0]
        shared = 2 * RR - height
        out[pl.ds((1 - top) * (RR - shared), shared)] = near[pl.ds(top * (RR - shared), shared)]


def pick_kernel(cols_n, *refs):
    n = 1 if cols_n == 2 else 2
    ins, outs = refs[:-n], refs[-n:]
    width = ins[0].shape[1]
    for i, src in enumerate(ins):
        rows = pl.ds(i * RR, RR)
        if cols_n == 2:
            first = pl.multiple_of((1 - lax.axis_index("col")) * (width - TILE), TILE)
            outs[0][rows] = src[:, pl.ds(first, TILE), :]
        else:
            outs[0][rows] = src[:, width - TILE :, :]
            outs[1][rows] = src[:, :TILE, :]


def lay_columns(groups, width, cols_n, row, count, src, first, side, side_row, sides, ext):
    rows = pl.ds(row, count)
    taken = pl.ds(first, count)
    for cols, ref in zip(groups, src):
        for j, col in enumerate(cols):
            ext[rows, (1 + col) * TILE : (2 + col) * TILE, :] = ref[taken, j * TILE : (j + 1) * TILE, :]
    me = lax.axis_index("col")
    zero = jnp.zeros((count, TILE, ext.shape[-1]), BF16)
    for on, at, ref in ((me > 0, 0, sides[0]), (me < cols_n - 1, TILE + width, sides[-1])):
        there = ref[pl.ds(side * RR + side_row, count)]
        ext[rows, at : at + TILE, :] = jnp.where(on, there, zero)


def spread(ext, cat, width):
    br = ext.shape[-1]
    for b in range(3):
        left = TILE - RC + b * RC
        cat[:, :, b * br : (b + 1) * br] = ext[:, left : left + width, :]


def conv_early(groups, cols_n, height, w, *refs):
    g = len(groups)
    near, far, halo = refs[:g], refs[g : 2 * g], refs[2 * g : 3 * g]
    sides = refs[3 * g : -6]
    out, partial, ext, cat, done, sem = refs[-6:]
    top = near_is_top()
    width = cat.shape[1]
    br = ext.shape[-1]
    rest = height - RR
    lay = functools.partial(lay_columns, groups, width, cols_n)
    local = top * RR
    lay((1 - top) * height, RR, halo, 0, 2, 0, sides, ext)
    lay(local + (1 - top) * rest, RR, near, 0, 0, 0, sides, ext)
    far_row = top * (RR - rest)
    lay(local + top * RR, rest, far, far_row, 1, far_row, sides, ext)
    spread(ext, cat, width)
    k = 3 * br
    total = None
    for a in range(3):
        term = jnp.dot(
            cat[a * RR : a * RR + rest].reshape(rest * width, k), w[a * k : (a + 1) * k, :], preferred_element_type=F32
        )
        total = term if total is None else total + term
    done[...] = jnp.maximum(total, 0).astype(BF16).reshape(rest, width, br)
    copy = pltpu.make_async_copy(done, out.at[pl.ds((1 - top) * RR, rest)], sem)
    copy.start()
    centre = cat[pl.ds(top * height, RR)].reshape(RR * width, k)
    inner = cat[pl.ds(top * rest + (1 - top) * RR, RR)].reshape(RR * width, k)
    inner_w = w[pl.ds(pl.multiple_of((1 - top) * 2 * k, k), k), :]
    partial[...] = jnp.dot(centre, w[k : 2 * k, :], preferred_element_type=F32) + jnp.dot(
        inner, inner_w, preferred_element_type=F32
    )
    copy.wait()


def conv_late(groups, cols_n, height, w, partial, *refs):
    g = len(groups)
    halo = refs[:g]
    sides = refs[g:-6]
    _, out, ext, cat, done, sem = refs[-6:]
    top = near_is_top()
    width = cat.shape[1]
    br = ext.shape[-1]
    lay_columns(groups, width, cols_n, 0, RR, halo, 0, 3, 0, sides, ext)
    spread(ext, cat, width)
    k = 3 * br
    outer_w = w[pl.ds(pl.multiple_of(top * 2 * k, k), k), :]
    total = partial[...] + jnp.dot(cat[...].reshape(RR * width, k), outer_w, preferred_element_type=F32)
    done[...] = jnp.maximum(total, 0).astype(BF16).reshape(RR, width, br)
    copy = pltpu.make_async_copy(done, out.at[pl.ds(top * (height - RR), RR)], sem)
    copy.start()
    copy.wait()


def plan(tile_cols):
    groups = [[0, tile_cols - 1], list(range(1, tile_cols - 1))]
    order = [(i, near) for i in range(len(groups)) for near in (True, False)]
    return groups, order


def shards(features, assignment, w_reduce, w_expand, w_short, w_branch, w_dilated):
    tile_rows, tile_cols, pixels, channels = features.shape
    mid, cout, br = w_reduce.shape[1], w_expand.shape[1], w_branch.shape[1]
    height, width = tile_rows * TILE, tile_cols * TILE
    assert tile_rows == 2 and pixels == TILE * TILE and TILE < RR <= height <= 2 * RR
    groups, order = plan(tile_cols)
    chunks = [(groups[i], near) for i, near in order]
    sizes = [span(c, height) * len(c[0]) for c in chunks]
    starts = [sum(sizes[:i]) for i in range(len(sizes))]
    per_row = 2 * (channels * mid + mid * cout + channels * cout + cout * br)
    n_copies = sum(len(list(sources(c, 0))) for c in chunks) + 2 + 3 * (cout // BLOCK)

    def grid_of(cols):
        return jax.ShapeDtypeStruct((RR, len(cols) * TILE, br), BF16)

    first, xs, wr, we, ws, wb = pl.pallas_call(
        functools.partial(first_chunk, chunks, height),
        out_shape=[
            grid_of(chunks[0][0]),
            jax.ShapeDtypeStruct((sum(sizes), channels), BF16),
            jax.ShapeDtypeStruct(w_reduce.shape, BF16),
            jax.ShapeDtypeStruct(w_expand.shape, BF16),
            jax.ShapeDtypeStruct(w_short.shape, BF16),
            jax.ShapeDtypeStruct(w_branch.shape, BF16),
        ],
        in_specs=[HBM] * 6,
        out_specs=[VM] * 6,
        scratch_shapes=[pltpu.SMEM(assignment.shape, jnp.int32), pltpu.SemaphoreType.DMA((n_copies,))],
        compiler_params=params(TRUNK_MIB),
        cost_estimate=cost(per_row * sizes[0], 12 * MIB),
        name="trunk_first",
    )(*[in_hbm(v) for v in (assignment, features, w_reduce, w_expand, w_short, w_branch)])

    rows_n = lax.axis_size("row")
    swap = [(i, i ^ 1) for i in range(rows_n) if i ^ 1 < rows_n]
    cross = [pair for i in range(1, rows_n - 1, 2) for pair in ((i, i + 1), (i + 1, i))]

    local, halo = {}, {}
    for n, (i, near) in enumerate(order):
        if n == 0:
            value = first
        else:
            extra = [] if near else [local[i, True]]
            value = pl.pallas_call(
                functools.partial(later_chunk, chunks[n], starts[n], height),
                out_shape=grid_of(groups[i]),
                in_specs=[SM] + [VM] * (5 + len(extra)),
                out_specs=VM,
                compiler_params=params(TRUNK_MIB),
                cost_estimate=cost(per_row * sizes[n], MIB),
            )(assignment, xs, wr, we, ws, wb, *extra)
        local[i, near] = value
        halo[i, near] = lax.ppermute(value, "row", swap if near else cross)

    cols_n = lax.axis_size("col")
    side = jax.ShapeDtypeStruct((4 * RR, TILE, br), BF16)
    one_swap = cols_n == 2
    picked = pl.pallas_call(
        functools.partial(pick_kernel, cols_n),
        out_shape=[side] if one_swap else [side, side],
        in_specs=[VM] * 4,
        out_specs=[VM] * (1 if one_swap else 2),
        compiler_params=params(4),
        cost_estimate=cost(0, MIB),
        name="pick",
    )(local[0, True], local[0, False], halo[0, True], halo[0, False])
    if one_swap:
        sides = [lax.ppermute(picked[0], "col", [(0, 1), (1, 0)])]
    else:
        sides = [
            lax.ppermute(picked[0], "col", [(i, i + 1) for i in range(cols_n - 1)]),
            lax.ppermute(picked[1], "col", [(i + 1, i) for i in range(cols_n - 1)]),
        ]

    taps = w_dilated.reshape(9 * br, br)
    rest = height - RR
    n_groups = len(groups)
    pick = lambda table, near: [table[i, near] for i in range(n_groups)]
    flops = 2 * width * 3 * br * br
    out, partial = pl.pallas_call(
        functools.partial(conv_early, groups, cols_n, height),
        out_shape=[
            jax.ShapeDtypeStruct((height, width, br), BF16),
            jax.ShapeDtypeStruct((RR * width, br), F32),
        ],
        in_specs=[VM] * (1 + 3 * n_groups + len(sides)),
        out_specs=[HBM, VM],
        scratch_shapes=[
            pltpu.VMEM((height + RR, width + 2 * TILE, br), BF16),
            pltpu.VMEM((height + RR, width, 3 * br), BF16),
            pltpu.VMEM((rest, width, br), BF16),
            pltpu.SemaphoreType.DMA,
        ],
        compiler_params=params(CONV_MIB),
        cost_estimate=cost(flops * (3 * rest + 2 * RR), 4 * MIB),
        name="conv_early",
    )(taps, *pick(local, True), *pick(local, False), *pick(halo, True), *sides)
    n_in = 2 + n_groups + len(sides)
    return pl.pallas_call(
        functools.partial(conv_late, groups, cols_n, height),
        out_shape=jax.ShapeDtypeStruct((height, width, br), BF16),
        in_specs=[VM] * n_in + [HBM],
        out_specs=HBM,
        input_output_aliases={n_in: 0},
        scratch_shapes=[
            pltpu.VMEM((RR, width + 2 * TILE, br), BF16),
            pltpu.VMEM((RR, width, 3 * br), BF16),
            pltpu.VMEM((RR, width, br), BF16),
            pltpu.SemaphoreType.DMA,
        ],
        compiler_params=params(16),
        cost_estimate=cost(flops * RR, 2 * MIB),
        name="conv_late",
    )(taps, partial, *pick(halo, False), *sides, out)


def solution(mesh):
    in_specs = (
        P(("groups", "row"), "col", None, None),
        P(("groups", "row"), "col"),
        P(),
        P(),
        P(),
        P(),
        P(),
    )
    out_specs = P(("groups", "row"), "col", None)

    return jax.shard_map(shards, mesh=mesh, in_specs=in_specs, out_specs=out_specs, check_vma=False)
```

time: 79.8 us -> 60.7 us (0.76); the launches traced: 79.6 us -> 59.6 us
  matrix products: 35.3 us -> 0 us
  Pallas kernels: 0 us -> 20.1 us
  starting transfers between devices: 10.6 us -> 16.1 us
  local copies, waits for them, and re-layouts: 4.53 us -> 0.01 us
  other arithmetic: 3.25 us -> 0 us
  waiting for transfers between devices: 25.7 us -> 23.2 us
    dot_general x3 -> x0, matrix products: 35.3 us -> none  [the longest x1 19.7 us: trunk(): jnp.dot(block_out, w_branch, preferred_element_type=jnp.float32)]
    pallas_call x0 -> x7, Pallas kernels: none -> 20.1 us  [the longest x1 10.3 us: shards(): pl.pallas_call(functools.partial(first_chunk, chunks, height), out_shape=...]
    ppermute x4 -> x5, starting transfers between devices: 10.6 us -> 16.1 us  [the longest x4 14.7 us: shards(): halo[i, near] = lax.ppermute(value, 'row', swap if near else cross)]
    ppermute x4 -> x5, waiting for transfers between devices: 25.7 us -> 23.2 us  [the longest x4 23.2 us: shards(): halo[i, near] = lax.ppermute(value, 'row', swap if near else cross)]
    unnamed x12 -> x4, local copies, waits for them, and re-layouts: 2.29 us -> 0.01 us
    concatenate x3 -> x0, other arithmetic: 2.27 us -> none  [extended_2(): jnp.concatenate([lax.ppermute(tail, axis, [(i, (i + 1) % count) for i in...]
    slice x4 -> x0, local copies, waits for them, and re-layouts: 1.95 us -> none  [the longest x1 1.5 us: shards(): extended[down_tap * RR:down_tap * RR + height, col_start:col_start + width]]
    ge x1 -> x0, other arithmetic: 0.83 us -> none  [shards(): tissue = tile_codes >= 0]
  transfers between devices with their start and end apart: 4 -> 5, of which waited for: 3 -> 3; matrix products, arithmetic and copies ran while one was open for 1% -> 0% of each run, Pallas kernels for 0% -> 9%
where the time goes in v2:
time: 60.7 us; the launch traced here: 59.6 us
  waiting for transfers between devices  23.2 us (38%)
  Pallas kernels  20.1 us (33%)
  starting transfers between devices  16.1 us (27%)
    ppermute x4, waiting for transfers between devices, shards(): halo[i, near] = lax.ppermute(value, 'row', swap if near else cross)  23.2 us
    ppermute x4, starting transfers between devices, shards(): halo[i, near] = lax.ppermute(value, 'row', swap if near else cross)  14.7 us
    pallas_call x1, Pallas kernels, shards(): pl.pallas_call(functools.partial(first_chunk, chunks, height), out_shape=...  10.3 us
    pallas_call x3, Pallas kernels, shards(): pl.pallas_call(functools.partial(later_chunk, chunks[n], starts[n], heigh...  4.29 us
    pallas_call x1, Pallas kernels, shards(): pl.pallas_call(functools.partial(conv_early, groups, cols_n, height), out...  3.97 us
    pallas_call x1, Pallas kernels, shards(): pl.pallas_call(functools.partial(conv_late, groups, cols_n, height), out_...  1.5 us
    ppermute x1, starting transfers between devices, shards(): sides = [lax.ppermute(picked[0], 'col', [(0, 1), (1, 0)])]  1.36 us
  transfers between devices with their start and end apart: 5, of which 3 were waited for; matrix products, arithmetic and copies ran while one was open for 0% of the time, Pallas kernels for 9%

profile of v2, /device:TPU:9, one launch (start us, length us, event | category | flops | bytes accessed | tf_op | source)
XLA Modules:
  0.0 59.6 jit_solution(4389746480455605845)
XLA Ops:
  0.0 0.0 copy-start.1
  0.0 10.3 %trunk_first.1 = (bf16[18,32,256]{2,1,0:T(8,128)(2,1)S(1)}, bf16[2048,1024]{1,0:T(8,128)(2,1)S(1)}, bf16[1024,512]{1,0:T(8,128)(2,1)S(1)}, bf16[512,2048]{1,0:T(...) custom-call(s32[2,4]{1,0:T(2,128)} %flags.5, bf16[2,4,256,1024]{3,2,1,0:T(8,128)(2,1)} %feats.1, ...), custom_call_target="tpu_custom_call" | custom-call | flops 4831838208 | bytes 12582912 | tf_op jit(solution)/shard_map/trunk_first/pallas_call | solution.py:305
  10.3 0.0 copy-done.1
  10.3 2.9 %shard_map.74.refs_1_.refs_2_ = bf16[18,32,256]{2,1,0:T(8,128)(2,1)S(1)} custom-call(s32[2,4]{1,0:T(2,128)S(1)} %copy-done.1, bf16[2048,1024]{1,0:T(8,128)(2,1)S(1)} %get-tuple-element.14.xs, bf16[1024,512]{1,0:T(8,128)(2,1)S(1)} %get-tuple-element.15.wr, bf16[512,2048]{1,0:T(8,128)(2,1)S(1)} %get-tuple-element.16.we, ...), custom_call_target="tpu_custom_call" | custom-call | flops 3758096384 | bytes 1048576 | tf_op jit(solution)/shard_map/pallas_call | solution.py:333
  13.2 1.9 %collective-permute-start.2 = (bf16[18,32,256]{2,1,0:T(8,128)(2,1)S(1)}, bf16[18,32,256]{2,1,0:T(8,128)(2,1)S(1)}, u32[]{:S(2)}, u32[]{:S(2)}) collective-permute-start(bf16[18,32,256]{2,1,0:T(8,128)(2,1)S(1)} %shard_map.74.refs_1_.refs_2_), channel_id=1, source_target_pairs={{2,4},{4,2},{6,8},{8,6},{10,12},{12,10},{3,5},{5,3},{7,9},{9,7},{1... | collective-permute-start | bytes 884744 | tf_op jit(solution)/shard_map/ppermute | solution.py:342
  15.1 3.2 %collective-permute-start = (bf16[18,32,256]{2,1,0:T(8,128)(2,1)S(1)}, bf16[18,32,256]{2,1,0:T(8,128)(2,1)S(1)}, u32[]{:S(2)}, u32[]{:S(2)}) collective-permute-start(bf16[18,32,256]{2,1,0:T(8,128)(2,1)S(1)} %get-tuple-element.13.refs_0_), channel_id=1, source_target_pairs={{0,2},{2,0},{4,6},{6,4},{8,10},{10,8},{12,14},{14,12},{1,3},{3,1},... | collective-permute-start | bytes 884744 | tf_op jit(solution)/shard_map/ppermute | solution.py:342
  18.3 5.4 %collective-permute-done.2.refs_3_.refs_0_ = bf16[18,32,256]{2,1,0:T(8,128)(2,1)S(1)} collective-permute-done((bf16[18,32,256]{2,1,0:T(8,128)(2,1)S(1)}, bf16[18,32,256]{2,1,0:T(8,128)(2,1)S(1)}, u32[]{:S(2)}, u32[]{:S(2)}) %collective-permute-start.2) | collective-permute-done | bytes 294944 | tf_op jit(solution)/shard_map/ppermute | solution.py:342
  23.7 6.8 %collective-permute-done.refs_2_.refs_4_ = bf16[18,32,256]{2,1,0:T(8,128)(2,1)S(1)} collective-permute-done((bf16[18,32,256]{2,1,0:T(8,128)(2,1)S(1)}, bf16[18,32,256]{2,1,0:T(8,128)(2,1)S(1)}, u32[]{:S(2)}, u32[]{:S(2)}) %collective-permute-start) | collective-permute-done | bytes 294944 | tf_op jit(solution)/shard_map/ppermute | solution.py:342
  30.6 1.4 %collective-permute-start.3 = (bf16[72,16,256]{2,1,0:T(8,128)(2,1)S(1)}, bf16[72,16,256]{2,1,0:T(8,128)(2,1)S(1)}, u32[]{:S(2)}, u32[]{:S(2)}) collective-permute-start(bf16[72,16,256]{2,1,0:T(8,128)(2,1)S(1)} %pick.1), channel_id=1, source_target_pairs={{0,1},{1,0},{2,3},{3,2},{4,5},{5,4},{6,7},{7,6},{8,9},{9,8},{10,11... | collective-permute-start | bytes 1769480 | tf_op jit(solution)/shard_map/ppermute | solution.py:357
  32.0 0.8 %shard_map.73.refs_0_.refs_1_ = bf16[18,32,256]{2,1,0:T(8,128)(2,1)S(1)} custom-call(s32[2,4]{1,0:T(2,128)S(1)} %copy-done.1, bf16[2048,1024]{1,0:T(8,128)(2,1)S(1)} %get-tuple-element.14.xs, bf16[1024,512]{1,0:T(8,128)(2,1)S(1)} %get-tuple-element.15.wr, bf16[512,2048]{1,0:T(8,128)(2,1)S(1)} %get-tuple-element.16.we, ...), custom_call_target="tpu_custom_call" | custom-call | flops 4831838208 | bytes 1048576 | tf_op jit(solution)/shard_map/pallas_call | solution.py:333
  32.8 0.0 copy-start
  32.8 7.5 %collective-permute-start.1 = (bf16[18,32,256]{2,1,0:T(8,128)(2,1)S(1)}, bf16[18,32,256]{2,1,0:T(8,128)(2,1)S(1)}, u32[]{:S(2)}, u32[]{:S(2)}) collective-permute-start(bf16[18,32,256]{2,1,0:T(8,128)(2,1)S(1)} %shard_map.73.refs_0_.refs_1_), channel_id=1, source_target_pairs={{0,2},{2,0},{4,6},{6,4},{8,10},{10,8},{12,14},{14,12},{1,3},{3,1},... | collective-permute-start | bytes 884744 | tf_op jit(solution)/shard_map/ppermute | solution.py:342
  40.3 0.6 %shard_map.75.refs_3_ = bf16[18,32,256]{2,1,0:T(8,128)(2,1)S(1)} custom-call(s32[2,4]{1,0:T(2,128)S(1)} %copy-done.1, bf16[2048,1024]{1,0:T(8,128)(2,1)S(1)} %get-tuple-element.14.xs, bf16[1024,512]{1,0:T(8,128)(2,1)S(1)} %get-tuple-element.15.wr, bf16[512,2048]{1,0:T(8,128)(2,1)S(1)} %get-tuple-element.16.we, bf16[1024,2048]{1,0:T(8,128)(2,1)S(1)} %get-tuple-element.17.ws, ...), custom_call_target="tpu_custom_call" | custom-call | flops 3758096384 | bytes 1048576 | tf_op jit(solution)/shard_map/pallas_call | solution.py:333
  40.9 2.1 %collective-permute-start.4 = (bf16[18,32,256]{2,1,0:T(8,128)(2,1)S(1)}, bf16[18,32,256]{2,1,0:T(8,128)(2,1)S(1)}, u32[]{:S(2)}, u32[]{:S(2)}) collective-permute-start(bf16[18,32,256]{2,1,0:T(8,128)(2,1)S(1)} %shard_map.75.refs_3_), channel_id=1, source_target_pairs={{2,4},{4,2},{6,8},{8,6},{10,12},{12,10},{3,5},{5,3},{7,9},{9,7},{1... | collective-permute-start | bytes 884744 | tf_op jit(solution)/shard_map/ppermute | solution.py:342
  43.0 10.9 %collective-permute-done.1.refs_5_ = bf16[18,32,256]{2,1,0:T(8,128)(2,1)S(1)} collective-permute-done((bf16[18,32,256]{2,1,0:T(8,128)(2,1)S(1)}, bf16[18,32,256]{2,1,0:T(8,128)(2,1)S(1)}, u32[]{:S(2)}, u32[]{:S(2)}) %collective-permute-start.1) | collective-permute-done | bytes 294944 | tf_op jit(solution)/shard_map/ppermute | solution.py:342
  54.0 0.0 collective-permute-done.3.refs_6_.refs_2_
  54.0 0.0 copy-done
  54.0 4.0 %conv_early.1 = (bf16[32,64,256]{2,1,0:T(8,128)(2,1)}, f32[1152,256]{1,0:T(8,128)S(1)}) custom-call(bf16[2304,256]{1,0:T(8,128)(2,1)S(1)} %bitcast.1, bf16[18,32,256]{2,1,0:T(8,128)(2,1)S(1)} %get-tuple-element.13.refs_0_, bf16[18,32,256]{2,1,0:T(8,128)(2,1)S(1)} %shard_map.73.refs_0_.refs_1_, bf16[18,32,256]{2,1,0:T(8,128)(2,1)S(1)} %shard_map.74.refs_1_.refs_2_, ...), custom_call_target="tpu_custom_call" | custom-call | flops 1962934272 | bytes 4194304 | tf_op jit(solution)/shard_map/conv_early/pallas_call | solution.py:369
  57.9 0.0 collective-permute-done.4.refs_1_
  58.0 1.5 %conv_late.1 = bf16[32,64,256]{2,1,0:T(8,128)(2,1)} custom-call(bf16[2304,256]{1,0:T(8,128)(2,1)S(1)} %bitcast.2, f32[1152,256]{1,0:T(8,128)S(1)} %get-tuple-element.19.partial, bf16[18,32,256]{2,1,0:T(8,128)(2,1)S(1)} %collective-permute-done.2.refs_3_.refs_0_, ...), custom_call_target="tpu_custom_call", output_to_operand_aliasing={{}: (5, {})} | custom-call | flops 452984832 | bytes 2097152 | tf_op jit(solution)/shard_map/conv_late/pallas_call | solution.py:388
  (1 shorter events, 0.0 us)
Async XLA Ops:
  0.0 10.3 %copy-start.1 = (s32[2,4]{1,0:T(2,128)S(1)}, s32[2,4]{1,0:T(2,128)}, u32[]{:S(2)}) copy-start(s32[2,4]{1,0:T(2,128)} %flags.5) | copy-start | bytes 100
  13.2 10.5 %collective-permute-start.2 = (bf16[18,32,256]{2,1,0:T(8,128)(2,1)S(1)}, bf16[18,32,256]{2,1,0:T(8,128)(2,1)S(1)}, u32[]{:S(2)}, u32[]{:S(2)}) collective-permute-start(bf16[18,32,256]{2,1,0:T(8,128)(2,1)S(1)} %shard_map.74.refs_1_.refs_2_), channel_id=1, source_target_pairs={{2,4},{4,2},{6,8},{8,6},{10,12},{12,10},{3,5},{5,3},{7,9},{9,7},{1... | collective-permute-start | bytes 884744 | tf_op jit(solution)/shard_map/ppermute | solution.py:342
  15.1 15.5 %collective-permute-start = (bf16[18,32,256]{2,1,0:T(8,128)(2,1)S(1)}, bf16[18,32,256]{2,1,0:T(8,128)(2,1)S(1)}, u32[]{:S(2)}, u32[]{:S(2)}) collective-permute-start(bf16[18,32,256]{2,1,0:T(8,128)(2,1)S(1)} %get-tuple-element.13.refs_0_), channel_id=1, source_target_pairs={{0,2},{2,0},{4,6},{6,4},{8,10},{10,8},{12,14},{14,12},{1,3},{3,1},... | collective-permute-start | bytes 884744 | tf_op jit(solution)/shard_map/ppermute | solution.py:342
  30.6 23.3 %collective-permute-start.3 = (bf16[72,16,256]{2,1,0:T(8,128)(2,1)S(1)}, bf16[72,16,256]{2,1,0:T(8,128)(2,1)S(1)}, u32[]{:S(2)}, u32[]{:S(2)}) collective-permute-start(bf16[72,16,256]{2,1,0:T(8,128)(2,1)S(1)} %pick.1), channel_id=1, source_target_pairs={{0,1},{1,0},{2,3},{3,2},{4,5},{5,4},{6,7},{7,6},{8,9},{9,8},{10,11... | collective-permute-start | bytes 1769480 | tf_op jit(solution)/shard_map/ppermute | solution.py:357
  32.8 21.2 %copy-start = (bf16[9,256,256]{2,1,0:T(8,128)(2,1)S(1)}, bf16[9,256,256]{2,1,0:T(8,128)(2,1)}, u32[]{:S(2)}) copy-start(bf16[9,256,256]{2,1,0:T(8,128)(2,1)} %param.13) | copy-start | bytes 3538948
  32.8 21.1 %collective-permute-start.1 = (bf16[18,32,256]{2,1,0:T(8,128)(2,1)S(1)}, bf16[18,32,256]{2,1,0:T(8,128)(2,1)S(1)}, u32[]{:S(2)}, u32[]{:S(2)}) collective-permute-start(bf16[18,32,256]{2,1,0:T(8,128)(2,1)S(1)} %shard_map.73.refs_0_.refs_1_), channel_id=1, source_target_pairs={{0,2},{2,0},{4,6},{6,4},{8,10},{10,8},{12,14},{14,12},{1,3},{3,1},... | collective-permute-start | bytes 884744 | tf_op jit(solution)/shard_map/ppermute | solution.py:342
  40.9 17.0 %collective-permute-start.4 = (bf16[18,32,256]{2,1,0:T(8,128)(2,1)S(1)}, bf16[18,32,256]{2,1,0:T(8,128)(2,1)S(1)}, u32[]{:S(2)}, u32[]{:S(2)}) collective-permute-start(bf16[18,32,256]{2,1,0:T(8,128)(2,1)S(1)} %shard_map.75.refs_3_), channel_id=1, source_target_pairs={{2,4},{4,2},{6,8},{8,6},{10,12},{12,10},{3,5},{5,3},{7,9},{9,7},{1... | collective-permute-start | bytes 884744 | tf_op jit(solution)/shard_map/ppermute | solution.py:342

commit v3 on v2

--- a/solution.py
+++ b/solution.py
@@ -12,6 +12,8 @@
 RR = 18
 RC = 15
 BLOCK = 512
+DEPTH = 3
+LATE = 3
 F32 = jnp.float32
 BF16 = jnp.bfloat16
 VM = pl.BlockSpec(memory_space=pltpu.VMEM)
@@ -36,6 +38,10 @@
 
 def near_is_top():
     return lax.rem(lax.axis_index("row"), 2)
+
+
+def top_of(near_first):
+    return near_is_top() if near_first else 1 - near_is_top()
 
 
 def columns_of(chunk):
@@ -89,7 +95,6 @@
 
 
 def first_chunk(chunks, height, asg, feats, wr_h, we_h, ws_h, wb_h, out, xs, wr, we, ws, wb, flags, sems):
-    top = near_is_top()
     steps = [[]]
     steps[0].append((asg, flags))
     at = 0
@@ -97,13 +102,13 @@
     for i, chunk in enumerate(chunks):
         moves = [
             (feats.at[tr, col, pl.ds(first, count), :], xs.at[pl.ds(at + row, count), :])
-            for tr, col, first, count, row in sources(chunk, top)
+            for tr, col, first, count, row in sources(chunk, top_of(chunk[2]))
         ]
         at += span(chunk, height) * len(columns_of(chunk))
         if i == 0:
             steps[0] += moves
         else:
-            later.append(moves)
+            later += moves
     steps[0].append((wr_h, wr))
     for k in range(0, we.shape[1], BLOCK):
         cols = pl.ds(k, BLOCK)
@@ -111,7 +116,7 @@
             [(ws_h.at[:, cols], ws.at[:, cols]), (we_h.at[:, cols], we.at[:, cols]), (wb_h.at[cols, :], wb.at[cols, :])]
         )
     n_weights = len(steps)
-    steps += later
+    steps.append(later)
     copies = []
     used = 0
     for step in steps:
@@ -126,23 +131,23 @@
     def ready(k):
         for copy in copies[k]:
             copy.wait()
-        begin(k + 2)
-
-    begin(0)
-    begin(1)
+        begin(k + DEPTH)
+
+    for k in range(DEPTH):
+        begin(k)
     ready(0)
     per = span(chunks[0], height)
     cols = columns_of(chunks[0])
     reduced = trunk_rows(xs[0 : per * len(cols), :], wr, we, ws, wb, lambda k: ready(k) if k else None)
     for j, col in enumerate(cols):
-        put_column(reduced[j * per : (j + 1) * per], chunks[0], col, j, top, flags, out)
+        put_column(reduced[j * per : (j + 1) * per], chunks[0], col, j, top_of(chunks[0][2]), flags, out)
     for k in range(n_weights, len(copies)):
         ready(k)
 
 
 def later_chunk(chunk, at, height, flags, xs, wr, we, ws, wb, *refs):
     out = refs[-1]
-    top = near_is_top()
+    top = top_of(chunk[2])
     per = span(chunk, height)
     cols = columns_of(chunk)
 
@@ -207,17 +212,19 @@
             outs[1][rows] = src[:, :TILE, :]
 
 
-def lay_columns(groups, width, cols_n, row, count, src, first, side, side_row, sides, ext):
-    rows = pl.ds(row, count)
-    taken = pl.ds(first, count)
-    for cols, ref in zip(groups, src):
-        for j, col in enumerate(cols):
-            ext[rows, (1 + col) * TILE : (2 + col) * TILE, :] = ref[taken, j * TILE : (j + 1) * TILE, :]
+def place(cols, src, first, count, ext, row):
+    for j, col in enumerate(cols):
+        ext[pl.ds(row, count), (1 + col) * TILE : (2 + col) * TILE, :] = src[
+            pl.ds(first, count), j * TILE : (j + 1) * TILE, :
+        ]
+
+
+def place_sides(cols_n, sides, part, first, count, ext, row):
     me = lax.axis_index("col")
-    zero = jnp.zeros((count, TILE, ext.shape[-1]), BF16)
-    for on, at, ref in ((me > 0, 0, sides[0]), (me < cols_n - 1, TILE + width, sides[-1])):
-        there = ref[pl.ds(side * RR + side_row, count)]
-        ext[rows, at : at + TILE, :] = jnp.where(on, there, zero)
+    wide = ext.shape[1]
+    for on, at, ref in ((me > 0, 0, sides[0]), (me < cols_n - 1, wide - TILE, sides[-1])):
+        there = ref[pl.ds(part * RR + first, count)]
+        ext[pl.ds(row, count), at : at + TILE, :] = jnp.where(on, there, jnp.zeros_like(there))
 
 
 def spread(ext, cat, width):
@@ -229,28 +236,31 @@
 
 def conv_early(groups, cols_n, height, w, *refs):
     g = len(groups)
-    near, far, halo = refs[:g], refs[g : 2 * g], refs[2 * g : 3 * g]
+    ones, twos, halo = refs[:g], refs[g : 2 * g], refs[2 * g : 3 * g]
     sides = refs[3 * g : -6]
     out, partial, ext, cat, done, sem = refs[-6:]
     top = near_is_top()
     width = cat.shape[1]
-    br = ext.shape[-1]
     rest = height - RR
-    lay = functools.partial(lay_columns, groups, width, cols_n)
     local = top * RR
-    lay((1 - top) * height, RR, halo, 0, 2, 0, sides, ext)
-    lay(local + (1 - top) * rest, RR, near, 0, 0, 0, sides, ext)
-    far_row = top * (RR - rest)
-    lay(local + top * RR, rest, far, far_row, 1, far_row, sides, ext)
+    for i, (cols, near_first) in enumerate(groups):
+        up = top_of(near_first)
+        skip = up * (RR - rest)
+        rows = ((0, ones[i], 0, RR, local + (1 - up) * rest), (1, twos[i], skip, rest, local + up * RR))
+        rows += ((2, halo[i], 0, RR, (1 - top) * height),)
+        for part, src, first, count, row in rows:
+            place(cols, src, first, count, ext, row)
+            if i == 0:
+                place_sides(cols_n, sides, part, first, count, ext, row)
     spread(ext, cat, width)
-    k = 3 * br
+    k = cat.shape[2]
     total = None
     for a in range(3):
         term = jnp.dot(
             cat[a * RR : a * RR + rest].reshape(rest * width, k), w[a * k : (a + 1) * k, :], preferred_element_type=F32
         )
         total = term if total is None else total + term
-    done[...] = jnp.maximum(total, 0).astype(BF16).reshape(rest, width, br)
+    done[...] = jnp.maximum(total, 0).astype(BF16).reshape(done.shape)
     copy = pltpu.make_async_copy(done, out.at[pl.ds((1 - top) * RR, rest)], sem)
     copy.start()
     centre = cat[pl.ds(top * height, RR)].reshape(RR * width, k)
@@ -266,24 +276,32 @@
     g = len(groups)
     halo = refs[:g]
     sides = refs[g:-6]
-    _, out, ext, cat, done, sem = refs[-6:]
+    _, out, ext, cat, done, sems = refs[-6:]
     top = near_is_top()
     width = cat.shape[1]
-    br = ext.shape[-1]
-    lay_columns(groups, width, cols_n, 0, RR, halo, 0, 3, 0, sides, ext)
+    for i, (cols, _) in enumerate(groups):
+        place(cols, halo[i], 0, RR, ext, 0)
+    place_sides(cols_n, sides, 3, 0, RR, ext, 0)
     spread(ext, cat, width)
-    k = 3 * br
+    k = cat.shape[2]
     outer_w = w[pl.ds(pl.multiple_of(top * 2 * k, k), k), :]
-    total = partial[...] + jnp.dot(cat[...].reshape(RR * width, k), outer_w, preferred_element_type=F32)
-    done[...] = jnp.maximum(total, 0).astype(BF16).reshape(RR, width, br)
-    copy = pltpu.make_async_copy(done, out.at[pl.ds(top * (height - RR), RR)], sem)
-    copy.start()
-    copy.wait()
+    step = RR // LATE
+    copies = []
+    for n in range(LATE):
+        at = n * step
+        taps = cat[at : at + step].reshape(step * width, k)
+        total = partial[at * width : (at + step) * width, :] + jnp.dot(taps, outer_w, preferred_element_type=F32)
+        done[at : at + step] = jnp.maximum(total, 0).astype(BF16).reshape(step, width, done.shape[2])
+        there = out.at[pl.ds(top * (height - RR) + at, step)]
+        copies.append(pltpu.make_async_copy(done.at[pl.ds(at, step)], there, sems.at[n]))
+        copies[-1].start()
+    for copy in copies:
+        copy.wait()
 
 
 def plan(tile_cols):
-    groups = [[0, tile_cols - 1], list(range(1, tile_cols - 1))]
-    order = [(i, near) for i in range(len(groups)) for near in (True, False)]
+    groups = [([0, tile_cols - 1], False), (list(range(1, tile_cols - 1)), True)]
+    order = [(0, True), (0, False), (1, True), (1, False)]
     return groups, order
 
 
@@ -293,7 +311,7 @@
     height, width = tile_rows * TILE, tile_cols * TILE
     assert tile_rows == 2 and pixels == TILE * TILE and TILE < RR <= height <= 2 * RR
     groups, order = plan(tile_cols)
-    chunks = [(groups[i], near) for i, near in order]
+    chunks = [(groups[i][0], one, groups[i][1]) for i, one in order]
     sizes = [span(c, height) * len(c[0]) for c in chunks]
     starts = [sum(sizes[:i]) for i in range(len(sizes))]
     per_row = 2 * (channels * mid + mid * cout + channels * cout + cout * br)
@@ -325,20 +343,21 @@
     cross = [pair for i in range(1, rows_n - 1, 2) for pair in ((i, i + 1), (i + 1, i))]
 
     local, halo = {}, {}
-    for n, (i, near) in enumerate(order):
+    for n, (i, one) in enumerate(order):
         if n == 0:
             value = first
         else:
-            extra = [] if near else [local[i, True]]
+            extra = [] if one else [local[i, True]]
             value = pl.pallas_call(
                 functools.partial(later_chunk, chunks[n], starts[n], height),
-                out_shape=grid_of(groups[i]),
+                out_shape=grid_of(groups[i][0]),
                 in_specs=[SM] + [VM] * (5 + len(extra)),
                 out_specs=VM,
                 compiler_params=params(TRUNK_MIB),
                 cost_estimate=cost(per_row * sizes[n], MIB),
             )(assignment, xs, wr, we, ws, wb, *extra)
-        local[i, near] = value
+        local[i, one] = value
+        near = one == groups[i][1]
         halo[i, near] = lax.ppermute(value, "row", swap if near else cross)
 
     cols_n = lax.axis_size("col")
@@ -395,7 +414,7 @@
             pltpu.VMEM((RR, width + 2 * TILE, br), BF16),
             pltpu.VMEM((RR, width, 3 * br), BF16),
             pltpu.VMEM((RR, width, br), BF16),
-            pltpu.SemaphoreType.DMA,
+            pltpu.SemaphoreType.DMA((LATE,)),
         ],
         compiler_params=params(16),
         cost_estimate=cost(flops * RR, 2 * MIB),

time: 60.7 us -> 56.7 us (0.934); the launches traced: 59.6 us -> 56.4 us
  Pallas kernels: 20.1 us -> 16.5 us
  starting transfers between devices: 16.1 us -> 17.5 us
  waiting for transfers between devices: 23.2 us -> 22 us
    pallas_call x3, Pallas kernels: 4.29 us -> 2.06 us  [shards(): pl.pallas_call(functools.partial(later_chunk, chunks[n], starts[n], heigh...]
    ppermute x4, starting transfers between devices: 14.7 us -> 16.2 us  [shards(): halo[i, near] = lax.ppermute(value, 'row', swap if near else cross)]
    pallas_call x1, Pallas kernels: 10.3 us -> 9.09 us  [shards(): pl.pallas_call(functools.partial(first_chunk, chunks, height), out_shape=...]
    ppermute x4, waiting for transfers between devices: 23.2 us -> 22 us  [shards(): halo[i, near] = lax.ppermute(value, 'row', swap if near else cross)]
  transfers between devices with their start and end apart: 5 -> 5, of which waited for: 3 -> 2; matrix products, arithmetic and copies ran while one was open for 0% -> 0% of each run, Pallas kernels for 9% -> 9%
where the time goes in v3:
time: 56.7 us; the launch traced here: 56.4 us
  waiting for transfers between devices  22 us (39%)
  starting transfers between devices  17.5 us (31%)
  Pallas kernels  16.5 us (29%)
    ppermute x4, waiting for transfers between devices, shards(): halo[i, near] = lax.ppermute(value, 'row', swap if near else cross)  22 us
    ppermute x4, starting transfers between devices, shards(): halo[i, near] = lax.ppermute(value, 'row', swap if near else cross)  16.2 us
    pallas_call x1, Pallas kernels, shards(): pl.pallas_call(functools.partial(first_chunk, chunks, height), out_shape=...  9.09 us
    pallas_call x1, Pallas kernels, shards(): pl.pallas_call(functools.partial(conv_early, groups, cols_n, height), out...  3.9 us
    pallas_call x3, Pallas kernels, shards(): pl.pallas_call(functools.partial(later_chunk, chunks[n], starts[n], heigh...  2.06 us
    pallas_call x1, Pallas kernels, shards(): pl.pallas_call(functools.partial(conv_late, groups, cols_n, height), out_...  1.45 us
    ppermute x1, starting transfers between devices, shards(): sides = [lax.ppermute(picked[0], 'col', [(0, 1), (1, 0)])]  1.32 us
  transfers between devices with their start and end apart: 5, of which 2 were waited for; matrix products, arithmetic and copies ran while one was open for 0% of the time, Pallas kernels for 9%

profile of v3, /device:TPU:9, one launch (start us, length us, event | category | flops | bytes accessed | tf_op | source)
XLA Modules:
  0.0 56.4 jit_solution(7413747733534145207)
XLA Ops:
  0.0 0.0 copy-start.1
  0.0 9.1 %trunk_first.1 = (bf16[18,32,256]{2,1,0:T(8,128)(2,1)S(1)}, bf16[2048,1024]{1,0:T(8,128)(2,1)S(1)}, bf16[1024,512]{1,0:T(8,128)(2,1)S(1)}, bf16[512,2048]{1,0:T(...) custom-call(s32[2,4]{1,0:T(2,128)} %flags.5, bf16[2,4,256,1024]{3,2,1,0:T(8,128)(2,1)} %feats.1, ...), custom_call_target="tpu_custom_call" | custom-call | flops 4831838208 | bytes 12582912 | tf_op jit(solution)/shard_map/trunk_first/pallas_call | solution.py:323
  9.1 0.0 copy-done.1
  9.1 0.6 %shard_map.74.refs_1_.refs_2_ = bf16[18,32,256]{2,1,0:T(8,128)(2,1)S(1)} custom-call(s32[2,4]{1,0:T(2,128)S(1)} %copy-done.1, bf16[2048,1024]{1,0:T(8,128)(2,1)S(1)} %get-tuple-element.14.xs, bf16[1024,512]{1,0:T(8,128)(2,1)S(1)} %get-tuple-element.15.wr, bf16[512,2048]{1,0:T(8,128)(2,1)S(1)} %get-tuple-element.16.we, ...), custom_call_target="tpu_custom_call" | custom-call | flops 3758096384 | bytes 1048576 | tf_op jit(solution)/shard_map/pallas_call | solution.py:351
  9.7 5.4 %collective-permute-start = (bf16[18,32,256]{2,1,0:T(8,128)(2,1)S(1)}, bf16[18,32,256]{2,1,0:T(8,128)(2,1)S(1)}, u32[]{:S(2)}, u32[]{:S(2)}) collective-permute-start(bf16[18,32,256]{2,1,0:T(8,128)(2,1)S(1)} %shard_map.74.refs_1_.refs_2_), channel_id=1, source_target_pairs={{0,2},{2,0},{4,6},{6,4},{8,10},{10,8},{12,14},{14,12},{1,3},{3,1},... | collective-permute-start | bytes 884744 | tf_op jit(solution)/shard_map/ppermute | solution.py:361
  15.2 1.9 %collective-permute-start.2 = (bf16[18,32,256]{2,1,0:T(8,128)(2,1)S(1)}, bf16[18,32,256]{2,1,0:T(8,128)(2,1)S(1)}, u32[]{:S(2)}, u32[]{:S(2)}) collective-permute-start(bf16[18,32,256]{2,1,0:T(8,128)(2,1)S(1)} %get-tuple-element.13.refs_0_), channel_id=1, source_target_pairs={{2,4},{4,2},{6,8},{8,6},{10,12},{12,10},{3,5},{5,3},{7,9},{9,7},{1... | collective-permute-start | bytes 884744 | tf_op jit(solution)/shard_map/ppermute | solution.py:361
  17.1 11.1 %collective-permute-done.refs_2_.refs_4_ = bf16[18,32,256]{2,1,0:T(8,128)(2,1)S(1)} collective-permute-done((bf16[18,32,256]{2,1,0:T(8,128)(2,1)S(1)}, bf16[18,32,256]{2,1,0:T(8,128)(2,1)S(1)}, u32[]{:S(2)}, u32[]{:S(2)}) %collective-permute-start) | collective-permute-done | bytes 294944 | tf_op jit(solution)/shard_map/ppermute | solution.py:361
  28.2 0.0 collective-permute-done.2.refs_3_.refs_0_
  28.3 1.3 %collective-permute-start.3 = (bf16[72,16,256]{2,1,0:T(8,128)(2,1)S(1)}, bf16[72,16,256]{2,1,0:T(8,128)(2,1)S(1)}, u32[]{:S(2)}, u32[]{:S(2)}) collective-permute-start(bf16[72,16,256]{2,1,0:T(8,128)(2,1)S(1)} %pick.1), channel_id=1, source_target_pairs={{0,1},{1,0},{2,3},{3,2},{4,5},{5,4},{6,7},{7,6},{8,9},{9,8},{10,11... | collective-permute-start | bytes 1769480 | tf_op jit(solution)/shard_map/ppermute | solution.py:376
  29.6 0.8 %shard_map.73.refs_0_.refs_1_ = bf16[18,32,256]{2,1,0:T(8,128)(2,1)S(1)} custom-call(s32[2,4]{1,0:T(2,128)S(1)} %copy-done.1, bf16[2048,1024]{1,0:T(8,128)(2,1)S(1)} %get-tuple-element.14.xs, bf16[1024,512]{1,0:T(8,128)(2,1)S(1)} %get-tuple-element.15.wr, bf16[512,2048]{1,0:T(8,128)(2,1)S(1)} %get-tuple-element.16.we, ...), custom_call_target="tpu_custom_call" | custom-call | flops 4831838208 | bytes 1048576 | tf_op jit(solution)/shard_map/pallas_call | solution.py:351
  30.4 0.0 copy-start
  30.4 6.7 %collective-permute-start.1 = (bf16[18,32,256]{2,1,0:T(8,128)(2,1)S(1)}, bf16[18,32,256]{2,1,0:T(8,128)(2,1)S(1)}, u32[]{:S(2)}, u32[]{:S(2)}) collective-permute-start(bf16[18,32,256]{2,1,0:T(8,128)(2,1)S(1)} %shard_map.73.refs_0_.refs_1_), channel_id=1, source_target_pairs={{0,2},{2,0},{4,6},{6,4},{8,10},{10,8},{12,14},{14,12},{1,3},{3,1},... | collective-permute-start | bytes 884744 | tf_op jit(solution)/shard_map/ppermute | solution.py:361
  37.1 0.6 %shard_map.75.refs_3_ = bf16[18,32,256]{2,1,0:T(8,128)(2,1)S(1)} custom-call(s32[2,4]{1,0:T(2,128)S(1)} %copy-done.1, bf16[2048,1024]{1,0:T(8,128)(2,1)S(1)} %get-tuple-element.14.xs, bf16[1024,512]{1,0:T(8,128)(2,1)S(1)} %get-tuple-element.15.wr, bf16[512,2048]{1,0:T(8,128)(2,1)S(1)} %get-tuple-element.16.we, bf16[1024,2048]{1,0:T(8,128)(2,1)S(1)} %get-tuple-element.17.ws, ...), custom_call_target="tpu_custom_call" | custom-call | flops 3758096384 | bytes 1048576 | tf_op jit(solution)/shard_map/pallas_call | solution.py:351
  37.7 2.1 %collective-permute-start.4 = (bf16[18,32,256]{2,1,0:T(8,128)(2,1)S(1)}, bf16[18,32,256]{2,1,0:T(8,128)(2,1)S(1)}, u32[]{:S(2)}, u32[]{:S(2)}) collective-permute-start(bf16[18,32,256]{2,1,0:T(8,128)(2,1)S(1)} %shard_map.75.refs_3_), channel_id=1, source_target_pairs={{2,4},{4,2},{6,8},{8,6},{10,12},{12,10},{3,5},{5,3},{7,9},{9,7},{1... | collective-permute-start | bytes 884744 | tf_op jit(solution)/shard_map/ppermute | solution.py:361
  39.9 10.9 %collective-permute-done.1.refs_5_ = bf16[18,32,256]{2,1,0:T(8,128)(2,1)S(1)} collective-permute-done((bf16[18,32,256]{2,1,0:T(8,128)(2,1)S(1)}, bf16[18,32,256]{2,1,0:T(8,128)(2,1)S(1)}, u32[]{:S(2)}, u32[]{:S(2)}) %collective-permute-start.1) | collective-permute-done | bytes 294944 | tf_op jit(solution)/shard_map/ppermute | solution.py:361
  50.8 0.0 collective-permute-done.3.refs_6_.refs_2_
  50.8 0.0 copy-done
  50.8 3.9 %conv_early.1 = (bf16[32,64,256]{2,1,0:T(8,128)(2,1)}, f32[1152,256]{1,0:T(8,128)S(1)}) custom-call(bf16[2304,256]{1,0:T(8,128)(2,1)S(1)} %bitcast.1, bf16[18,32,256]{2,1,0:T(8,128)(2,1)S(1)} %get-tuple-element.13.refs_0_, bf16[18,32,256]{2,1,0:T(8,128)(2,1)S(1)} %shard_map.73.refs_0_.refs_1_, bf16[18,32,256]{2,1,0:T(8,128)(2,1)S(1)} %shard_map.74.refs_1_.refs_2_, ...), custom_call_target="tpu_custom_call" | custom-call | flops 1962934272 | bytes 4194304 | tf_op jit(solution)/shard_map/conv_early/pallas_call | solution.py:388
  54.7 0.0 collective-permute-done.4.refs_1_
  54.7 1.4 %conv_late.1 = bf16[32,64,256]{2,1,0:T(8,128)(2,1)} custom-call(bf16[2304,256]{1,0:T(8,128)(2,1)S(1)} %bitcast.2, f32[1152,256]{1,0:T(8,128)S(1)} %get-tuple-element.19.partial, bf16[18,32,256]{2,1,0:T(8,128)(2,1)S(1)} %collective-permute-done.2.refs_3_.refs_0_, ...), custom_call_target="tpu_custom_call", output_to_operand_aliasing={{}: (5, {})} | custom-call | flops 452984832 | bytes 2097152 | tf_op jit(solution)/shard_map/conv_late/pallas_call | solution.py:407
  (1 shorter events, 0.0 us)
Async XLA Ops:
  0.0 9.1 %copy-start.1 = (s32[2,4]{1,0:T(2,128)S(1)}, s32[2,4]{1,0:T(2,128)}, u32[]{:S(2)}) copy-start(s32[2,4]{1,0:T(2,128)} %flags.5) | copy-start | bytes 100
  9.7 18.5 %collective-permute-start = (bf16[18,32,256]{2,1,0:T(8,128)(2,1)S(1)}, bf16[18,32,256]{2,1,0:T(8,128)(2,1)S(1)}, u32[]{:S(2)}, u32[]{:S(2)}) collective-permute-start(bf16[18,32,256]{2,1,0:T(8,128)(2,1)S(1)} %shard_map.74.refs_1_.refs_2_), channel_id=1, source_target_pairs={{0,2},{2,0},{4,6},{6,4},{8,10},{10,8},{12,14},{14,12},{1,3},{3,1},... | collective-permute-start | bytes 884744 | tf_op jit(solution)/shard_map/ppermute | solution.py:361
  15.2 13.0 %collective-permute-start.2 = (bf16[18,32,256]{2,1,0:T(8,128)(2,1)S(1)}, bf16[18,32,256]{2,1,0:T(8,128)(2,1)S(1)}, u32[]{:S(2)}, u32[]{:S(2)}) collective-permute-start(bf16[18,32,256]{2,1,0:T(8,128)(2,1)S(1)} %get-tuple-element.13.refs_0_), channel_id=1, source_target_pairs={{2,4},{4,2},{6,8},{8,6},{10,12},{12,10},{3,5},{5,3},{7,9},{9,7},{1... | collective-permute-start | bytes 884744 | tf_op jit(solution)/shard_map/ppermute | solution.py:361
  28.3 22.6 %collective-permute-start.3 = (bf16[72,16,256]{2,1,0:T(8,128)(2,1)S(1)}, bf16[72,16,256]{2,1,0:T(8,128)(2,1)S(1)}, u32[]{:S(2)}, u32[]{:S(2)}) collective-permute-start(bf16[72,16,256]{2,1,0:T(8,128)(2,1)S(1)} %pick.1), channel_id=1, source_target_pairs={{0,1},{1,0},{2,3},{3,2},{4,5},{5,4},{6,7},{7,6},{8,9},{9,8},{10,11... | collective-permute-start | bytes 1769480 | tf_op jit(solution)/shard_map/ppermute | solution.py:376
  30.4 20.4 %copy-start = (bf16[9,256,256]{2,1,0:T(8,128)(2,1)S(1)}, bf16[9,256,256]{2,1,0:T(8,128)(2,1)}, u32[]{:S(2)}) copy-start(bf16[9,256,256]{2,1,0:T(8,128)(2,1)} %param.13) | copy-start | bytes 3538948
  30.4 20.4 %collective-permute-start.1 = (bf16[18,32,256]{2,1,0:T(8,128)(2,1)S(1)}, bf16[18,32,256]{2,1,0:T(8,128)(2,1)S(1)}, u32[]{:S(2)}, u32[]{:S(2)}) collective-permute-start(bf16[18,32,256]{2,1,0:T(8,128)(2,1)S(1)} %shard_map.73.refs_0_.refs_1_), channel_id=1, source_target_pairs={{0,2},{2,0},{4,6},{6,4},{8,10},{10,8},{12,14},{14,12},{1,3},{3,1},... | collective-permute-start | bytes 884744 | tf_op jit(solution)/shard_map/ppermute | solution.py:361
  37.7 17.0 %collective-permute-start.4 = (bf16[18,32,256]{2,1,0:T(8,128)(2,1)S(1)}, bf16[18,32,256]{2,1,0:T(8,128)(2,1)S(1)}, u32[]{:S(2)}, u32[]{:S(2)}) collective-permute-start(bf16[18,32,256]{2,1,0:T(8,128)(2,1)S(1)} %shard_map.75.refs_3_), channel_id=1, source_target_pairs={{2,4},{4,2},{6,8},{8,6},{10,12},{12,10},{3,5},{5,3},{7,9},{9,7},{1... | collective-permute-start | bytes 884744 | tf_op jit(solution)/shard_map/ppermute | solution.py:361

commit v4 on v3

--- a/solution.py
+++ b/solution.py
@@ -13,7 +13,6 @@
 RC = 15
 BLOCK = 512
 DEPTH = 3
-LATE = 3
 F32 = jnp.float32
 BF16 = jnp.bfloat16
 VM = pl.BlockSpec(memory_space=pltpu.VMEM)
@@ -236,71 +235,66 @@
 
 def conv_early(groups, cols_n, height, w, *refs):
     g = len(groups)
-    ones, twos, halo = refs[:g], refs[g : 2 * g], refs[2 * g : 3 * g]
-    sides = refs[3 * g : -6]
-    out, partial, ext, cat, done, sem = refs[-6:]
-    top = near_is_top()
+    ones, twos = refs[:g], refs[g : 2 * g]
+    sides = refs[2 * g : -3]
+    partial, ext, cat = refs[-3:]
     width = cat.shape[1]
     rest = height - RR
-    local = top * RR
     for i, (cols, near_first) in enumerate(groups):
         up = top_of(near_first)
         skip = up * (RR - rest)
-        rows = ((0, ones[i], 0, RR, local + (1 - up) * rest), (1, twos[i], skip, rest, local + up * RR))
-        rows += ((2, halo[i], 0, RR, (1 - top) * height),)
-        for part, src, first, count, row in rows:
+        for part, src, first, count, row in ((0, ones[i], 0, RR, (1 - up) * rest), (1, twos[i], skip, rest, up * RR)):
             place(cols, src, first, count, ext, row)
             if i == 0:
                 place_sides(cols_n, sides, part, first, count, ext, row)
     spread(ext, cat, width)
     k = cat.shape[2]
-    total = None
-    for a in range(3):
-        term = jnp.dot(
-            cat[a * RR : a * RR + rest].reshape(rest * width, k), w[a * k : (a + 1) * k, :], preferred_element_type=F32
-        )
-        total = term if total is None else total + term
-    done[...] = jnp.maximum(total, 0).astype(BF16).reshape(done.shape)
-    copy = pltpu.make_async_copy(done, out.at[pl.ds((1 - top) * RR, rest)], sem)
-    copy.start()
-    centre = cat[pl.ds(top * height, RR)].reshape(RR * width, k)
-    inner = cat[pl.ds(top * rest + (1 - top) * RR, RR)].reshape(RR * width, k)
-    inner_w = w[pl.ds(pl.multiple_of((1 - top) * 2 * k, k), k), :]
-    partial[...] = jnp.dot(centre, w[k : 2 * k, :], preferred_element_type=F32) + jnp.dot(
-        inner, inner_w, preferred_element_type=F32
-    )
-    copy.wait()
+    for at, count in blocks_of(height):
+        total = None
+        for a in range(3):
+            row = at + (a - 1) * RR
+            if 0 <= row < height:
+                taps = cat[row : row + count].reshape(count * width, k)
+                term = jnp.dot(taps, w[a * k : (a + 1) * k, :], preferred_element_type=F32)
+                total = term if total is None else total + term
+        partial[at * width : (at + count) * width, :] = total
 
 
 def conv_late(groups, cols_n, height, w, partial, *refs):
     g = len(groups)
-    halo = refs[:g]
-    sides = refs[g:-6]
-    _, out, ext, cat, done, sems = refs[-6:]
+    near, far = refs[:g], refs[g : 2 * g]
+    sides = refs[2 * g : -5]
+    out, ext, cat, done, sems = refs[-5:]
     top = near_is_top()
     width = cat.shape[1]
-    for i, (cols, _) in enumerate(groups):
-        place(cols, halo[i], 0, RR, ext, 0)
-    place_sides(cols_n, sides, 3, 0, RR, ext, 0)
+    for part, halo, row in ((2, near, (1 - top) * RR), (3, far, top * RR)):
+        for i, (cols, _) in enumerate(groups):
+            place(cols, halo[i], 0, RR, ext, row)
+        place_sides(cols_n, sides, part, 0, RR, ext, row)
     spread(ext, cat, width)
     k = cat.shape[2]
-    outer_w = w[pl.ds(pl.multiple_of(top * 2 * k, k), k), :]
-    step = RR // LATE
     copies = []
-    for n in range(LATE):
-        at = n * step
-        taps = cat[at : at + step].reshape(step * width, k)
-        total = partial[at * width : (at + step) * width, :] + jnp.dot(taps, outer_w, preferred_element_type=F32)
-        done[at : at + step] = jnp.maximum(total, 0).astype(BF16).reshape(step, width, done.shape[2])
-        there = out.at[pl.ds(top * (height - RR) + at, step)]
-        copies.append(pltpu.make_async_copy(done.at[pl.ds(at, step)], there, sems.at[n]))
+    for n, (at, count) in enumerate(blocks_of(height)):
+        total = partial[at * width : (at + count) * width, :]
+        for a, row in ((0, at if at < RR else -1), (2, at - height + 2 * RR if at >= height - RR else -1)):
+            if row >= 0:
+                taps = cat[row : row + count].reshape(count * width, k)
+                total = total + jnp.dot(taps, w[a * k : (a + 1) * k, :], preferred_element_type=F32)
+        done[at : at + count] = jnp.maximum(total, 0).astype(BF16).reshape(count, width, done.shape[2])
+        copies.append(pltpu.make_async_copy(done.at[pl.ds(at, count)], out.at[pl.ds(at, count)], sems.at[n]))
         copies[-1].start()
     for copy in copies:
         copy.wait()
 
 
+def blocks_of(height):
+    rest = height - RR
+    cuts = [0, rest // 2, rest, RR, RR + rest // 2, height]
+    return [(lo, hi - lo) for lo, hi in zip(cuts, cuts[1:]) if hi > lo]
+
+
 def plan(tile_cols):
-    groups = [([0, tile_cols - 1], False), (list(range(1, tile_cols - 1)), True)]
+    groups = [([0, tile_cols - 1], True), (list(range(1, tile_cols - 1)), True)]
     order = [(0, True), (0, False), (1, True), (1, False)]
     return groups, order
 
@@ -381,45 +375,34 @@
         ]
 
     taps = w_dilated.reshape(9 * br, br)
-    rest = height - RR
     n_groups = len(groups)
-    pick = lambda table, near: [table[i, near] for i in range(n_groups)]
+    pick = lambda table, key: [table[i, key] for i in range(n_groups)]
     flops = 2 * width * 3 * br * br
-    out, partial = pl.pallas_call(
+    partial = pl.pallas_call(
         functools.partial(conv_early, groups, cols_n, height),
-        out_shape=[
-            jax.ShapeDtypeStruct((height, width, br), BF16),
-            jax.ShapeDtypeStruct((RR * width, br), F32),
-        ],
-        in_specs=[VM] * (1 + 3 * n_groups + len(sides)),
-        out_specs=[HBM, VM],
-        scratch_shapes=[
-            pltpu.VMEM((height + RR, width + 2 * TILE, br), BF16),
-            pltpu.VMEM((height + RR, width, 3 * br), BF16),
-            pltpu.VMEM((rest, width, br), BF16),
-            pltpu.SemaphoreType.DMA,
-        ],
+        out_shape=jax.ShapeDtypeStruct((height * width, br), F32),
+        in_specs=[VM] * (1 + 2 * n_groups + len(sides)),
+        out_specs=VM,
+        scratch_shapes=[pltpu.VMEM((height, width + 2 * TILE, br), BF16), pltpu.VMEM((height, width, 3 * br), BF16)],
         compiler_params=params(CONV_MIB),
-        cost_estimate=cost(flops * (3 * rest + 2 * RR), 4 * MIB),
+        cost_estimate=cost(flops * (3 * height - 2 * RR), 4 * MIB),
         name="conv_early",
-    )(taps, *pick(local, True), *pick(local, False), *pick(halo, True), *sides)
-    n_in = 2 + n_groups + len(sides)
+    )(taps, *pick(local, True), *pick(local, False), *sides)
     return pl.pallas_call(
         functools.partial(conv_late, groups, cols_n, height),
         out_shape=jax.ShapeDtypeStruct((height, width, br), BF16),
-        in_specs=[VM] * n_in + [HBM],
+        in_specs=[VM] * (2 + 2 * n_groups + len(sides)),
         out_specs=HBM,
-        input_output_aliases={n_in: 0},
         scratch_shapes=[
-            pltpu.VMEM((RR, width + 2 * TILE, br), BF16),
-            pltpu.VMEM((RR, width, 3 * br), BF16),
-            pltpu.VMEM((RR, width, br), BF16),
-            pltpu.SemaphoreType.DMA((LATE,)),
+            pltpu.VMEM((2 * RR, width + 2 * TILE, br), BF16),
+            pltpu.VMEM((2 * RR, width, 3 * br), BF16),
+            pltpu.VMEM((height, width, br), BF16),
+            pltpu.SemaphoreType.DMA((len(blocks_of(height)),)),
         ],
-        compiler_params=params(16),
-        cost_estimate=cost(flops * RR, 2 * MIB),
+        compiler_params=params(CONV_MIB),
+        cost_estimate=cost(flops * 2 * RR, 4 * MIB),
         name="conv_late",
-    )(taps, partial, *pick(halo, False), *sides, out)
+    )(taps, partial, *pick(halo, True), *pick(halo, False), *sides)
 
 
 def solution(mesh):

time: 56.7 us -> 63.2 us (1.11)
  the two profiles are of different devices: /device:TPU:9 before, /device:TPU:18 now
where the time goes in v4:
time: 63.2 us; the launch traced here: 63 us
  Pallas kernels  28.9 us (46%)
  waiting for transfers between devices  24.4 us (39%)
  starting transfers between devices  9.53 us (15%)
    ppermute x4, waiting for transfers between devices, shards(): halo[i, near] = lax.ppermute(value, 'row', swap if near else cross)  24.4 us
    pallas_call x3, Pallas kernels, shards(): pl.pallas_call(functools.partial(later_chunk, chunks[n], starts[n], heigh...  15.4 us
    ppermute x4, starting transfers between devices, shards(): halo[i, near] = lax.ppermute(value, 'row', swap if near else cross)  9.44 us
    pallas_call x1, Pallas kernels, shards(): pl.pallas_call(functools.partial(first_chunk, chunks, height), out_shape=...  9.08 us
    pallas_call x1, Pallas kernels, shards(): pl.pallas_call(functools.partial(conv_late, groups, cols_n, height), out_...  2.37 us
    pallas_call x1, Pallas kernels, shards(): pl.pallas_call(functools.partial(conv_early, groups, cols_n, height), out...  1.94 us
  transfers between devices with their start and end apart: 5, of which 4 were waited for; matrix products, arithmetic and copies ran while one was open for 0% of the time, Pallas kernels for 20%

profile of v4, /device:TPU:18, one launch (start us, length us, event | category | flops | bytes accessed | tf_op | source)
XLA Modules:
  0.0 63.0 jit_solution(4533738029973609872)
XLA Ops:
  0.0 0.0 copy-start.1
  0.0 9.1 %trunk_first.1 = (bf16[18,32,256]{2,1,0:T(8,128)(2,1)S(1)}, bf16[2048,1024]{1,0:T(8,128)(2,1)S(1)}, bf16[1024,512]{1,0:T(8,128)(2,1)S(1)}, bf16[512,2048]{1,0:T(...) custom-call(s32[2,4]{1,0:T(2,128)} %flags.5, bf16[2,4,256,1024]{3,2,1,0:T(8,128)(2,1)} %feats.1, ...), custom_call_target="tpu_custom_call" | custom-call | flops 4831838208 | bytes 12582912 | tf_op jit(solution)/shard_map/trunk_first/pallas_call | solution.py:317
  9.1 0.0 copy-done.1
  9.1 4.7 %shard_map.74.refs_1_.refs_2_ = bf16[18,32,256]{2,1,0:T(8,128)(2,1)S(1)} custom-call(s32[2,4]{1,0:T(2,128)S(1)} %copy-done.1, bf16[2048,1024]{1,0:T(8,128)(2,1)S(1)} %get-tuple-element.12.xs, bf16[1024,512]{1,0:T(8,128)(2,1)S(1)} %get-tuple-element.13.wr, bf16[512,2048]{1,0:T(8,128)(2,1)S(1)} %get-tuple-element.14.we, ...), custom_call_target="tpu_custom_call" | custom-call | flops 3758096384 | bytes 1048576 | tf_op jit(solution)/shard_map/pallas_call | solution.py:345
  13.8 1.9 %collective-permute-start.1 = (bf16[18,32,256]{2,1,0:T(8,128)(2,1)S(1)}, bf16[18,32,256]{2,1,0:T(8,128)(2,1)S(1)}, u32[]{:S(2)}, u32[]{:S(2)}) collective-permute-start(bf16[18,32,256]{2,1,0:T(8,128)(2,1)S(1)} %shard_map.74.refs_1_.refs_2_), channel_id=1, source_target_pairs={{2,4},{4,2},{6,8},{8,6},{10,12},{12,10},{3,5},{5,3},{7,9},{9,7},{1... | collective-permute-start | bytes 884744 | tf_op jit(solution)/shard_map/ppermute | solution.py:355
  15.8 3.1 %collective-permute-start = (bf16[18,32,256]{2,1,0:T(8,128)(2,1)S(1)}, bf16[18,32,256]{2,1,0:T(8,128)(2,1)S(1)}, u32[]{:S(2)}, u32[]{:S(2)}) collective-permute-start(bf16[18,32,256]{2,1,0:T(8,128)(2,1)S(1)} %get-tuple-element.11.refs_0_), channel_id=1, source_target_pairs={{0,2},{2,0},{4,6},{6,4},{8,10},{10,8},{12,14},{14,12},{1,3},{3,1},... | collective-permute-start | bytes 884744 | tf_op jit(solution)/shard_map/ppermute | solution.py:355
  18.9 6.6 %collective-permute-done.1.refs_3_.refs_2_ = bf16[18,32,256]{2,1,0:T(8,128)(2,1)S(1)} collective-permute-done((bf16[18,32,256]{2,1,0:T(8,128)(2,1)S(1)}, bf16[18,32,256]{2,1,0:T(8,128)(2,1)S(1)}, u32[]{:S(2)}, u32[]{:S(2)}) %collective-permute-start.1) | collective-permute-done | bytes 294944 | tf_op jit(solution)/shard_map/ppermute | solution.py:355
  25.5 6.2 %collective-permute-done.refs_2_.refs_0_ = bf16[18,32,256]{2,1,0:T(8,128)(2,1)S(1)} collective-permute-done((bf16[18,32,256]{2,1,0:T(8,128)(2,1)S(1)}, bf16[18,32,256]{2,1,0:T(8,128)(2,1)S(1)}, u32[]{:S(2)}, u32[]{:S(2)}) %collective-permute-start) | collective-permute-done | bytes 294944 | tf_op jit(solution)/shard_map/ppermute | solution.py:355
  31.7 0.1 collective-permute-start.2
  31.8 6.0 %shard_map.73.refs_0_.refs_1_ = bf16[18,32,256]{2,1,0:T(8,128)(2,1)S(1)} custom-call(s32[2,4]{1,0:T(2,128)S(1)} %copy-done.1, bf16[2048,1024]{1,0:T(8,128)(2,1)S(1)} %get-tuple-element.12.xs, bf16[1024,512]{1,0:T(8,128)(2,1)S(1)} %get-tuple-element.13.wr, bf16[512,2048]{1,0:T(8,128)(2,1)S(1)} %get-tuple-element.14.we, ...), custom_call_target="tpu_custom_call" | custom-call | flops 4831838208 | bytes 1048576 | tf_op jit(solution)/shard_map/pallas_call | solution.py:345
  37.8 0.0 copy-start
  37.8 4.7 %shard_map.75.refs_3_ = bf16[18,32,256]{2,1,0:T(8,128)(2,1)S(1)} custom-call(s32[2,4]{1,0:T(2,128)S(1)} %copy-done.1, bf16[2048,1024]{1,0:T(8,128)(2,1)S(1)} %get-tuple-element.12.xs, bf16[1024,512]{1,0:T(8,128)(2,1)S(1)} %get-tuple-element.13.wr, bf16[512,2048]{1,0:T(8,128)(2,1)S(1)} %get-tuple-element.14.we, bf16[1024,2048]{1,0:T(8,128)(2,1)S(1)} %get-tuple-element.15.ws, ...), custom_call_target="tpu_custom_call" | custom-call | flops 3758096384 | bytes 1048576 | tf_op jit(solution)/shard_map/pallas_call | solution.py:345
  42.6 2.1 %collective-permute-start.4 = (bf16[18,32,256]{2,1,0:T(8,128)(2,1)S(1)}, bf16[18,32,256]{2,1,0:T(8,128)(2,1)S(1)}, u32[]{:S(2)}, u32[]{:S(2)}) collective-permute-start(bf16[18,32,256]{2,1,0:T(8,128)(2,1)S(1)} %shard_map.75.refs_3_), channel_id=1, source_target_pairs={{2,4},{4,2},{6,8},{8,6},{10,12},{12,10},{3,5},{5,3},{7,9},{9,7},{1... | collective-permute-start | bytes 884744 | tf_op jit(solution)/shard_map/ppermute | solution.py:355
  44.7 2.3 %collective-permute-start.3 = (bf16[18,32,256]{2,1,0:T(8,128)(2,1)S(1)}, bf16[18,32,256]{2,1,0:T(8,128)(2,1)S(1)}, u32[]{:S(2)}, u32[]{:S(2)}) collective-permute-start(bf16[18,32,256]{2,1,0:T(8,128)(2,1)S(1)} %shard_map.73.refs_0_.refs_1_), channel_id=1, source_target_pairs={{0,2},{2,0},{4,6},{6,4},{8,10},{10,8},{12,14},{14,12},{1,3},{3,1},... | collective-permute-start | bytes 884744 | tf_op jit(solution)/shard_map/ppermute | solution.py:355
  47.0 0.0 collective-permute-done.2.refs_4_
  47.0 0.0 copy-done
  47.0 1.9 %conv_early.1.partial = f32[2048,256]{1,0:T(8,128)S(1)} custom-call(bf16[2304,256]{1,0:T(8,128)(2,1)S(1)} %bitcast.1, bf16[18,32,256]{2,1,0:T(8,128)(2,1)S(1)} %get-tuple-element.11.refs_0_, bf16[18,32,256]{2,1,0:T(8,128)(2,1)S(1)} %shard_map.73.refs_0_.refs_1_, bf16[18,32,256]{2,1,0:T(8,128)(2,1)S(1)} %shard_map.74.refs_1_.refs_2_, ...), custom_call_target="tpu_custom_call" | custom-call | flops 1509949440 | bytes 4194304 | tf_op jit(solution)/shard_map/conv_early/pallas_call | solution.py:381
  49.0 5.9 %collective-permute-done.4.refs_3_ = bf16[18,32,256]{2,1,0:T(8,128)(2,1)S(1)} collective-permute-done((bf16[18,32,256]{2,1,0:T(8,128)(2,1)S(1)}, bf16[18,32,256]{2,1,0:T(8,128)(2,1)S(1)}, u32[]{:S(2)}, u32[]{:S(2)}) %collective-permute-start.4) | collective-permute-done | bytes 294944 | tf_op jit(solution)/shard_map/ppermute | solution.py:355
  54.9 5.6 %collective-permute-done.3.refs_1_ = bf16[18,32,256]{2,1,0:T(8,128)(2,1)S(1)} collective-permute-done((bf16[18,32,256]{2,1,0:T(8,128)(2,1)S(1)}, bf16[18,32,256]{2,1,0:T(8,128)(2,1)S(1)}, u32[]{:S(2)}, u32[]{:S(2)}) %collective-permute-start.3) | collective-permute-done | bytes 294944 | tf_op jit(solution)/shard_map/ppermute | solution.py:355
  60.5 2.4 %conv_late.1 = bf16[32,64,256]{2,1,0:T(8,128)(2,1)} custom-call(bf16[2304,256]{1,0:T(8,128)(2,1)S(1)} %bitcast.2, f32[2048,256]{1,0:T(8,128)S(1)} %conv_early.1.partial, bf16[18,32,256]{2,1,0:T(8,128)(2,1)S(1)} %collective-permute-done.refs_2_.refs_0_, bf16[18,32,256]{2,1,0:T(8,128)(2,1)S(1)} %collective-permute-done.3.refs_1_, ...), custom_call_target="tpu_custom_call" | custom-call | flops 905969664 | bytes 4194304 | tf_op jit(solution)/shard_map/conv_late/pallas_call | solution.py:391
  (1 shorter events, 0.0 us)
Async XLA Ops:
  0.0 9.1 %copy-start.1 = (s32[2,4]{1,0:T(2,128)S(1)}, s32[2,4]{1,0:T(2,128)}, u32[]{:S(2)}) copy-start(s32[2,4]{1,0:T(2,128)} %flags.5) | copy-start | bytes 100
  13.8 11.6 %collective-permute-start.1 = (bf16[18,32,256]{2,1,0:T(8,128)(2,1)S(1)}, bf16[18,32,256]{2,1,0:T(8,128)(2,1)S(1)}, u32[]{:S(2)}, u32[]{:S(2)}) collective-permute-start(bf16[18,32,256]{2,1,0:T(8,128)(2,1)S(1)} %shard_map.74.refs_1_.refs_2_), channel_id=1, source_target_pairs={{2,4},{4,2},{6,8},{8,6},{10,12},{12,10},{3,5},{5,3},{7,9},{9,7},{1... | collective-permute-start | bytes 884744 | tf_op jit(solution)/shard_map/ppermute | solution.py:355
  15.8 15.9 %collective-permute-start = (bf16[18,32,256]{2,1,0:T(8,128)(2,1)S(1)}, bf16[18,32,256]{2,1,0:T(8,128)(2,1)S(1)}, u32[]{:S(2)}, u32[]{:S(2)}) collective-permute-start(bf16[18,32,256]{2,1,0:T(8,128)(2,1)S(1)} %get-tuple-element.11.refs_0_), channel_id=1, source_target_pairs={{0,2},{2,0},{4,6},{6,4},{8,10},{10,8},{12,14},{14,12},{1,3},{3,1},... | collective-permute-start | bytes 884744 | tf_op jit(solution)/shard_map/ppermute | solution.py:355
  31.7 15.3 %collective-permute-start.2 = (bf16[72,16,256]{2,1,0:T(8,128)(2,1)S(1)}, bf16[72,16,256]{2,1,0:T(8,128)(2,1)S(1)}, u32[]{:S(2)}, u32[]{:S(2)}) collective-permute-start(bf16[72,16,256]{2,1,0:T(8,128)(2,1)S(1)} %pick.1), channel_id=1, source_target_pairs={{0,1},{1,0},{2,3},{3,2},{4,5},{5,4},{6,7},{7,6},{8,9},{9,8},{10,11... | collective-permute-start | bytes 1769480 | tf_op jit(solution)/shard_map/ppermute | solution.py:370
  37.8 9.2 %copy-start = (bf16[9,256,256]{2,1,0:T(8,128)(2,1)S(1)}, bf16[9,256,256]{2,1,0:T(8,128)(2,1)}, u32[]{:S(2)}) copy-start(bf16[9,256,256]{2,1,0:T(8,128)(2,1)} %param.13) | copy-start | bytes 3538948
  42.6 12.3 %collective-permute-start.4 = (bf16[18,32,256]{2,1,0:T(8,128)(2,1)S(1)}, bf16[18,32,256]{2,1,0:T(8,128)(2,1)S(1)}, u32[]{:S(2)}, u32[]{:S(2)}) collective-permute-start(bf16[18,32,256]{2,1,0:T(8,128)(2,1)S(1)} %shard_map.75.refs_3_), channel_id=1, source_target_pairs={{2,4},{4,2},{6,8},{8,6},{10,12},{12,10},{3,5},{5,3},{7,9},{9,7},{1... | collective-permute-start | bytes 884744 | tf_op jit(solution)/shard_map/ppermute | solution.py:355
  44.7 15.8 %collective-permute-start.3 = (bf16[18,32,256]{2,1,0:T(8,128)(2,1)S(1)}, bf16[18,32,256]{2,1,0:T(8,128)(2,1)S(1)}, u32[]{:S(2)}, u32[]{:S(2)}) collective-permute-start(bf16[18,32,256]{2,1,0:T(8,128)(2,1)S(1)} %shard_map.73.refs_0_.refs_1_), channel_id=1, source_target_pairs={{0,2},{2,0},{4,6},{6,4},{8,10},{10,8},{12,14},{14,12},{1,3},{3,1},... | collective-permute-start | bytes 884744 | tf_op jit(solution)/shard_map/ppermute | solution.py:355

commit v5 on v4

--- a/solution.py
+++ b/solution.py
@@ -211,19 +211,21 @@
             outs[1][rows] = src[:, :TILE, :]
 
 
-def place(cols, src, first, count, ext, row):
+def place(cols, src, first, count, ext, row, on=None):
     for j, col in enumerate(cols):
-        ext[pl.ds(row, count), (1 + col) * TILE : (2 + col) * TILE, :] = src[
-            pl.ds(first, count), j * TILE : (j + 1) * TILE, :
-        ]
-
-
-def place_sides(cols_n, sides, part, first, count, ext, row):
+        there = src[pl.ds(first, count), j * TILE : (j + 1) * TILE, :]
+        if on is not None:
+            there = jnp.where(on, there, jnp.zeros_like(there))
+        ext[pl.ds(row, count), (1 + col) * TILE : (2 + col) * TILE, :] = there
+
+
+def place_sides(cols_n, sides, part, first, count, ext, row, on=None):
     me = lax.axis_index("col")
     wide = ext.shape[1]
-    for on, at, ref in ((me > 0, 0, sides[0]), (me < cols_n - 1, wide - TILE, sides[-1])):
+    for here, at, ref in ((me > 0, 0, sides[0]), (me < cols_n - 1, wide - TILE, sides[-1])):
         there = ref[pl.ds(part * RR + first, count)]
-        ext[pl.ds(row, count), at : at + TILE, :] = jnp.where(on, there, jnp.zeros_like(there))
+        here = here if on is None else here & on
+        ext[pl.ds(row, count), at : at + TILE, :] = jnp.where(here, there, jnp.zeros_like(there))
 
 
 def spread(ext, cat, width):
@@ -260,17 +262,19 @@
         partial[at * width : (at + count) * width, :] = total
 
 
-def conv_late(groups, cols_n, height, w, partial, *refs):
+def conv_late(groups, rows_n, cols_n, height, w, partial, *refs):
     g = len(groups)
     near, far = refs[:g], refs[g : 2 * g]
     sides = refs[2 * g : -5]
     out, ext, cat, done, sems = refs[-5:]
     top = near_is_top()
     width = cat.shape[1]
-    for part, halo, row in ((2, near, (1 - top) * RR), (3, far, top * RR)):
+    me = lax.axis_index("row")
+    inside = (me > 0) & (me < rows_n - 1)
+    for part, halo, row, on in ((2, near, (1 - top) * RR, None), (3, far, top * RR, inside)):
         for i, (cols, _) in enumerate(groups):
-            place(cols, halo[i], 0, RR, ext, row)
-        place_sides(cols_n, sides, part, 0, RR, ext, row)
+            place(cols, halo[i], 0, RR, ext, row, on)
+        place_sides(cols_n, sides, part, 0, RR, ext, row, on)
     spread(ext, cat, width)
     k = cat.shape[2]
     copies = []
@@ -332,9 +336,23 @@
         name="trunk_first",
     )(*[in_hbm(v) for v in (assignment, features, w_reduce, w_expand, w_short, w_branch)])
 
-    rows_n = lax.axis_size("row")
-    swap = [(i, i ^ 1) for i in range(rows_n) if i ^ 1 < rows_n]
-    cross = [pair for i in range(1, rows_n - 1, 2) for pair in ((i, i + 1), (i + 1, i))]
+    rows_n, cols_n = lax.axis_size("row"), lax.axis_size("col")
+    assert rows_n % 2 == 0 and cols_n % 2 == 0
+
+    def partner(row, col, near):
+        if near:
+            return row ^ 1, col
+        if row in (0, rows_n - 1):
+            return row, col ^ 1
+        return (row + 1 if row % 2 else row - 1), col
+
+    def swap(near):
+        pairs = []
+        for row in range(rows_n):
+            for col in range(cols_n):
+                to_row, to_col = partner(row, col, near)
+                pairs.append((row * cols_n + col, to_row * cols_n + to_col))
+        return pairs
 
     local, halo = {}, {}
     for n, (i, one) in enumerate(order):
@@ -352,9 +370,8 @@
             )(assignment, xs, wr, we, ws, wb, *extra)
         local[i, one] = value
         near = one == groups[i][1]
-        halo[i, near] = lax.ppermute(value, "row", swap if near else cross)
-
-    cols_n = lax.axis_size("col")
+        halo[i, near] = lax.ppermute(value, ("row", "col"), swap(near))
+
     side = jax.ShapeDtypeStruct((4 * RR, TILE, br), BF16)
     one_swap = cols_n == 2
     picked = pl.pallas_call(
@@ -389,7 +406,7 @@
         name="conv_early",
     )(taps, *pick(local, True), *pick(local, False), *sides)
     return pl.pallas_call(
-        functools.partial(conv_late, groups, cols_n, height),
+        functools.partial(conv_late, groups, rows_n, cols_n, height),
         out_shape=jax.ShapeDtypeStruct((height, width, br), BF16),
         in_specs=[VM] * (2 + 2 * n_groups + len(sides)),
         out_specs=HBM,

time: 63.2 us -> 59.6 us (0.943)
  starting transfers between devices: 9.53 us -> 5.45 us
    ppermute x4, starting transfers between devices: 9.44 us -> 5.37 us  [shards(): halo[i, near] = lax.ppermute(value, ('row', 'col'), swap(near))]
  transfers between devices with their start and end apart: 5 -> 5, of which waited for: 4 -> 4; matrix products, arithmetic and copies ran while one was open for 0% -> 0% of each run, Pallas kernels for 20% -> 22%
where the time goes in v5:
time: 59.6 us; the launch traced here: 59.4 us
  Pallas kernels  29.1 us (49%)
  waiting for transfers between devices  24.6 us (41%)
  starting transfers between devices  5.45 us (9%)
    ppermute x4, waiting for transfers between devices, shards(): halo[i, near] = lax.ppermute(value, ('row', 'col'), swap(near))  24.6 us
    pallas_call x3, Pallas kernels, shards(): pl.pallas_call(functools.partial(later_chunk, chunks[n], starts[n], heigh...  15.7 us
    pallas_call x1, Pallas kernels, shards(): pl.pallas_call(functools.partial(first_chunk, chunks, height), out_shape=...  9.08 us
    ppermute x4, starting transfers between devices, shards(): halo[i, near] = lax.ppermute(value, ('row', 'col'), swap(near))  5.37 us
    pallas_call x1, Pallas kernels, shards(): pl.pallas_call(functools.partial(conv_late, groups, rows_n, cols_n, heigh...  2.41 us
    pallas_call x1, Pallas kernels, shards(): pl.pallas_call(functools.partial(conv_early, groups, cols_n, height), out...  1.94 us
  transfers between devices with their start and end apart: 5, of which 4 were waited for; matrix products, arithmetic and copies ran while one was open for 0% of the time, Pallas kernels for 22%

profile of v5, /device:TPU:18, one launch (start us, length us, event | category | flops | bytes accessed | tf_op | source)
XLA Modules:
  0.0 59.4 jit_solution(3118011750474879571)
XLA Ops:
  0.0 0.0 copy-start.1
  0.0 9.1 %trunk_first.1 = (bf16[18,32,256]{2,1,0:T(8,128)(2,1)S(1)}, bf16[2048,1024]{1,0:T(8,128)(2,1)S(1)}, bf16[1024,512]{1,0:T(8,128)(2,1)S(1)}, bf16[512,2048]{1,0:T(...) custom-call(s32[2,4]{1,0:T(2,128)} %flags.5, bf16[2,4,256,1024]{3,2,1,0:T(8,128)(2,1)} %feats.1, ...), custom_call_target="tpu_custom_call" | custom-call | flops 4831838208 | bytes 12582912 | tf_op jit(solution)/shard_map/trunk_first/pallas_call | solution.py:321
  9.1 0.0 copy-done.1
  9.1 4.7 %shard_map.74.refs_1_.refs_2_ = bf16[18,32,256]{2,1,0:T(8,128)(2,1)S(1)} custom-call(s32[2,4]{1,0:T(2,128)S(1)} %copy-done.1, bf16[2048,1024]{1,0:T(8,128)(2,1)S(1)} %get-tuple-element.12.xs, bf16[1024,512]{1,0:T(8,128)(2,1)S(1)} %get-tuple-element.13.wr, bf16[512,2048]{1,0:T(8,128)(2,1)S(1)} %get-tuple-element.14.we, ...), custom_call_target="tpu_custom_call" | custom-call | flops 3758096384 | bytes 1048576 | tf_op jit(solution)/shard_map/pallas_call | solution.py:363
  13.8 0.1 collective-permute-start.1
  13.9 3.0 %collective-permute-start = (bf16[18,32,256]{2,1,0:T(8,128)(2,1)S(1)}, bf16[18,32,256]{2,1,0:T(8,128)(2,1)S(1)}, u32[]{:S(2)}, u32[]{:S(2)}) collective-permute-start(bf16[18,32,256]{2,1,0:T(8,128)(2,1)S(1)} %get-tuple-element.11.refs_0_), channel_id=1, source_target_pairs={{0,2},{1,3},{2,0},{3,1},{4,6},{5,7},{6,4},{7,5},{8,10},{9,11},{10,... | collective-permute-start | bytes 884744 | tf_op jit(solution)/shard_map/ppermute | solution.py:373
  16.9 6.7 %collective-permute-done.1.refs_3_.refs_2_ = bf16[18,32,256]{2,1,0:T(8,128)(2,1)S(1)} collective-permute-done((bf16[18,32,256]{2,1,0:T(8,128)(2,1)S(1)}, bf16[18,32,256]{2,1,0:T(8,128)(2,1)S(1)}, u32[]{:S(2)}, u32[]{:S(2)}) %collective-permute-start.1) | collective-permute-done | bytes 294944 | tf_op jit(solution)/shard_map/ppermute | solution.py:373
  23.7 6.2 %collective-permute-done.refs_2_.refs_0_ = bf16[18,32,256]{2,1,0:T(8,128)(2,1)S(1)} collective-permute-done((bf16[18,32,256]{2,1,0:T(8,128)(2,1)S(1)}, bf16[18,32,256]{2,1,0:T(8,128)(2,1)S(1)}, u32[]{:S(2)}, u32[]{:S(2)}) %collective-permute-start) | collective-permute-done | bytes 294944 | tf_op jit(solution)/shard_map/ppermute | solution.py:373
  29.9 0.1 collective-permute-start.2
  30.0 6.0 %shard_map.73.refs_0_.refs_1_ = bf16[18,32,256]{2,1,0:T(8,128)(2,1)S(1)} custom-call(s32[2,4]{1,0:T(2,128)S(1)} %copy-done.1, bf16[2048,1024]{1,0:T(8,128)(2,1)S(1)} %get-tuple-element.12.xs, bf16[1024,512]{1,0:T(8,128)(2,1)S(1)} %get-tuple-element.13.wr, bf16[512,2048]{1,0:T(8,128)(2,1)S(1)} %get-tuple-element.14.we, ...), custom_call_target="tpu_custom_call" | custom-call | flops 4831838208 | bytes 1048576 | tf_op jit(solution)/shard_map/pallas_call | solution.py:363
  36.0 0.0 copy-start
  36.0 4.9 %shard_map.75.refs_3_ = bf16[18,32,256]{2,1,0:T(8,128)(2,1)S(1)} custom-call(s32[2,4]{1,0:T(2,128)S(1)} %copy-done.1, bf16[2048,1024]{1,0:T(8,128)(2,1)S(1)} %get-tuple-element.12.xs, bf16[1024,512]{1,0:T(8,128)(2,1)S(1)} %get-tuple-element.13.wr, bf16[512,2048]{1,0:T(8,128)(2,1)S(1)} %get-tuple-element.14.we, bf16[1024,2048]{1,0:T(8,128)(2,1)S(1)} %get-tuple-element.15.ws, ...), custom_call_target="tpu_custom_call" | custom-call | flops 3758096384 | bytes 1048576 | tf_op jit(solution)/shard_map/pallas_call | solution.py:363
  41.0 0.1 collective-permute-start.4
  41.0 2.2 %collective-permute-start.3 = (bf16[18,32,256]{2,1,0:T(8,128)(2,1)S(1)}, bf16[18,32,256]{2,1,0:T(8,128)(2,1)S(1)}, u32[]{:S(2)}, u32[]{:S(2)}) collective-permute-start(bf16[18,32,256]{2,1,0:T(8,128)(2,1)S(1)} %shard_map.73.refs_0_.refs_1_), channel_id=1, source_target_pairs={{0,2},{1,3},{2,0},{3,1},{4,6},{5,7},{6,4},{7,5},{8,10},{9,11},{10,... | collective-permute-start | bytes 884744 | tf_op jit(solution)/shard_map/ppermute | solution.py:373
  43.2 0.0 collective-permute-done.2.refs_4_
  43.2 0.0 copy-done
  43.2 1.9 %conv_early.1.partial = f32[2048,256]{1,0:T(8,128)S(1)} custom-call(bf16[2304,256]{1,0:T(8,128)(2,1)S(1)} %bitcast.1, bf16[18,32,256]{2,1,0:T(8,128)(2,1)S(1)} %get-tuple-element.11.refs_0_, bf16[18,32,256]{2,1,0:T(8,128)(2,1)S(1)} %shard_map.73.refs_0_.refs_1_, bf16[18,32,256]{2,1,0:T(8,128)(2,1)S(1)} %shard_map.74.refs_1_.refs_2_, ...), custom_call_target="tpu_custom_call" | custom-call | flops 1509949440 | bytes 4194304 | tf_op jit(solution)/shard_map/conv_early/pallas_call | solution.py:398
  45.2 6.2 %collective-permute-done.4.refs_3_ = bf16[18,32,256]{2,1,0:T(8,128)(2,1)S(1)} collective-permute-done((bf16[18,32,256]{2,1,0:T(8,128)(2,1)S(1)}, bf16[18,32,256]{2,1,0:T(8,128)(2,1)S(1)}, u32[]{:S(2)}, u32[]{:S(2)}) %collective-permute-start.4) | collective-permute-done | bytes 294944 | tf_op jit(solution)/shard_map/ppermute | solution.py:373
  51.4 5.4 %collective-permute-done.3.refs_1_ = bf16[18,32,256]{2,1,0:T(8,128)(2,1)S(1)} collective-permute-done((bf16[18,32,256]{2,1,0:T(8,128)(2,1)S(1)}, bf16[18,32,256]{2,1,0:T(8,128)(2,1)S(1)}, u32[]{:S(2)}, u32[]{:S(2)}) %collective-permute-start.3) | collective-permute-done | bytes 294944 | tf_op jit(solution)/shard_map/ppermute | solution.py:373
  56.8 2.4 %conv_late.1 = bf16[32,64,256]{2,1,0:T(8,128)(2,1)} custom-call(bf16[2304,256]{1,0:T(8,128)(2,1)S(1)} %bitcast.2, f32[2048,256]{1,0:T(8,128)S(1)} %conv_early.1.partial, bf16[18,32,256]{2,1,0:T(8,128)(2,1)S(1)} %collective-permute-done.refs_2_.refs_0_, bf16[18,32,256]{2,1,0:T(8,128)(2,1)S(1)} %collective-permute-done.3.refs_1_, ...), custom_call_target="tpu_custom_call" | custom-call | flops 905969664 | bytes 4194304 | tf_op jit(solution)/shard_map/conv_late/pallas_call | solution.py:408
  (1 shorter events, 0.0 us)
Async XLA Ops:
  0.0 9.1 %copy-start.1 = (s32[2,4]{1,0:T(2,128)S(1)}, s32[2,4]{1,0:T(2,128)}, u32[]{:S(2)}) copy-start(s32[2,4]{1,0:T(2,128)} %flags.5) | copy-start | bytes 100
  13.8 9.8 %collective-permute-start.1 = (bf16[18,32,256]{2,1,0:T(8,128)(2,1)S(1)}, bf16[18,32,256]{2,1,0:T(8,128)(2,1)S(1)}, u32[]{:S(2)}, u32[]{:S(2)}) collective-permute-start(bf16[18,32,256]{2,1,0:T(8,128)(2,1)S(1)} %shard_map.74.refs_1_.refs_2_), channel_id=1, source_target_pairs={{0,1},{1,0},{2,4},{3,5},{4,2},{5,3},{6,8},{7,9},{8,6},{9,7},{10,12... | collective-permute-start | bytes 884744 | tf_op jit(solution)/shard_map/ppermute | solution.py:373
  13.9 16.0 %collective-permute-start = (bf16[18,32,256]{2,1,0:T(8,128)(2,1)S(1)}, bf16[18,32,256]{2,1,0:T(8,128)(2,1)S(1)}, u32[]{:S(2)}, u32[]{:S(2)}) collective-permute-start(bf16[18,32,256]{2,1,0:T(8,128)(2,1)S(1)} %get-tuple-element.11.refs_0_), channel_id=1, source_target_pairs={{0,2},{1,3},{2,0},{3,1},{4,6},{5,7},{6,4},{7,5},{8,10},{9,11},{10,... | collective-permute-start | bytes 884744 | tf_op jit(solution)/shard_map/ppermute | solution.py:373
  29.9 13.3 %collective-permute-start.2 = (bf16[72,16,256]{2,1,0:T(8,128)(2,1)S(1)}, bf16[72,16,256]{2,1,0:T(8,128)(2,1)S(1)}, u32[]{:S(2)}, u32[]{:S(2)}) collective-permute-start(bf16[72,16,256]{2,1,0:T(8,128)(2,1)S(1)} %pick.1), channel_id=1, source_target_pairs={{0,1},{1,0},{2,3},{3,2},{4,5},{5,4},{6,7},{7,6},{8,9},{9,8},{10,11... | collective-permute-start | bytes 1769480 | tf_op jit(solution)/shard_map/ppermute | solution.py:387
  36.0 7.3 %copy-start = (bf16[9,256,256]{2,1,0:T(8,128)(2,1)S(1)}, bf16[9,256,256]{2,1,0:T(8,128)(2,1)}, u32[]{:S(2)}) copy-start(bf16[9,256,256]{2,1,0:T(8,128)(2,1)} %param.13) | copy-start | bytes 3538948
  41.0 10.5 %collective-permute-start.4 = (bf16[18,32,256]{2,1,0:T(8,128)(2,1)S(1)}, bf16[18,32,256]{2,1,0:T(8,128)(2,1)S(1)}, u32[]{:S(2)}, u32[]{:S(2)}) collective-permute-start(bf16[18,32,256]{2,1,0:T(8,128)(2,1)S(1)} %shard_map.75.refs_3_), channel_id=1, source_target_pairs={{0,1},{1,0},{2,4},{3,5},{4,2},{5,3},{6,8},{7,9},{8,6},{9,7},{10,12... | collective-permute-start | bytes 884744 | tf_op jit(solution)/shard_map/ppermute | solution.py:373
  41.0 15.8 %collective-permute-start.3 = (bf16[18,32,256]{2,1,0:T(8,128)(2,1)S(1)}, bf16[18,32,256]{2,1,0:T(8,128)(2,1)S(1)}, u32[]{:S(2)}, u32[]{:S(2)}) collective-permute-start(bf16[18,32,256]{2,1,0:T(8,128)(2,1)S(1)} %shard_map.73.refs_0_.refs_1_), channel_id=1, source_target_pairs={{0,2},{1,3},{2,0},{3,1},{4,6},{5,7},{6,4},{7,5},{8,10},{9,11},{10,... | collective-permute-start | bytes 884744 | tf_op jit(solution)/shard_map/ppermute | solution.py:373

commit v6 on v5

--- a/solution.py
+++ b/solution.py
@@ -13,6 +13,7 @@
 RC = 15
 BLOCK = 512
 DEPTH = 3
+WAITS = (1, 3)
 F32 = jnp.float32
 BF16 = jnp.bfloat16
 VM = pl.BlockSpec(memory_space=pltpu.VMEM)
@@ -109,8 +110,11 @@
         else:
             later += moves
     steps[0].append((wr_h, wr))
-    for k in range(0, we.shape[1], BLOCK):
-        cols = pl.ds(k, BLOCK)
+    ends = [sum(WAITS[: i + 1]) for i in range(len(WAITS))]
+    first_of = {}
+    for i, n_blocks in enumerate(WAITS):
+        first_of[1 + ends[i] - n_blocks] = 1 + i
+        cols = pl.ds((ends[i] - n_blocks) * BLOCK, n_blocks * BLOCK)
         steps.append(
             [(ws_h.at[:, cols], ws.at[:, cols]), (we_h.at[:, cols], we.at[:, cols]), (wb_h.at[cols, :], wb.at[cols, :])]
         )
@@ -137,7 +141,7 @@
     ready(0)
     per = span(chunks[0], height)
     cols = columns_of(chunks[0])
-    reduced = trunk_rows(xs[0 : per * len(cols), :], wr, we, ws, wb, lambda k: ready(k) if k else None)
+    reduced = trunk_rows(xs[0 : per * len(cols), :], wr, we, ws, wb, lambda k: ready(first_of[k]) if k in first_of else None)
     for j, col in enumerate(cols):
         put_column(reduced[j * per : (j + 1) * per], chunks[0], col, j, top_of(chunks[0][2]), flags, out)
     for k in range(n_weights, len(copies)):
@@ -235,56 +239,87 @@
         cat[:, :, b * br : (b + 1) * br] = ext[:, left : left + width, :]
 
 
-def conv_early(groups, cols_n, height, w, *refs):
+def conv_early(groups, rows_n, cols_n, height, w, *refs):
     g = len(groups)
     ones, twos = refs[:g], refs[g : 2 * g]
-    sides = refs[2 * g : -3]
+    near, far = refs[2 * g : 2 * g + 2]
+    sides = refs[2 * g + 2 : -3]
     partial, ext, cat = refs[-3:]
     width = cat.shape[1]
     rest = height - RR
+    top = near_is_top()
     for i, (cols, near_first) in enumerate(groups):
         up = top_of(near_first)
         skip = up * (RR - rest)
-        for part, src, first, count, row in ((0, ones[i], 0, RR, (1 - up) * rest), (1, twos[i], skip, rest, up * RR)):
-            place(cols, src, first, count, ext, row)
+        rows = [(0, ones[i], 0, RR, RR + (1 - up) * rest, None), (1, twos[i], skip, rest, RR + up * RR, None)]
+        if i == 0:
+            rows += [(2, near, 0, RR, (1 - top) * (RR + height), None)]
+            rows += [(3, far, 0, RR, top * (RR + height), far_inside(rows_n))]
+        for part, src, first, count, row, on in rows:
+            place(cols, src, first, count, ext, row, on)
             if i == 0:
-                place_sides(cols_n, sides, part, first, count, ext, row)
+                place_sides(cols_n, sides, part, first, count, ext, row, on)
+    for cols, _ in groups[1:]:
+        for col in cols:
+            at = (1 + col) * TILE
+            zero = jnp.zeros((RR, TILE, ext.shape[2]), BF16)
+            ext[0:RR, at : at + TILE, :] = zero
+            ext[RR + height :, at : at + TILE, :] = zero
     spread(ext, cat, width)
     k = cat.shape[2]
     for at, count in blocks_of(height):
         total = None
         for a in range(3):
-            row = at + (a - 1) * RR
-            if 0 <= row < height:
-                taps = cat[row : row + count].reshape(count * width, k)
-                term = jnp.dot(taps, w[a * k : (a + 1) * k, :], preferred_element_type=F32)
-                total = term if total is None else total + term
-        partial[at * width : (at + count) * width, :] = total
-
-
-def conv_late(groups, rows_n, cols_n, height, w, partial, *refs):
-    g = len(groups)
+            taps = cat[at + a * RR : at + a * RR + count].reshape(count * width, k)
+            term = jnp.dot(taps, w[a * k : (a + 1) * k, :], preferred_element_type=F32)
+            total = term if total is None else total + term
+        partial[at : at + count] = total.reshape(count, width, total.shape[1])
+
+
+def far_inside(rows_n):
+    me = lax.axis_index("row")
+    return (me > 0) & (me < rows_n - 1)
+
+
+def conv_late(groups, rows_n, height, w, partial, *refs):
+    g = len(groups) - 1
     near, far = refs[:g], refs[g : 2 * g]
-    sides = refs[2 * g : -5]
-    out, ext, cat, done, sems = refs[-5:]
+    out, apart, done, sems = refs[-4:]
     top = near_is_top()
-    width = cat.shape[1]
-    me = lax.axis_index("row")
-    inside = (me > 0) & (me < rows_n - 1)
-    for part, halo, row, on in ((2, near, (1 - top) * RR, None), (3, far, top * RR, inside)):
-        for i, (cols, _) in enumerate(groups):
-            place(cols, halo[i], 0, RR, ext, row, on)
-        place_sides(cols_n, sides, part, 0, RR, ext, row, on)
-    spread(ext, cat, width)
-    k = cat.shape[2]
+    width, br = partial.shape[1:]
+    used = sorted(col for cols, _ in groups[1:] for col in cols)
+    lo, hi = used[0] * TILE, (used[-1] + 1) * TILE
+    zero = jnp.zeros((2 * RR, TILE, br), F32)
+    for b in range(3):
+        apart[b, :, 0:TILE, :] = zero
+        apart[b, :, TILE + hi - lo : 2 * TILE + hi - lo, :] = zero
+    for halo, row, a, on in ((near, (1 - top) * RR, (1 - top) * 2, None), (far, top * RR, top * 2, far_inside(rows_n))):
+        for i, (cols, _) in enumerate(groups[1:]):
+            there = halo[i][...]
+            if on is not None:
+                there = jnp.where(on, there, jnp.zeros_like(there))
+            there = there.reshape(RR * len(cols) * TILE, br)
+            for b in range(3):
+                tap = w[pl.ds(pl.multiple_of((3 * a + b) * br, br), br), :]
+                term = jnp.dot(there, tap, preferred_element_type=F32).reshape(RR, len(cols) * TILE, br)
+                for j, col in enumerate(cols):
+                    at = (1 + col) * TILE - lo
+                    apart[b, pl.ds(row, RR), at : at + TILE, :] = term[:, j * TILE : (j + 1) * TILE, :]
+    reach = []
+    for b in range(3):
+        shift = (b - 1) * RC
+        reach.append((max(0, lo - shift) // TILE * TILE, min(width, -(-(hi - shift) // TILE) * TILE)))
+    cuts = sorted({0, width, *[edge for span_b in reach for edge in span_b]})
     copies = []
     for n, (at, count) in enumerate(blocks_of(height)):
-        total = partial[at * width : (at + count) * width, :]
-        for a, row in ((0, at if at < RR else -1), (2, at - height + 2 * RR if at >= height - RR else -1)):
-            if row >= 0:
-                taps = cat[row : row + count].reshape(count * width, k)
-                total = total + jnp.dot(taps, w[a * k : (a + 1) * k, :], preferred_element_type=F32)
-        done[at : at + count] = jnp.maximum(total, 0).astype(BF16).reshape(count, width, done.shape[2])
+        for left, right in zip(cuts, cuts[1:]):
+            total = partial[at : at + count, left:right, :]
+            for row in (at if at < RR else -1, at - height + 2 * RR if at >= height - RR else -1):
+                for b in range(3):
+                    if row >= 0 and reach[b][0] <= left and right <= reach[b][1]:
+                        first = left + (b - 1) * RC + TILE - lo
+                        total = total + apart[b, row : row + count, first : first + right - left, :]
+            done[at : at + count, left:right, :] = jnp.maximum(total, 0).astype(BF16)
         copies.append(pltpu.make_async_copy(done.at[pl.ds(at, count)], out.at[pl.ds(at, count)], sems.at[n]))
         copies[-1].start()
     for copy in copies:
@@ -395,31 +430,35 @@
     n_groups = len(groups)
     pick = lambda table, key: [table[i, key] for i in range(n_groups)]
     flops = 2 * width * 3 * br * br
+    edge_halos = [halo[0, True], halo[0, False]]
     partial = pl.pallas_call(
-        functools.partial(conv_early, groups, cols_n, height),
-        out_shape=jax.ShapeDtypeStruct((height * width, br), F32),
-        in_specs=[VM] * (1 + 2 * n_groups + len(sides)),
+        functools.partial(conv_early, groups, rows_n, cols_n, height),
+        out_shape=jax.ShapeDtypeStruct((height, width, br), F32),
+        in_specs=[VM] * (3 + 2 * n_groups + len(sides)),
         out_specs=VM,
-        scratch_shapes=[pltpu.VMEM((height, width + 2 * TILE, br), BF16), pltpu.VMEM((height, width, 3 * br), BF16)],
+        scratch_shapes=[
+            pltpu.VMEM((height + 2 * RR, width + 2 * TILE, br), BF16),
+            pltpu.VMEM((height + 2 * RR, width, 3 * br), BF16),
+        ],
         compiler_params=params(CONV_MIB),
-        cost_estimate=cost(flops * (3 * height - 2 * RR), 4 * MIB),
+        cost_estimate=cost(flops * 3 * height, 4 * MIB),
         name="conv_early",
-    )(taps, *pick(local, True), *pick(local, False), *sides)
+    )(taps, *pick(local, True), *pick(local, False), *edge_halos, *sides)
+    inner = sum(len(cols) for cols, _ in groups[1:]) * TILE
     return pl.pallas_call(
-        functools.partial(conv_late, groups, rows_n, cols_n, height),
+        functools.partial(conv_late, groups, rows_n, height),
         out_shape=jax.ShapeDtypeStruct((height, width, br), BF16),
-        in_specs=[VM] * (2 + 2 * n_groups + len(sides)),
+        in_specs=[VM] * (2 * n_groups),
         out_specs=HBM,
         scratch_shapes=[
-            pltpu.VMEM((2 * RR, width + 2 * TILE, br), BF16),
-            pltpu.VMEM((2 * RR, width, 3 * br), BF16),
+            pltpu.VMEM((3, 2 * RR, inner + 2 * TILE, br), F32),
             pltpu.VMEM((height, width, br), BF16),
             pltpu.SemaphoreType.DMA((len(blocks_of(height)),)),
         ],
         compiler_params=params(CONV_MIB),
-        cost_estimate=cost(flops * 2 * RR, 4 * MIB),
+        cost_estimate=cost(flops * RR, 4 * MIB),
         name="conv_late",
-    )(taps, partial, *pick(halo, True), *pick(halo, False), *sides)
+    )(taps, partial, *pick(halo, True)[1:], *pick(halo, False)[1:])
 
 
 def solution(mesh):

time: 59.6 us -> 58.5 us (0.982)
  waiting for transfers between devices: 24.6 us -> 23.5 us
    ppermute x4, waiting for transfers between devices: 24.6 us -> 23.5 us  [shards(): halo[i, near] = lax.ppermute(value, ('row', 'col'), swap(near))]
    pallas_call x1, Pallas kernels: 9.08 us -> 7.99 us  [shards(): pl.pallas_call(functools.partial(first_chunk, chunks, height), out_shape=...]
    pallas_call x2, Pallas kernels: 4.35 us -> 5.42 us  [the longest x1 3.03 us: shards(): pl.pallas_call(functools.partial(conv_early, groups, rows_n, cols_n, heig...]
  transfers between devices with their start and end apart: 5 -> 5, of which waited for: 4 -> 4; matrix products, arithmetic and copies ran while one was open for 0% -> 0% of each run, Pallas kernels for 22% -> 24%
where the time goes in v6:
time: 58.5 us; the launch traced here: 58.4 us
  Pallas kernels  29.2 us (50%)
  waiting for transfers between devices  23.5 us (40%)
  starting transfers between devices  5.44 us (9%)
    ppermute x4, waiting for transfers between devices, shards(): halo[i, near] = lax.ppermute(value, ('row', 'col'), swap(near))  23.5 us
    pallas_call x3, Pallas kernels, shards(): pl.pallas_call(functools.partial(later_chunk, chunks[n], starts[n], heigh...  15.7 us
    pallas_call x1, Pallas kernels, shards(): pl.pallas_call(functools.partial(first_chunk, chunks, height), out_shape=...  7.99 us
    ppermute x4, starting transfers between devices, shards(): halo[i, near] = lax.ppermute(value, ('row', 'col'), swap(near))  5.36 us
    pallas_call x1, Pallas kernels, shards(): pl.pallas_call(functools.partial(conv_early, groups, rows_n, cols_n, heig...  3.03 us
    pallas_call x1, Pallas kernels, shards(): pl.pallas_call(functools.partial(conv_late, groups, rows_n, height), out_...  2.39 us
  transfers between devices with their start and end apart: 5, of which 4 were waited for; matrix products, arithmetic and copies ran while one was open for 0% of the time, Pallas kernels for 24%

profile of v6, /device:TPU:18, one launch (start us, length us, event | category | flops | bytes accessed | tf_op | source)
XLA Modules:
  0.0 58.4 jit_solution(14476659875937361248)
XLA Ops:
  0.0 0.0 copy-start.1
  0.0 8.0 %trunk_first.1 = (bf16[18,32,256]{2,1,0:T(8,128)(2,1)S(1)}, bf16[2048,1024]{1,0:T(8,128)(2,1)S(1)}, bf16[1024,512]{1,0:T(8,128)(2,1)S(1)}, bf16[512,2048]{1,0:T(...) custom-call(s32[2,4]{1,0:T(2,128)} %flags.5, bf16[2,4,256,1024]{3,2,1,0:T(8,128)(2,1)} %feats.1, ...), custom_call_target="tpu_custom_call" | custom-call | flops 4831838208 | bytes 12582912 | tf_op jit(solution)/shard_map/trunk_first/pallas_call | solution.py:356
  8.0 0.0 copy-done.1
  8.0 4.8 %shard_map.74.refs_1_.refs_2_ = bf16[18,32,256]{2,1,0:T(8,128)(2,1)S(1)} custom-call(s32[2,4]{1,0:T(2,128)S(1)} %copy-done.1, bf16[2048,1024]{1,0:T(8,128)(2,1)S(1)} %get-tuple-element.12.xs, bf16[1024,512]{1,0:T(8,128)(2,1)S(1)} %get-tuple-element.13.wr, bf16[512,2048]{1,0:T(8,128)(2,1)S(1)} %get-tuple-element.14.we, ...), custom_call_target="tpu_custom_call" | custom-call | flops 3758096384 | bytes 1048576 | tf_op jit(solution)/shard_map/pallas_call | solution.py:398
  12.8 0.1 collective-permute-start.1
  12.9 3.0 %collective-permute-start = (bf16[18,32,256]{2,1,0:T(8,128)(2,1)S(1)}, bf16[18,32,256]{2,1,0:T(8,128)(2,1)S(1)}, u32[]{:S(2)}, u32[]{:S(2)}) collective-permute-start(bf16[18,32,256]{2,1,0:T(8,128)(2,1)S(1)} %get-tuple-element.11.refs_0_), channel_id=1, source_target_pairs={{0,2},{1,3},{2,0},{3,1},{4,6},{5,7},{6,4},{7,5},{8,10},{9,11},{10,... | collective-permute-start | bytes 884744 | tf_op jit(solution)/shard_map/ppermute | solution.py:408
  15.9 6.7 %collective-permute-done.1.refs_3_.refs_5_ = bf16[18,32,256]{2,1,0:T(8,128)(2,1)S(1)} collective-permute-done((bf16[18,32,256]{2,1,0:T(8,128)(2,1)S(1)}, bf16[18,32,256]{2,1,0:T(8,128)(2,1)S(1)}, u32[]{:S(2)}, u32[]{:S(2)}) %collective-permute-start.1) | collective-permute-done | bytes 294944 | tf_op jit(solution)/shard_map/ppermute | solution.py:408
  22.6 6.2 %collective-permute-done.refs_2_.refs_4_ = bf16[18,32,256]{2,1,0:T(8,128)(2,1)S(1)} collective-permute-done((bf16[18,32,256]{2,1,0:T(8,128)(2,1)S(1)}, bf16[18,32,256]{2,1,0:T(8,128)(2,1)S(1)}, u32[]{:S(2)}, u32[]{:S(2)}) %collective-permute-start) | collective-permute-done | bytes 294944 | tf_op jit(solution)/shard_map/ppermute | solution.py:408
  28.8 0.1 collective-permute-start.2
  28.9 6.0 %shard_map.73.refs_0_.refs_1_ = bf16[18,32,256]{2,1,0:T(8,128)(2,1)S(1)} custom-call(s32[2,4]{1,0:T(2,128)S(1)} %copy-done.1, bf16[2048,1024]{1,0:T(8,128)(2,1)S(1)} %get-tuple-element.12.xs, bf16[1024,512]{1,0:T(8,128)(2,1)S(1)} %get-tuple-element.13.wr, bf16[512,2048]{1,0:T(8,128)(2,1)S(1)} %get-tuple-element.14.we, ...), custom_call_target="tpu_custom_call" | custom-call | flops 4831838208 | bytes 1048576 | tf_op jit(solution)/shard_map/pallas_call | solution.py:398
  34.9 0.0 copy-start
  34.9 5.0 %shard_map.75.refs_3_ = bf16[18,32,256]{2,1,0:T(8,128)(2,1)S(1)} custom-call(s32[2,4]{1,0:T(2,128)S(1)} %copy-done.1, bf16[2048,1024]{1,0:T(8,128)(2,1)S(1)} %get-tuple-element.12.xs, bf16[1024,512]{1,0:T(8,128)(2,1)S(1)} %get-tuple-element.13.wr, bf16[512,2048]{1,0:T(8,128)(2,1)S(1)} %get-tuple-element.14.we, bf16[1024,2048]{1,0:T(8,128)(2,1)S(1)} %get-tuple-element.15.ws, ...), custom_call_target="tpu_custom_call" | custom-call | flops 3758096384 | bytes 1048576 | tf_op jit(solution)/shard_map/pallas_call | solution.py:398
  39.9 0.1 collective-permute-start.4
  40.0 2.2 %collective-permute-start.3 = (bf16[18,32,256]{2,1,0:T(8,128)(2,1)S(1)}, bf16[18,32,256]{2,1,0:T(8,128)(2,1)S(1)}, u32[]{:S(2)}, u32[]{:S(2)}) collective-permute-start(bf16[18,32,256]{2,1,0:T(8,128)(2,1)S(1)} %shard_map.73.refs_0_.refs_1_), channel_id=1, source_target_pairs={{0,2},{1,3},{2,0},{3,1},{4,6},{5,7},{6,4},{7,5},{8,10},{9,11},{10,... | collective-permute-start | bytes 884744 | tf_op jit(solution)/shard_map/ppermute | solution.py:408
  42.2 0.0 collective-permute-done.2.refs_6_
  42.2 0.0 copy-done
  42.2 3.0 %conv_early.1.partial = f32[32,64,256]{2,1,0:T(8,128)S(1)} custom-call(bf16[2304,256]{1,0:T(8,128)(2,1)S(1)} %bitcast.1, bf16[18,32,256]{2,1,0:T(8,128)(2,1)S(1)} %get-tuple-element.11.refs_0_, bf16[18,32,256]{2,1,0:T(8,128)(2,1)S(1)} %shard_map.73.refs_0_.refs_1_, bf16[18,32,256]{2,1,0:T(8,128)(2,1)S(1)} %shard_map.74.refs_1_.refs_2_, ...), custom_call_target="tpu_custom_call" | custom-call | flops 2415919104 | bytes 4194304 | tf_op jit(solution)/shard_map/conv_early/pallas_call | solution.py:434
  45.2 5.1 %collective-permute-done.4.refs_1_ = bf16[18,32,256]{2,1,0:T(8,128)(2,1)S(1)} collective-permute-done((bf16[18,32,256]{2,1,0:T(8,128)(2,1)S(1)}, bf16[18,32,256]{2,1,0:T(8,128)(2,1)S(1)}, u32[]{:S(2)}, u32[]{:S(2)}) %collective-permute-start.4) | collective-permute-done | bytes 294944 | tf_op jit(solution)/shard_map/ppermute | solution.py:408
  50.4 5.4 %collective-permute-done.3.refs_0_ = bf16[18,32,256]{2,1,0:T(8,128)(2,1)S(1)} collective-permute-done((bf16[18,32,256]{2,1,0:T(8,128)(2,1)S(1)}, bf16[18,32,256]{2,1,0:T(8,128)(2,1)S(1)}, u32[]{:S(2)}, u32[]{:S(2)}) %collective-permute-start.3) | collective-permute-done | bytes 294944 | tf_op jit(solution)/shard_map/ppermute | solution.py:408
  55.8 2.4 %conv_late.1 = bf16[32,64,256]{2,1,0:T(8,128)(2,1)} custom-call(bf16[2304,256]{1,0:T(8,128)(2,1)S(1)} %bitcast.2, f32[32,64,256]{2,1,0:T(8,128)S(1)} %conv_early.1.partial, bf16[18,32,256]{2,1,0:T(8,128)(2,1)S(1)} %collective-permute-done.3.refs_0_, bf16[18,32,256]{2,1,0:T(8,128)(2,1)S(1)} %collective-permute-done.4.refs_1_), custom_call_target="tpu_custom_call" | custom-call | flops 452984832 | bytes 4194304 | tf_op jit(solution)/shard_map/conv_late/pallas_call | solution.py:448
  (1 shorter events, 0.0 us)
Async XLA Ops:
  0.0 8.0 %copy-start.1 = (s32[2,4]{1,0:T(2,128)S(1)}, s32[2,4]{1,0:T(2,128)}, u32[]{:S(2)}) copy-start(s32[2,4]{1,0:T(2,128)} %flags.5) | copy-start | bytes 100
  12.8 9.8 %collective-permute-start.1 = (bf16[18,32,256]{2,1,0:T(8,128)(2,1)S(1)}, bf16[18,32,256]{2,1,0:T(8,128)(2,1)S(1)}, u32[]{:S(2)}, u32[]{:S(2)}) collective-permute-start(bf16[18,32,256]{2,1,0:T(8,128)(2,1)S(1)} %shard_map.74.refs_1_.refs_2_), channel_id=1, source_target_pairs={{0,1},{1,0},{2,4},{3,5},{4,2},{5,3},{6,8},{7,9},{8,6},{9,7},{10,12... | collective-permute-start | bytes 884744 | tf_op jit(solution)/shard_map/ppermute | solution.py:408
  12.9 15.9 %collective-permute-start = (bf16[18,32,256]{2,1,0:T(8,128)(2,1)S(1)}, bf16[18,32,256]{2,1,0:T(8,128)(2,1)S(1)}, u32[]{:S(2)}, u32[]{:S(2)}) collective-permute-start(bf16[18,32,256]{2,1,0:T(8,128)(2,1)S(1)} %get-tuple-element.11.refs_0_), channel_id=1, source_target_pairs={{0,2},{1,3},{2,0},{3,1},{4,6},{5,7},{6,4},{7,5},{8,10},{9,11},{10,... | collective-permute-start | bytes 884744 | tf_op jit(solution)/shard_map/ppermute | solution.py:408
  28.8 13.4 %collective-permute-start.2 = (bf16[72,16,256]{2,1,0:T(8,128)(2,1)S(1)}, bf16[72,16,256]{2,1,0:T(8,128)(2,1)S(1)}, u32[]{:S(2)}, u32[]{:S(2)}) collective-permute-start(bf16[72,16,256]{2,1,0:T(8,128)(2,1)S(1)} %pick.1), channel_id=1, source_target_pairs={{0,1},{1,0},{2,3},{3,2},{4,5},{5,4},{6,7},{7,6},{8,9},{9,8},{10,11... | collective-permute-start | bytes 1769480 | tf_op jit(solution)/shard_map/ppermute | solution.py:422
  34.9 7.3 %copy-start = (bf16[9,256,256]{2,1,0:T(8,128)(2,1)S(1)}, bf16[9,256,256]{2,1,0:T(8,128)(2,1)}, u32[]{:S(2)}) copy-start(bf16[9,256,256]{2,1,0:T(8,128)(2,1)} %param.13) | copy-start | bytes 3538948
  39.9 10.5 %collective-permute-start.4 = (bf16[18,32,256]{2,1,0:T(8,128)(2,1)S(1)}, bf16[18,32,256]{2,1,0:T(8,128)(2,1)S(1)}, u32[]{:S(2)}, u32[]{:S(2)}) collective-permute-start(bf16[18,32,256]{2,1,0:T(8,128)(2,1)S(1)} %shard_map.75.refs_3_), channel_id=1, source_target_pairs={{0,1},{1,0},{2,4},{3,5},{4,2},{5,3},{6,8},{7,9},{8,6},{9,7},{10,12... | collective-permute-start | bytes 884744 | tf_op jit(solution)/shard_map/ppermute | solution.py:408
  40.0 15.8 %collective-permute-start.3 = (bf16[18,32,256]{2,1,0:T(8,128)(2,1)S(1)}, bf16[18,32,256]{2,1,0:T(8,128)(2,1)S(1)}, u32[]{:S(2)}, u32[]{:S(2)}) collective-permute-start(bf16[18,32,256]{2,1,0:T(8,128)(2,1)S(1)} %shard_map.73.refs_0_.refs_1_), channel_id=1, source_target_pairs={{0,2},{1,3},{2,0},{3,1},{4,6},{5,7},{6,4},{7,5},{8,10},{9,11},{10,... | collective-permute-start | bytes 884744 | tf_op jit(solution)/shard_map/ppermute | solution.py:408

commit v7 on v6

--- a/solution.py
+++ b/solution.py
@@ -14,6 +14,7 @@
 BLOCK = 512
 DEPTH = 3
 WAITS = (1, 3)
+LATE = 2
 F32 = jnp.float32
 BF16 = jnp.bfloat16
 VM = pl.BlockSpec(memory_space=pltpu.VMEM)
@@ -241,30 +242,28 @@
 
 def conv_early(groups, rows_n, cols_n, height, w, *refs):
     g = len(groups)
-    ones, twos = refs[:g], refs[g : 2 * g]
-    near, far = refs[2 * g : 2 * g + 2]
-    sides = refs[2 * g + 2 : -3]
-    partial, ext, cat = refs[-3:]
+    ones, twos, far = refs[:g], refs[g : 2 * g], refs[2 * g : 3 * g]
+    near = refs[3 * g]
+    sides = refs[3 * g + 1 : -6]
+    out, partial, ext, cat, done, sem = refs[-6:]
     width = cat.shape[1]
     rest = height - RR
     top = near_is_top()
+    near_row = (1 - top) * (RR + height)
     for i, (cols, near_first) in enumerate(groups):
         up = top_of(near_first)
         skip = up * (RR - rest)
         rows = [(0, ones[i], 0, RR, RR + (1 - up) * rest, None), (1, twos[i], skip, rest, RR + up * RR, None)]
+        rows += [(3, far[i], 0, RR, top * (RR + height), far_inside(rows_n))]
         if i == 0:
-            rows += [(2, near, 0, RR, (1 - top) * (RR + height), None)]
-            rows += [(3, far, 0, RR, top * (RR + height), far_inside(rows_n))]
+            rows += [(2, near, 0, RR, near_row, None)]
         for part, src, first, count, row, on in rows:
             place(cols, src, first, count, ext, row, on)
             if i == 0:
                 place_sides(cols_n, sides, part, first, count, ext, row, on)
     for cols, _ in groups[1:]:
         for col in cols:
-            at = (1 + col) * TILE
-            zero = jnp.zeros((RR, TILE, ext.shape[2]), BF16)
-            ext[0:RR, at : at + TILE, :] = zero
-            ext[RR + height :, at : at + TILE, :] = zero
+            ext[pl.ds(near_row, RR), (1 + col) * TILE : (2 + col) * TILE, :] = jnp.zeros((RR, TILE, ext.shape[2]), BF16)
     spread(ext, cat, width)
     k = cat.shape[2]
     for at, count in blocks_of(height):
@@ -274,6 +273,11 @@
             term = jnp.dot(taps, w[a * k : (a + 1) * k, :], preferred_element_type=F32)
             total = term if total is None else total + term
         partial[at : at + count] = total.reshape(count, width, total.shape[1])
+    rows = pl.ds(top * RR, rest)
+    done[...] = jnp.maximum(partial[rows], 0).astype(BF16)
+    copy = pltpu.make_async_copy(done, out.at[rows], sem)
+    copy.start()
+    copy.wait()
 
 
 def far_inside(rows_n):
@@ -281,46 +285,43 @@
     return (me > 0) & (me < rows_n - 1)
 
 
-def conv_late(groups, rows_n, height, w, partial, *refs):
-    g = len(groups) - 1
-    near, far = refs[:g], refs[g : 2 * g]
-    out, apart, done, sems = refs[-4:]
+def conv_late(groups, height, w, partial, *refs):
+    near = refs[: len(groups) - 1]
+    _, out, apart, done, sems = refs[-5:]
     top = near_is_top()
     width, br = partial.shape[1:]
+    rest = height - RR
     used = sorted(col for cols, _ in groups[1:] for col in cols)
     lo, hi = used[0] * TILE, (used[-1] + 1) * TILE
-    zero = jnp.zeros((2 * RR, TILE, br), F32)
-    for b in range(3):
-        apart[b, :, 0:TILE, :] = zero
-        apart[b, :, TILE + hi - lo : 2 * TILE + hi - lo, :] = zero
-    for halo, row, a, on in ((near, (1 - top) * RR, (1 - top) * 2, None), (far, top * RR, top * 2, far_inside(rows_n))):
-        for i, (cols, _) in enumerate(groups[1:]):
-            there = halo[i][...]
-            if on is not None:
-                there = jnp.where(on, there, jnp.zeros_like(there))
-            there = there.reshape(RR * len(cols) * TILE, br)
-            for b in range(3):
-                tap = w[pl.ds(pl.multiple_of((3 * a + b) * br, br), br), :]
-                term = jnp.dot(there, tap, preferred_element_type=F32).reshape(RR, len(cols) * TILE, br)
-                for j, col in enumerate(cols):
-                    at = (1 + col) * TILE - lo
-                    apart[b, pl.ds(row, RR), at : at + TILE, :] = term[:, j * TILE : (j + 1) * TILE, :]
     reach = []
     for b in range(3):
         shift = (b - 1) * RC
         reach.append((max(0, lo - shift) // TILE * TILE, min(width, -(-(hi - shift) // TILE) * TILE)))
     cuts = sorted({0, width, *[edge for span_b in reach for edge in span_b]})
+    zero = jnp.zeros((RR, TILE, br), F32)
+    for b in range(3):
+        apart[b, :, 0:TILE, :] = zero
+        apart[b, :, TILE + hi - lo : 2 * TILE + hi - lo, :] = zero
+    for i, (cols, _) in enumerate(groups[1:]):
+        there = near[i][...].reshape(RR * len(cols) * TILE, br)
+        for b in range(3):
+            tap = w[pl.ds(pl.multiple_of((6 * (1 - top) + b) * br, br), br), :]
+            term = jnp.dot(there, tap, preferred_element_type=F32).reshape(RR, len(cols) * TILE, br)
+            for j, col in enumerate(cols):
+                at = (1 + col) * TILE - lo
+                apart[b, :, at : at + TILE, :] = term[:, j * TILE : (j + 1) * TILE, :]
     copies = []
-    for n, (at, count) in enumerate(blocks_of(height)):
+    step = RR // LATE
+    for at in range(0, RR, step):
+        rows = pl.ds((1 - top) * rest + at, step)
         for left, right in zip(cuts, cuts[1:]):
-            total = partial[at : at + count, left:right, :]
-            for row in (at if at < RR else -1, at - height + 2 * RR if at >= height - RR else -1):
-                for b in range(3):
-                    if row >= 0 and reach[b][0] <= left and right <= reach[b][1]:
-                        first = left + (b - 1) * RC + TILE - lo
-                        total = total + apart[b, row : row + count, first : first + right - left, :]
-            done[at : at + count, left:right, :] = jnp.maximum(total, 0).astype(BF16)
-        copies.append(pltpu.make_async_copy(done.at[pl.ds(at, count)], out.at[pl.ds(at, count)], sems.at[n]))
+            total = partial[rows, left:right, :]
+            for b in range(3):
+                if reach[b][0] <= left and right <= reach[b][1]:
+                    first = left + (b - 1) * RC + TILE - lo
+                    total = total + apart[b, at : at + step, first : first + right - left, :]
+            done[at : at + step, left:right, :] = jnp.maximum(total, 0).astype(BF16)
+        copies.append(pltpu.make_async_copy(done.at[pl.ds(at, step)], out.at[rows], sems.at[len(copies)]))
         copies[-1].start()
     for copy in copies:
         copy.wait()
@@ -333,7 +334,7 @@
 
 
 def plan(tile_cols):
-    groups = [([0, tile_cols - 1], True), (list(range(1, tile_cols - 1)), True)]
+    groups = [([0, tile_cols - 1], True), (list(range(1, tile_cols - 1)), False)]
     order = [(0, True), (0, False), (1, True), (1, False)]
     return groups, order
 
@@ -427,38 +428,44 @@
         ]
 
     taps = w_dilated.reshape(9 * br, br)
+    rest = height - RR
     n_groups = len(groups)
     pick = lambda table, key: [table[i, key] for i in range(n_groups)]
     flops = 2 * width * 3 * br * br
-    edge_halos = [halo[0, True], halo[0, False]]
-    partial = pl.pallas_call(
+    out, partial = pl.pallas_call(
         functools.partial(conv_early, groups, rows_n, cols_n, height),
-        out_shape=jax.ShapeDtypeStruct((height, width, br), F32),
-        in_specs=[VM] * (3 + 2 * n_groups + len(sides)),
-        out_specs=VM,
+        out_shape=[
+            jax.ShapeDtypeStruct((height, width, br), BF16),
+            jax.ShapeDtypeStruct((height, width, br), F32),
+        ],
+        in_specs=[VM] * (2 + 3 * n_groups + len(sides)),
+        out_specs=[HBM, VM],
         scratch_shapes=[
             pltpu.VMEM((height + 2 * RR, width + 2 * TILE, br), BF16),
             pltpu.VMEM((height + 2 * RR, width, 3 * br), BF16),
+            pltpu.VMEM((rest, width, br), BF16),
+            pltpu.SemaphoreType.DMA,
         ],
         compiler_params=params(CONV_MIB),
         cost_estimate=cost(flops * 3 * height, 4 * MIB),
         name="conv_early",
-    )(taps, *pick(local, True), *pick(local, False), *edge_halos, *sides)
+    )(taps, *pick(local, True), *pick(local, False), *pick(halo, False), halo[0, True], *sides)
     inner = sum(len(cols) for cols, _ in groups[1:]) * TILE
     return pl.pallas_call(
-        functools.partial(conv_late, groups, rows_n, height),
+        functools.partial(conv_late, groups, height),
         out_shape=jax.ShapeDtypeStruct((height, width, br), BF16),
-        in_specs=[VM] * (2 * n_groups),
+        in_specs=[VM] * (1 + n_groups) + [HBM],
         out_specs=HBM,
+        input_output_aliases={1 + n_groups: 0},
         scratch_shapes=[
-            pltpu.VMEM((3, 2 * RR, inner + 2 * TILE, br), F32),
-            pltpu.VMEM((height, width, br), BF16),
-            pltpu.SemaphoreType.DMA((len(blocks_of(height)),)),
+            pltpu.VMEM((3, RR, inner + 2 * TILE, br), F32),
+            pltpu.VMEM((RR, width, br), BF16),
+            pltpu.SemaphoreType.DMA((LATE,)),
         ],
         compiler_params=params(CONV_MIB),
         cost_estimate=cost(flops * RR, 4 * MIB),
         name="conv_late",
-    )(taps, partial, *pick(halo, True)[1:], *pick(halo, False)[1:])
+    )(taps, partial, *pick(halo, True)[1:], out)
 
 
 def solution(mesh):

time: 58.5 us -> 53.4 us (0.913)
  the two profiles are of different devices: /device:TPU:18 before, /device:TPU:11 now
where the time goes in v7:
time: 53.4 us; the launch traced here: 53.2 us
  Pallas kernels  27.4 us (51%)
  waiting for transfers between devices  22.1 us (41%)
  starting transfers between devices  3.46 us (6%)
    ppermute x4, waiting for transfers between devices, shards(): halo[i, near] = lax.ppermute(value, ('row', 'col'), swap(near))  22.1 us
    pallas_call x3, Pallas kernels, shards(): pl.pallas_call(functools.partial(later_chunk, chunks[n], starts[n], heigh...  13.8 us
    pallas_call x1, Pallas kernels, shards(): pl.pallas_call(functools.partial(first_chunk, chunks, height), out_shape=...  7.99 us
    pallas_call x1, Pallas kernels, shards(): pl.pallas_call(functools.partial(conv_early, groups, rows_n, cols_n, heig...  4.28 us
    ppermute x4, starting transfers between devices, shards(): halo[i, near] = lax.ppermute(value, ('row', 'col'), swap(near))  2.9 us
    pallas_call x1, Pallas kernels, shards(): pl.pallas_call(functools.partial(conv_late, groups, height), out_shape=ja...  1.23 us
  transfers between devices with their start and end apart: 5, of which 4 were waited for; matrix products, arithmetic and copies ran while one was open for 0% of the time, Pallas kernels for 25%

profile of v7, /device:TPU:11, one launch (start us, length us, event | category | flops | bytes accessed | tf_op | source)
XLA Modules:
  0.0 53.2 jit_solution(12341792612530450645)
XLA Ops:
  0.0 0.0 copy-start.1
  0.0 8.0 %trunk_first.1 = (bf16[18,32,256]{2,1,0:T(8,128)(2,1)S(1)}, bf16[2048,1024]{1,0:T(8,128)(2,1)S(1)}, bf16[1024,512]{1,0:T(8,128)(2,1)S(1)}, bf16[512,2048]{1,0:T(...) custom-call(s32[2,4]{1,0:T(2,128)} %flags.5, bf16[2,4,256,1024]{3,2,1,0:T(8,128)(2,1)} %feats.1, ...), custom_call_target="tpu_custom_call" | custom-call | flops 4831838208 | bytes 12582912 | tf_op jit(solution)/shard_map/trunk_first/pallas_call | solution.py:357
  8.0 0.0 copy-done.1
  8.0 4.8 %shard_map.74.refs_1_.refs_2_ = bf16[18,32,256]{2,1,0:T(8,128)(2,1)S(1)} custom-call(s32[2,4]{1,0:T(2,128)S(1)} %copy-done.1, bf16[2048,1024]{1,0:T(8,128)(2,1)S(1)} %get-tuple-element.14.xs, bf16[1024,512]{1,0:T(8,128)(2,1)S(1)} %get-tuple-element.15.wr, bf16[512,2048]{1,0:T(8,128)(2,1)S(1)} %get-tuple-element.16.we, ...), custom_call_target="tpu_custom_call" | custom-call | flops 3758096384 | bytes 1048576 | tf_op jit(solution)/shard_map/pallas_call | solution.py:399
  12.8 0.1 collective-permute-start
  12.8 2.5 %collective-permute-start.2 = (bf16[18,32,256]{2,1,0:T(8,128)(2,1)S(1)}, bf16[18,32,256]{2,1,0:T(8,128)(2,1)S(1)}, u32[]{:S(2)}, u32[]{:S(2)}) collective-permute-start(bf16[18,32,256]{2,1,0:T(8,128)(2,1)S(1)} %get-tuple-element.13.refs_0_), channel_id=1, source_target_pairs={{0,2},{1,3},{2,0},{3,1},{4,6},{5,7},{6,4},{7,5},{8,10},{9,11},{10,... | collective-permute-start | bytes 884744 | tf_op jit(solution)/shard_map/ppermute | solution.py:409
  15.3 6.3 %collective-permute-done.refs_3_.refs_4_ = bf16[18,32,256]{2,1,0:T(8,128)(2,1)S(1)} collective-permute-done((bf16[18,32,256]{2,1,0:T(8,128)(2,1)S(1)}, bf16[18,32,256]{2,1,0:T(8,128)(2,1)S(1)}, u32[]{:S(2)}, u32[]{:S(2)}) %collective-permute-start) | collective-permute-done | bytes 294944 | tf_op jit(solution)/shard_map/ppermute | solution.py:409
  21.7 7.3 %collective-permute-done.2.refs_2_.refs_6_ = bf16[18,32,256]{2,1,0:T(8,128)(2,1)S(1)} collective-permute-done((bf16[18,32,256]{2,1,0:T(8,128)(2,1)S(1)}, bf16[18,32,256]{2,1,0:T(8,128)(2,1)S(1)}, u32[]{:S(2)}, u32[]{:S(2)}) %collective-permute-start.2) | collective-permute-done | bytes 294944 | tf_op jit(solution)/shard_map/ppermute | solution.py:409
  29.0 0.6 %collective-permute-start.3 = (bf16[72,16,256]{2,1,0:T(8,128)(2,1)S(1)}, bf16[72,16,256]{2,1,0:T(8,128)(2,1)S(1)}, u32[]{:S(2)}, u32[]{:S(2)}) collective-permute-start(bf16[72,16,256]{2,1,0:T(8,128)(2,1)S(1)} %pick.1), channel_id=1, source_target_pairs={{0,1},{1,0},{2,3},{3,2},{4,5},{5,4},{6,7},{7,6},{8,9},{9,8},{10,11... | collective-permute-start | bytes 1769480 | tf_op jit(solution)/shard_map/ppermute | solution.py:423
  29.6 6.0 %shard_map.73.refs_0_.refs_1_ = bf16[18,32,256]{2,1,0:T(8,128)(2,1)S(1)} custom-call(s32[2,4]{1,0:T(2,128)S(1)} %copy-done.1, bf16[2048,1024]{1,0:T(8,128)(2,1)S(1)} %get-tuple-element.14.xs, bf16[1024,512]{1,0:T(8,128)(2,1)S(1)} %get-tuple-element.15.wr, bf16[512,2048]{1,0:T(8,128)(2,1)S(1)} %get-tuple-element.16.we, ...), custom_call_target="tpu_custom_call" | custom-call | flops 4831838208 | bytes 1048576 | tf_op jit(solution)/shard_map/pallas_call | solution.py:399
  35.6 0.0 copy-start
  35.6 0.1 collective-permute-start.1
  35.7 3.1 %shard_map.75.refs_3_ = bf16[18,32,256]{2,1,0:T(8,128)(2,1)S(1)} custom-call(s32[2,4]{1,0:T(2,128)S(1)} %copy-done.1, bf16[2048,1024]{1,0:T(8,128)(2,1)S(1)} %get-tuple-element.14.xs, bf16[1024,512]{1,0:T(8,128)(2,1)S(1)} %get-tuple-element.15.wr, bf16[512,2048]{1,0:T(8,128)(2,1)S(1)} %get-tuple-element.16.we, bf16[1024,2048]{1,0:T(8,128)(2,1)S(1)} %get-tuple-element.17.ws, ...), custom_call_target="tpu_custom_call" | custom-call | flops 3758096384 | bytes 1048576 | tf_op jit(solution)/shard_map/pallas_call | solution.py:399
  38.8 0.3 collective-permute-start.4
  39.1 6.1 %collective-permute-done.1.refs_5_ = bf16[18,32,256]{2,1,0:T(8,128)(2,1)S(1)} collective-permute-done((bf16[18,32,256]{2,1,0:T(8,128)(2,1)S(1)}, bf16[18,32,256]{2,1,0:T(8,128)(2,1)S(1)}, u32[]{:S(2)}, u32[]{:S(2)}) %collective-permute-start.1) | collective-permute-done | bytes 294944 | tf_op jit(solution)/shard_map/ppermute | solution.py:409
  45.2 0.0 collective-permute-done.3.refs_7_
  45.2 0.0 copy-done
  45.2 4.3 %conv_early.1 = (bf16[32,64,256]{2,1,0:T(8,128)(2,1)}, f32[32,64,256]{2,1,0:T(8,128)S(1)}) custom-call(bf16[2304,256]{1,0:T(8,128)(2,1)S(1)} %bitcast.1, bf16[18,32,256]{2,1,0:T(8,128)(2,1)S(1)} %get-tuple-element.13.refs_0_, bf16[18,32,256]{2,1,0:T(8,128)(2,1)S(1)} %shard_map.73.refs_0_.refs_1_, bf16[18,32,256]{2,1,0:T(8,128)(2,1)S(1)} %shard_map.74.refs_1_.refs_2_, ...), custom_call_target="tpu_custom_call" | custom-call | flops 2415919104 | bytes 4194304 | tf_op jit(solution)/shard_map/conv_early/pallas_call | solution.py:435
  49.5 2.4 %collective-permute-done.4.refs_0_ = bf16[18,32,256]{2,1,0:T(8,128)(2,1)S(1)} collective-permute-done((bf16[18,32,256]{2,1,0:T(8,128)(2,1)S(1)}, bf16[18,32,256]{2,1,0:T(8,128)(2,1)S(1)}, u32[]{:S(2)}, u32[]{:S(2)}) %collective-permute-start.4) | collective-permute-done | bytes 294944 | tf_op jit(solution)/shard_map/ppermute | solution.py:409
  51.8 1.2 %conv_late.1 = bf16[32,64,256]{2,1,0:T(8,128)(2,1)} custom-call(bf16[2304,256]{1,0:T(8,128)(2,1)S(1)} %bitcast.2, f32[32,64,256]{2,1,0:T(8,128)S(1)} %get-tuple-element.19.partial, bf16[18,32,256]{2,1,0:T(8,128)(2,1)S(1)} %collective-permute-done.4.refs_0_, bf16[32,64,256]{2,1,0:T(8,128)(2,1)} %get-tuple-element.20.refs_1_), custom_call_target="tpu_custom_call", output_to_operand_aliasing={{}: (3, {})} | custom-call | flops 452984832 | bytes 4194304 | tf_op jit(solution)/shard_map/conv_late/pallas_call | solution.py:454
  (1 shorter events, 0.0 us)
Async XLA Ops:
  0.0 8.0 %copy-start.1 = (s32[2,4]{1,0:T(2,128)S(1)}, s32[2,4]{1,0:T(2,128)}, u32[]{:S(2)}) copy-start(s32[2,4]{1,0:T(2,128)} %flags.5) | copy-start | bytes 100
  12.8 8.9 %collective-permute-start = (bf16[18,32,256]{2,1,0:T(8,128)(2,1)S(1)}, bf16[18,32,256]{2,1,0:T(8,128)(2,1)S(1)}, u32[]{:S(2)}, u32[]{:S(2)}) collective-permute-start(bf16[18,32,256]{2,1,0:T(8,128)(2,1)S(1)} %shard_map.74.refs_1_.refs_2_), channel_id=1, source_target_pairs={{0,1},{1,0},{2,4},{3,5},{4,2},{5,3},{6,8},{7,9},{8,6},{9,7},{10,12... | collective-permute-start | bytes 884744 | tf_op jit(solution)/shard_map/ppermute | solution.py:409
  12.8 16.1 %collective-permute-start.2 = (bf16[18,32,256]{2,1,0:T(8,128)(2,1)S(1)}, bf16[18,32,256]{2,1,0:T(8,128)(2,1)S(1)}, u32[]{:S(2)}, u32[]{:S(2)}) collective-permute-start(bf16[18,32,256]{2,1,0:T(8,128)(2,1)S(1)} %get-tuple-element.13.refs_0_), channel_id=1, source_target_pairs={{0,2},{1,3},{2,0},{3,1},{4,6},{5,7},{6,4},{7,5},{8,10},{9,11},{10,... | collective-permute-start | bytes 884744 | tf_op jit(solution)/shard_map/ppermute | solution.py:409
  29.0 16.1 %collective-permute-start.3 = (bf16[72,16,256]{2,1,0:T(8,128)(2,1)S(1)}, bf16[72,16,256]{2,1,0:T(8,128)(2,1)S(1)}, u32[]{:S(2)}, u32[]{:S(2)}) collective-permute-start(bf16[72,16,256]{2,1,0:T(8,128)(2,1)S(1)} %pick.1), channel_id=1, source_target_pairs={{0,1},{1,0},{2,3},{3,2},{4,5},{5,4},{6,7},{7,6},{8,9},{9,8},{10,11... | collective-permute-start | bytes 1769480 | tf_op jit(solution)/shard_map/ppermute | solution.py:423
  35.6 9.6 %copy-start = (bf16[9,256,256]{2,1,0:T(8,128)(2,1)S(1)}, bf16[9,256,256]{2,1,0:T(8,128)(2,1)}, u32[]{:S(2)}) copy-start(bf16[9,256,256]{2,1,0:T(8,128)(2,1)} %param.13) | copy-start | bytes 3538948
  35.6 9.6 %collective-permute-start.1 = (bf16[18,32,256]{2,1,0:T(8,128)(2,1)S(1)}, bf16[18,32,256]{2,1,0:T(8,128)(2,1)S(1)}, u32[]{:S(2)}, u32[]{:S(2)}) collective-permute-start(bf16[18,32,256]{2,1,0:T(8,128)(2,1)S(1)} %shard_map.73.refs_0_.refs_1_), channel_id=1, source_target_pairs={{0,1},{1,0},{2,4},{3,5},{4,2},{5,3},{6,8},{7,9},{8,6},{9,7},{10,12... | collective-permute-start | bytes 884744 | tf_op jit(solution)/shard_map/ppermute | solution.py:409
  38.8 13.1 %collective-permute-start.4 = (bf16[18,32,256]{2,1,0:T(8,128)(2,1)S(1)}, bf16[18,32,256]{2,1,0:T(8,128)(2,1)S(1)}, u32[]{:S(2)}, u32[]{:S(2)}) collective-permute-start(bf16[18,32,256]{2,1,0:T(8,128)(2,1)S(1)} %shard_map.75.refs_3_), channel_id=1, source_target_pairs={{0,2},{1,3},{2,0},{3,1},{4,6},{5,7},{6,4},{7,5},{8,10},{9,11},{10,... | collective-permute-start | bytes 884744 | tf_op jit(solution)/shard_map/ppermute | solution.py:409

commit v8 on v7

--- a/solution.py
+++ b/solution.py
@@ -202,11 +202,10 @@
         out[pl.ds((1 - top) * (RR - shared), shared)] = near[pl.ds(top * (RR - shared), shared)]
 
 
-def pick_kernel(cols_n, *refs):
-    n = 1 if cols_n == 2 else 2
-    ins, outs = refs[:-n], refs[-n:]
-    width = ins[0].shape[1]
-    for i, src in enumerate(ins):
+def pick_kernel(cols_n, used, *refs):
+    outs = refs[-(1 if cols_n == 2 else 2) :]
+    width = refs[0].shape[1]
+    for i, src in enumerate(refs[:used]):
         rows = pl.ds(i * RR, RR)
         if cols_n == 2:
             first = pl.multiple_of((1 - lax.axis_index("col")) * (width - TILE), TILE)
@@ -243,40 +242,39 @@
 def conv_early(groups, rows_n, cols_n, height, w, *refs):
     g = len(groups)
     ones, twos, far = refs[:g], refs[g : 2 * g], refs[2 * g : 3 * g]
-    near = refs[3 * g]
-    sides = refs[3 * g + 1 : -6]
+    sides = refs[3 * g : -6]
     out, partial, ext, cat, done, sem = refs[-6:]
     width = cat.shape[1]
+    br = ext.shape[2]
     rest = height - RR
-    top = near_is_top()
-    near_row = (1 - top) * (RR + height)
+    far_top = 1 - near_is_top()
+    local = far_top * RR
     for i, (cols, near_first) in enumerate(groups):
         up = top_of(near_first)
         skip = up * (RR - rest)
-        rows = [(0, ones[i], 0, RR, RR + (1 - up) * rest, None), (1, twos[i], skip, rest, RR + up * RR, None)]
-        rows += [(3, far[i], 0, RR, top * (RR + height), far_inside(rows_n))]
-        if i == 0:
-            rows += [(2, near, 0, RR, near_row, None)]
+        rows = [(0, ones[i], 0, RR, local + (1 - up) * rest, None), (1, twos[i], skip, rest, local + up * RR, None)]
+        rows += [(2, far[i], 0, RR, (1 - far_top) * height, far_inside(rows_n))]
         for part, src, first, count, row, on in rows:
             place(cols, src, first, count, ext, row, on)
             if i == 0:
                 place_sides(cols_n, sides, part, first, count, ext, row, on)
-    for cols, _ in groups[1:]:
-        for col in cols:
-            ext[pl.ds(near_row, RR), (1 + col) * TILE : (2 + col) * TILE, :] = jnp.zeros((RR, TILE, ext.shape[2]), BF16)
     spread(ext, cat, width)
     k = cat.shape[2]
-    for at, count in blocks_of(height):
-        total = None
-        for a in range(3):
-            taps = cat[at + a * RR : at + a * RR + count].reshape(count * width, k)
-            term = jnp.dot(taps, w[a * k : (a + 1) * k, :], preferred_element_type=F32)
-            total = term if total is None else total + term
-        partial[at : at + count] = total.reshape(count, width, total.shape[1])
-    rows = pl.ds(top * RR, rest)
-    done[...] = jnp.maximum(partial[rows], 0).astype(BF16)
-    copy = pltpu.make_async_copy(done, out.at[rows], sem)
+    total = None
+    for a in range(3):
+        taps = cat[a * RR : a * RR + rest].reshape(rest * width, k)
+        term = jnp.dot(taps, w[a * k : (a + 1) * k, :], preferred_element_type=F32)
+        total = term if total is None else total + term
+    done[...] = jnp.maximum(total, 0).astype(BF16).reshape(rest, width, br)
+    copy = pltpu.make_async_copy(done, out.at[pl.ds((1 - far_top) * RR, rest)], sem)
     copy.start()
+    centre = cat[pl.ds(far_top * height, RR)].reshape(RR * width, k)
+    inner = cat[pl.ds(far_top * rest + (1 - far_top) * RR, RR)].reshape(RR * width, k)
+    inner_w = w[pl.ds(pl.multiple_of((1 - far_top) * 2 * k, k), k), :]
+    total = jnp.dot(centre, w[k : 2 * k, :], preferred_element_type=F32) + jnp.dot(
+        inner, inner_w, preferred_element_type=F32
+    )
+    partial[...] = total.reshape(RR, width, br)
     copy.wait()
 
 
@@ -285,56 +283,46 @@
     return (me > 0) & (me < rows_n - 1)
 
 
-def conv_late(groups, height, w, partial, *refs):
-    near = refs[: len(groups) - 1]
+def conv_late(groups, cols_n, height, w, partial, *refs):
+    near = refs[: len(groups)]
+    sides = refs[len(groups) : -5]
     _, out, apart, done, sems = refs[-5:]
     top = near_is_top()
     width, br = partial.shape[1:]
     rest = height - RR
-    used = sorted(col for cols, _ in groups[1:] for col in cols)
-    lo, hi = used[0] * TILE, (used[-1] + 1) * TILE
-    reach = []
-    for b in range(3):
-        shift = (b - 1) * RC
-        reach.append((max(0, lo - shift) // TILE * TILE, min(width, -(-(hi - shift) // TILE) * TILE)))
-    cuts = sorted({0, width, *[edge for span_b in reach for edge in span_b]})
-    zero = jnp.zeros((RR, TILE, br), F32)
-    for b in range(3):
-        apart[b, :, 0:TILE, :] = zero
-        apart[b, :, TILE + hi - lo : 2 * TILE + hi - lo, :] = zero
-    for i, (cols, _) in enumerate(groups[1:]):
-        there = near[i][...].reshape(RR * len(cols) * TILE, br)
+
+    def product(value, b):
+        tap = w[pl.ds(pl.multiple_of((6 * (1 - top) + b) * br, br), br), :]
+        rows, cols = value.shape[:2]
+        return jnp.dot(value.reshape(rows * cols, br), tap, preferred_element_type=F32).reshape(rows, cols, br)
+
+    for i, (cols, _) in enumerate(groups):
         for b in range(3):
-            tap = w[pl.ds(pl.multiple_of((6 * (1 - top) + b) * br, br), br), :]
-            term = jnp.dot(there, tap, preferred_element_type=F32).reshape(RR, len(cols) * TILE, br)
+            term = product(near[i][...], b)
             for j, col in enumerate(cols):
-                at = (1 + col) * TILE - lo
-                apart[b, :, at : at + TILE, :] = term[:, j * TILE : (j + 1) * TILE, :]
+                apart[b, :, (1 + col) * TILE : (2 + col) * TILE, :] = term[:, j * TILE : (j + 1) * TILE, :]
+    me = lax.axis_index("col")
+    for on, b, at, ref in ((me > 0, 0, 0, sides[0]), (me < cols_n - 1, 2, TILE + width, sides[-1])):
+        there = ref[...]
+        apart[b, :, at : at + TILE, :] = product(jnp.where(on, there, jnp.zeros_like(there)), b)
     copies = []
     step = RR // LATE
     for at in range(0, RR, step):
-        rows = pl.ds((1 - top) * rest + at, step)
-        for left, right in zip(cuts, cuts[1:]):
-            total = partial[rows, left:right, :]
-            for b in range(3):
-                if reach[b][0] <= left and right <= reach[b][1]:
-                    first = left + (b - 1) * RC + TILE - lo
-                    total = total + apart[b, at : at + step, first : first + right - left, :]
-            done[at : at + step, left:right, :] = jnp.maximum(total, 0).astype(BF16)
-        copies.append(pltpu.make_async_copy(done.at[pl.ds(at, step)], out.at[rows], sems.at[len(copies)]))
+        rows = pl.ds(at, step)
+        total = partial[rows]
+        for b in range(3):
+            left = TILE - RC + b * RC
+            total = total + apart[b, at : at + step, left : left + width, :]
+        done[rows] = jnp.maximum(total, 0).astype(BF16)
+        there = out.at[pl.ds((1 - top) * rest + at, step)]
+        copies.append(pltpu.make_async_copy(done.at[rows], there, sems.at[len(copies)]))
         copies[-1].start()
     for copy in copies:
         copy.wait()
 
 
-def blocks_of(height):
-    rest = height - RR
-    cuts = [0, rest // 2, rest, RR, RR + rest // 2, height]
-    return [(lo, hi - lo) for lo, hi in zip(cuts, cuts[1:]) if hi > lo]
-
-
 def plan(tile_cols):
-    groups = [([0, tile_cols - 1], True), (list(range(1, tile_cols - 1)), False)]
+    groups = [([0, tile_cols - 1], False), (list(range(1, tile_cols - 1)), False)]
     order = [(0, True), (0, False), (1, True), (1, False)]
     return groups, order
 
@@ -408,21 +396,21 @@
         near = one == groups[i][1]
         halo[i, near] = lax.ppermute(value, ("row", "col"), swap(near))
 
-    side = jax.ShapeDtypeStruct((4 * RR, TILE, br), BF16)
-    one_swap = cols_n == 2
-    picked = pl.pallas_call(
-        functools.partial(pick_kernel, cols_n),
-        out_shape=[side] if one_swap else [side, side],
-        in_specs=[VM] * 4,
-        out_specs=[VM] * (1 if one_swap else 2),
-        compiler_params=params(4),
-        cost_estimate=cost(0, MIB),
-        name="pick",
-    )(local[0, True], local[0, False], halo[0, True], halo[0, False])
-    if one_swap:
-        sides = [lax.ppermute(picked[0], "col", [(0, 1), (1, 0)])]
-    else:
-        sides = [
+    def trade(arrays, after=()):
+        used = len(arrays)
+        side = jax.ShapeDtypeStruct((used * RR, TILE, br), BF16)
+        n_out = 1 if cols_n == 2 else 2
+        picked = pl.pallas_call(
+            functools.partial(pick_kernel, cols_n, used),
+            out_shape=[side] * n_out,
+            in_specs=[VM] * used + [pl.BlockSpec(memory_space=pl.ANY)] * len(after),
+            out_specs=[VM] * n_out,
+            compiler_params=params(4),
+            cost_estimate=cost(0, MIB),
+        )(*arrays, *after)
+        if cols_n == 2:
+            return [lax.ppermute(picked[0], "col", [(0, 1), (1, 0)])]
+        return [
             lax.ppermute(picked[0], "col", [(i, i + 1) for i in range(cols_n - 1)]),
             lax.ppermute(picked[1], "col", [(i + 1, i) for i in range(cols_n - 1)]),
         ]
@@ -432,40 +420,42 @@
     n_groups = len(groups)
     pick = lambda table, key: [table[i, key] for i in range(n_groups)]
     flops = 2 * width * 3 * br * br
+    sides = trade([local[0, True], local[0, False], halo[0, False]])
     out, partial = pl.pallas_call(
         functools.partial(conv_early, groups, rows_n, cols_n, height),
         out_shape=[
             jax.ShapeDtypeStruct((height, width, br), BF16),
-            jax.ShapeDtypeStruct((height, width, br), F32),
+            jax.ShapeDtypeStruct((RR, width, br), F32),
         ],
-        in_specs=[VM] * (2 + 3 * n_groups + len(sides)),
+        in_specs=[VM] * (1 + 3 * n_groups + len(sides)),
         out_specs=[HBM, VM],
         scratch_shapes=[
-            pltpu.VMEM((height + 2 * RR, width + 2 * TILE, br), BF16),
-            pltpu.VMEM((height + 2 * RR, width, 3 * br), BF16),
+            pltpu.VMEM((height + RR, width + 2 * TILE, br), BF16),
+            pltpu.VMEM((height + RR, width, 3 * br), BF16),
             pltpu.VMEM((rest, width, br), BF16),
             pltpu.SemaphoreType.DMA,
         ],
         compiler_params=params(CONV_MIB),
-        cost_estimate=cost(flops * 3 * height, 4 * MIB),
+        cost_estimate=cost(flops * (3 * rest + 2 * RR), 4 * MIB),
         name="conv_early",
-    )(taps, *pick(local, True), *pick(local, False), *pick(halo, False), halo[0, True], *sides)
-    inner = sum(len(cols) for cols, _ in groups[1:]) * TILE
+    )(taps, *pick(local, True), *pick(local, False), *pick(halo, False), *sides)
+    rims = trade([halo[0, True]], [partial])
+    n_in = 2 + n_groups + len(rims)
     return pl.pallas_call(
-        functools.partial(conv_late, groups, height),
+        functools.partial(conv_late, groups, cols_n, height),
         out_shape=jax.ShapeDtypeStruct((height, width, br), BF16),
-        in_specs=[VM] * (1 + n_groups) + [HBM],
+        in_specs=[VM] * n_in + [HBM],
         out_specs=HBM,
-        input_output_aliases={1 + n_groups: 0},
+        input_output_aliases={n_in: 0},
         scratch_shapes=[
-            pltpu.VMEM((3, RR, inner + 2 * TILE, br), F32),
+            pltpu.VMEM((3, RR, width + 2 * TILE, br), F32),
             pltpu.VMEM((RR, width, br), BF16),
             pltpu.SemaphoreType.DMA((LATE,)),
         ],
-        compiler_params=params(CONV_MIB),
+        compiler_params=params(16),
         cost_estimate=cost(flops * RR, 4 * MIB),
         name="conv_late",
-    )(taps, partial, *pick(halo, True)[1:], out)
+    )(taps, partial, *pick(halo, True), *rims, out)
 
 
 def solution(mesh):

time: 53.4 us -> 42.8 us (0.80)
  the two profiles are of different devices: /device:TPU:11 before, /device:TPU:21 now
where the time goes in v8:
time: 42.8 us; the launch traced here: 42.6 us
  Pallas kernels  29.2 us (68%)
  waiting for transfers between devices  8.91 us (21%)
  starting transfers between devices  4.19 us (10%)
    pallas_call x3, Pallas kernels, shards(): pl.pallas_call(functools.partial(later_chunk, chunks[n], starts[n], heigh...  15.7 us
    ppermute x4, waiting for transfers between devices, shards(): halo[i, near] = lax.ppermute(value, ('row', 'col'), swap(near))  8.9 us
    pallas_call x1, Pallas kernels, shards(): pl.pallas_call(functools.partial(first_chunk, chunks, height), out_shape=...  7.99 us
    pallas_call x1, Pallas kernels, shards(): pl.pallas_call(functools.partial(conv_early, groups, rows_n, cols_n, heig...  3.95 us
    ppermute x2, starting transfers between devices, trade(): return [lax.ppermute(picked[0], 'col', [(0, 1), (1, 0)])]  2.67 us
    pallas_call x1, Pallas kernels, shards(): pl.pallas_call(functools.partial(conv_late, groups, cols_n, height), out_...  1.58 us
    ppermute x4, starting transfers between devices, shards(): halo[i, near] = lax.ppermute(value, ('row', 'col'), swap(near))  1.52 us
  transfers between devices with their start and end apart: 6, of which 3 were waited for; matrix products, arithmetic and copies ran while one was open for 0% of the time, Pallas kernels for 46%

profile of v8, /device:TPU:21, one launch (start us, length us, event | category | flops | bytes accessed | tf_op | source)
XLA Modules:
  0.0 42.6 jit_solution(4621672556922722554)
XLA Ops:
  0.0 0.0 copy-start.1
  0.0 8.0 %trunk_first.1 = (bf16[18,32,256]{2,1,0:T(8,128)(2,1)S(1)}, bf16[2048,1024]{1,0:T(8,128)(2,1)S(1)}, bf16[1024,512]{1,0:T(8,128)(2,1)S(1)}, bf16[512,2048]{1,0:T(...) custom-call(s32[2,4]{1,0:T(2,128)} %flags.5, bf16[2,4,256,1024]{3,2,1,0:T(8,128)(2,1)} %feats.1, ...), custom_call_target="tpu_custom_call" | custom-call | flops 4831838208 | bytes 12582912 | tf_op jit(solution)/shard_map/trunk_first/pallas_call | solution.py:345
  8.0 1.3 %collective-permute-start = (bf16[18,32,256]{2,1,0:T(8,128)(2,1)S(1)}, bf16[18,32,256]{2,1,0:T(8,128)(2,1)S(1)}, u32[]{:S(2)}, u32[]{:S(2)}) collective-permute-start(bf16[18,32,256]{2,1,0:T(8,128)(2,1)S(1)} %get-tuple-element.13.refs_0_), channel_id=1, source_target_pairs={{0,1},{1,0},{2,4},{3,5},{4,2},{5,3},{6,8},{7,9},{8,6},{9,7},{10,12... | collective-permute-start | bytes 884744 | tf_op jit(solution)/shard_map/ppermute | solution.py:397
  9.3 0.0 copy-done.1
  9.3 4.7 %shard_map.74.refs_1_.refs_2_ = bf16[18,32,256]{2,1,0:T(8,128)(2,1)S(1)} custom-call(s32[2,4]{1,0:T(2,128)S(1)} %copy-done.1, bf16[2048,1024]{1,0:T(8,128)(2,1)S(1)} %get-tuple-element.14.xs, bf16[1024,512]{1,0:T(8,128)(2,1)S(1)} %get-tuple-element.15.wr, bf16[512,2048]{1,0:T(8,128)(2,1)S(1)} %get-tuple-element.16.we, ...), custom_call_target="tpu_custom_call" | custom-call | flops 3758096384 | bytes 1048576 | tf_op jit(solution)/shard_map/pallas_call | solution.py:387
  14.1 0.1 collective-permute-start.3
  14.1 2.8 %collective-permute-done.refs_2_.refs_4_ = bf16[18,32,256]{2,1,0:T(8,128)(2,1)S(1)} collective-permute-done((bf16[18,32,256]{2,1,0:T(8,128)(2,1)S(1)}, bf16[18,32,256]{2,1,0:T(8,128)(2,1)S(1)}, u32[]{:S(2)}, u32[]{:S(2)}) %collective-permute-start) | collective-permute-done | bytes 294944 | tf_op jit(solution)/shard_map/ppermute | solution.py:397
  16.9 1.7 %collective-permute-start.2 = (bf16[54,16,256]{2,1,0:T(8,128)(2,1)S(1)}, bf16[54,16,256]{2,1,0:T(8,128)(2,1)S(1)}, u32[]{:S(2)}, u32[]{:S(2)}) collective-permute-start(bf16[54,16,256]{2,1,0:T(8,128)(2,1)S(1)} %shard_map.76), channel_id=1, source_target_pairs={{0,1},{1,0},{2,3},{3,2},{4,5},{5,4},{6,7},{7,6},{8,9},{9,8},{10,11... | collective-permute-start | bytes 1327112 | tf_op jit(solution)/shard_map/ppermute | solution.py:412
  18.6 6.0 %shard_map.73.refs_0_.refs_1_ = bf16[18,32,256]{2,1,0:T(8,128)(2,1)S(1)} custom-call(s32[2,4]{1,0:T(2,128)S(1)} %copy-done.1, bf16[2048,1024]{1,0:T(8,128)(2,1)S(1)} %get-tuple-element.14.xs, bf16[1024,512]{1,0:T(8,128)(2,1)S(1)} %get-tuple-element.15.wr, bf16[512,2048]{1,0:T(8,128)(2,1)S(1)} %get-tuple-element.16.we, ...), custom_call_target="tpu_custom_call" | custom-call | flops 4831838208 | bytes 1048576 | tf_op jit(solution)/shard_map/pallas_call | solution.py:387
  24.6 0.0 copy-start
  24.6 0.1 collective-permute-start.1
  24.7 5.0 %shard_map.75.refs_3_ = bf16[18,32,256]{2,1,0:T(8,128)(2,1)S(1)} custom-call(s32[2,4]{1,0:T(2,128)S(1)} %copy-done.1, bf16[2048,1024]{1,0:T(8,128)(2,1)S(1)} %get-tuple-element.14.xs, bf16[1024,512]{1,0:T(8,128)(2,1)S(1)} %get-tuple-element.15.wr, bf16[512,2048]{1,0:T(8,128)(2,1)S(1)} %get-tuple-element.16.we, bf16[1024,2048]{1,0:T(8,128)(2,1)S(1)} %get-tuple-element.17.ws, ...), custom_call_target="tpu_custom_call" | custom-call | flops 3758096384 | bytes 1048576 | tf_op jit(solution)/shard_map/pallas_call | solution.py:387
  29.6 0.1 collective-permute-start.4
  29.7 4.4 %collective-permute-done.1.refs_5_ = bf16[18,32,256]{2,1,0:T(8,128)(2,1)S(1)} collective-permute-done((bf16[18,32,256]{2,1,0:T(8,128)(2,1)S(1)}, bf16[18,32,256]{2,1,0:T(8,128)(2,1)S(1)}, u32[]{:S(2)}, u32[]{:S(2)}) %collective-permute-start.1) | collective-permute-done | bytes 294944 | tf_op jit(solution)/shard_map/ppermute | solution.py:397
  34.1 0.0 collective-permute-done.2.refs_6_
  34.1 0.0 copy-done
  34.1 3.9 %conv_early.1 = (bf16[32,64,256]{2,1,0:T(8,128)(2,1)}, f32[18,64,256]{2,1,0:T(8,128)S(1)}) custom-call(bf16[2304,256]{1,0:T(8,128)(2,1)S(1)} %bitcast.1, bf16[18,32,256]{2,1,0:T(8,128)(2,1)S(1)} %get-tuple-element.13.refs_0_, bf16[18,32,256]{2,1,0:T(8,128)(2,1)S(1)} %shard_map.73.refs_0_.refs_1_, bf16[18,32,256]{2,1,0:T(8,128)(2,1)S(1)} %shard_map.74.refs_1_.refs_2_, ...), custom_call_target="tpu_custom_call" | custom-call | flops 1962934272 | bytes 4194304 | tf_op jit(solution)/shard_map/conv_early/pallas_call | solution.py:424
  38.1 0.0 collective-permute-done.3.refs_0_
  38.1 1.0 %collective-permute-start.5 = (bf16[18,16,256]{2,1,0:T(8,128)(2,1)S(1)}, bf16[18,16,256]{2,1,0:T(8,128)(2,1)S(1)}, u32[]{:S(2)}, u32[]{:S(2)}) collective-permute-start(bf16[18,16,256]{2,1,0:T(8,128)(2,1)S(1)} %shard_map.77), channel_id=1, source_target_pairs={{0,1},{1,0},{2,3},{3,2},{4,5},{5,4},{6,7},{7,6},{8,9},{9,8},{10,11... | collective-permute-start | bytes 442376 | tf_op jit(solution)/shard_map/ppermute | solution.py:412
  39.1 1.7 %collective-permute-done.4.refs_1_ = bf16[18,32,256]{2,1,0:T(8,128)(2,1)S(1)} collective-permute-done((bf16[18,32,256]{2,1,0:T(8,128)(2,1)S(1)}, bf16[18,32,256]{2,1,0:T(8,128)(2,1)S(1)}, u32[]{:S(2)}, u32[]{:S(2)}) %collective-permute-start.4) | collective-permute-done | bytes 294944 | tf_op jit(solution)/shard_map/ppermute | solution.py:397
  40.9 0.0 collective-permute-done.5.refs_2_
  40.9 1.6 %conv_late.1 = bf16[32,64,256]{2,1,0:T(8,128)(2,1)} custom-call(bf16[2304,256]{1,0:T(8,128)(2,1)S(1)} %bitcast.2, f32[18,64,256]{2,1,0:T(8,128)S(1)} %get-tuple-element.19.refs_1_.partial, bf16[18,32,256]{2,1,0:T(8,128)(2,1)S(1)} %collective-permute-done.3.refs_0_, ...), custom_call_target="tpu_custom_call", output_to_operand_aliasing={{}: (5, {})} | custom-call | flops 452984832 | bytes 4194304 | tf_op jit(solution)/shard_map/conv_late/pallas_call | solution.py:444
  (2 shorter events, 0.0 us)
Async XLA Ops:
  0.0 9.3 %copy-start.1 = (s32[2,4]{1,0:T(2,128)S(1)}, s32[2,4]{1,0:T(2,128)}, u32[]{:S(2)}) copy-start(s32[2,4]{1,0:T(2,128)} %flags.5) | copy-start | bytes 100
  8.0 8.9 %collective-permute-start = (bf16[18,32,256]{2,1,0:T(8,128)(2,1)S(1)}, bf16[18,32,256]{2,1,0:T(8,128)(2,1)S(1)}, u32[]{:S(2)}, u32[]{:S(2)}) collective-permute-start(bf16[18,32,256]{2,1,0:T(8,128)(2,1)S(1)} %get-tuple-element.13.refs_0_), channel_id=1, source_target_pairs={{0,1},{1,0},{2,4},{3,5},{4,2},{5,3},{6,8},{7,9},{8,6},{9,7},{10,12... | collective-permute-start | bytes 884744 | tf_op jit(solution)/shard_map/ppermute | solution.py:397
  14.1 24.0 %collective-permute-start.3 = (bf16[18,32,256]{2,1,0:T(8,128)(2,1)S(1)}, bf16[18,32,256]{2,1,0:T(8,128)(2,1)S(1)}, u32[]{:S(2)}, u32[]{:S(2)}) collective-permute-start(bf16[18,32,256]{2,1,0:T(8,128)(2,1)S(1)} %shard_map.74.refs_1_.refs_2_), channel_id=1, source_target_pairs={{0,2},{1,3},{2,0},{3,1},{4,6},{5,7},{6,4},{7,5},{8,10},{9,11},{10,... | collective-permute-start | bytes 884744 | tf_op jit(solution)/shard_map/ppermute | solution.py:397
  16.9 17.2 %collective-permute-start.2 = (bf16[54,16,256]{2,1,0:T(8,128)(2,1)S(1)}, bf16[54,16,256]{2,1,0:T(8,128)(2,1)S(1)}, u32[]{:S(2)}, u32[]{:S(2)}) collective-permute-start(bf16[54,16,256]{2,1,0:T(8,128)(2,1)S(1)} %shard_map.76), channel_id=1, source_target_pairs={{0,1},{1,0},{2,3},{3,2},{4,5},{5,4},{6,7},{7,6},{8,9},{9,8},{10,11... | collective-permute-start | bytes 1327112 | tf_op jit(solution)/shard_map/ppermute | solution.py:412
  24.6 9.5 %copy-start = (bf16[9,256,256]{2,1,0:T(8,128)(2,1)S(1)}, bf16[9,256,256]{2,1,0:T(8,128)(2,1)}, u32[]{:S(2)}) copy-start(bf16[9,256,256]{2,1,0:T(8,128)(2,1)} %param.13) | copy-start | bytes 3538948
  24.6 9.5 %collective-permute-start.1 = (bf16[18,32,256]{2,1,0:T(8,128)(2,1)S(1)}, bf16[18,32,256]{2,1,0:T(8,128)(2,1)S(1)}, u32[]{:S(2)}, u32[]{:S(2)}) collective-permute-start(bf16[18,32,256]{2,1,0:T(8,128)(2,1)S(1)} %shard_map.73.refs_0_.refs_1_), channel_id=1, source_target_pairs={{0,1},{1,0},{2,4},{3,5},{4,2},{5,3},{6,8},{7,9},{8,6},{9,7},{10,12... | collective-permute-start | bytes 884744 | tf_op jit(solution)/shard_map/ppermute | solution.py:397
  29.6 11.2 %collective-permute-start.4 = (bf16[18,32,256]{2,1,0:T(8,128)(2,1)S(1)}, bf16[18,32,256]{2,1,0:T(8,128)(2,1)S(1)}, u32[]{:S(2)}, u32[]{:S(2)}) collective-permute-start(bf16[18,32,256]{2,1,0:T(8,128)(2,1)S(1)} %shard_map.75.refs_3_), channel_id=1, source_target_pairs={{0,2},{1,3},{2,0},{3,1},{4,6},{5,7},{6,4},{7,5},{8,10},{9,11},{10,... | collective-permute-start | bytes 884744 | tf_op jit(solution)/shard_map/ppermute | solution.py:397
  38.1 2.8 %collective-permute-start.5 = (bf16[18,16,256]{2,1,0:T(8,128)(2,1)S(1)}, bf16[18,16,256]{2,1,0:T(8,128)(2,1)S(1)}, u32[]{:S(2)}, u32[]{:S(2)}) collective-permute-start(bf16[18,16,256]{2,1,0:T(8,128)(2,1)S(1)} %shard_map.77), channel_id=1, source_target_pairs={{0,1},{1,0},{2,3},{3,2},{4,5},{5,4},{6,7},{7,6},{8,9},{9,8},{10,11... | collective-permute-start | bytes 442376 | tf_op jit(solution)/shard_map/ppermute | solution.py:412

commit v9 on v8

--- a/solution.py
+++ b/solution.py
@@ -283,39 +283,73 @@
     return (me > 0) & (me < rows_n - 1)
 
 
-def conv_late(groups, cols_n, height, w, partial, *refs):
-    near = refs[: len(groups)]
-    sides = refs[len(groups) : -5]
+def products(halo, cols, w, taps, base, apart):
+    top = near_is_top()
+    value = halo[...]
+    rows, wide, br = value.shape
+    for b in taps:
+        tap = w[pl.ds(pl.multiple_of((6 * (1 - top) + b) * br, br), br), :]
+        term = jnp.dot(value.reshape(rows * wide, br), tap, preferred_element_type=F32).reshape(rows, wide, br)
+        for j, col in enumerate(cols):
+            at = (1 + col) * TILE - base
+            apart[b, :, at : at + TILE, :] = term[:, j * TILE : (j + 1) * TILE, :]
+
+
+def conv_mid(groups, cols_n, w, partial, near, *refs):
+    sides = refs[:-3]
+    out, apart, rim = refs[-3:]
+    width, br = partial.shape[1:]
+    tile_cols = width // TILE
+    for cols, _ in groups[1:]:
+        for col in cols:
+            for b in range(3):
+                apart[b, :, (1 + col) * TILE : (2 + col) * TILE, :] = jnp.zeros((RR, TILE, br), F32)
+    products(near, groups[0][0], w, range(3), 0, apart)
+    me = lax.axis_index("col")
+    for on, b, col, ref in ((me > 0, 0, -1, sides[0]), (me < cols_n - 1, 2, tile_cols, sides[-1])):
+        there = ref[...]
+        rim[...] = jnp.where(on, there, jnp.zeros_like(there))
+        products(rim, [col], w, [b], 0, apart)
+    for at in range(0, RR, 6):
+        rows = slice(at, min(at + 6, RR))
+        total = partial[rows]
+        for b in range(3):
+            left = TILE - RC + b * RC
+            total = total + apart[b, rows, left : left + width, :]
+        out[rows] = total
+
+
+def conv_late(groups, height, w, partial, *refs):
+    near = refs[: len(groups) - 1]
     _, out, apart, done, sems = refs[-5:]
     top = near_is_top()
     width, br = partial.shape[1:]
     rest = height - RR
-
-    def product(value, b):
-        tap = w[pl.ds(pl.multiple_of((6 * (1 - top) + b) * br, br), br), :]
-        rows, cols = value.shape[:2]
-        return jnp.dot(value.reshape(rows * cols, br), tap, preferred_element_type=F32).reshape(rows, cols, br)
-
-    for i, (cols, _) in enumerate(groups):
-        for b in range(3):
-            term = product(near[i][...], b)
-            for j, col in enumerate(cols):
-                apart[b, :, (1 + col) * TILE : (2 + col) * TILE, :] = term[:, j * TILE : (j + 1) * TILE, :]
-    me = lax.axis_index("col")
-    for on, b, at, ref in ((me > 0, 0, 0, sides[0]), (me < cols_n - 1, 2, TILE + width, sides[-1])):
-        there = ref[...]
-        apart[b, :, at : at + TILE, :] = product(jnp.where(on, there, jnp.zeros_like(there)), b)
+    used = sorted(col for cols, _ in groups[1:] for col in cols)
+    lo, hi = used[0] * TILE, (used[-1] + 1) * TILE
+    reach = []
+    for b in range(3):
+        shift = (b - 1) * RC
+        reach.append((max(0, lo - shift) // TILE * TILE, min(width, -(-(hi - shift) // TILE) * TILE)))
+    cuts = sorted({0, width, *[edge for span_b in reach for edge in span_b]})
+    zero = jnp.zeros((RR, TILE, br), F32)
+    for b in range(3):
+        apart[b, :, 0:TILE, :] = zero
+        apart[b, :, TILE + hi - lo : 2 * TILE + hi - lo, :] = zero
+    for i, (cols, _) in enumerate(groups[1:]):
+        products(near[i], cols, w, range(3), lo, apart)
     copies = []
     step = RR // LATE
     for at in range(0, RR, step):
-        rows = pl.ds(at, step)
-        total = partial[rows]
-        for b in range(3):
-            left = TILE - RC + b * RC
-            total = total + apart[b, at : at + step, left : left + width, :]
-        done[rows] = jnp.maximum(total, 0).astype(BF16)
+        for left, right in zip(cuts, cuts[1:]):
+            total = partial[at : at + step, left:right, :]
+            for b in range(3):
+                if reach[b][0] <= left and right <= reach[b][1]:
+                    first = left + (b - 1) * RC + TILE - lo
+                    total = total + apart[b, at : at + step, first : first + right - left, :]
+            done[at : at + step, left:right, :] = jnp.maximum(total, 0).astype(BF16)
         there = out.at[pl.ds((1 - top) * rest + at, step)]
-        copies.append(pltpu.make_async_copy(done.at[rows], there, sems.at[len(copies)]))
+        copies.append(pltpu.make_async_copy(done.at[pl.ds(at, step)], there, sems.at[len(copies)]))
         copies[-1].start()
     for copy in copies:
         copy.wait()
@@ -440,22 +474,36 @@
         name="conv_early",
     )(taps, *pick(local, True), *pick(local, False), *pick(halo, False), *sides)
     rims = trade([halo[0, True]], [partial])
-    n_in = 2 + n_groups + len(rims)
+    partial = pl.pallas_call(
+        functools.partial(conv_mid, groups, cols_n),
+        out_shape=jax.ShapeDtypeStruct((RR, width, br), F32),
+        in_specs=[VM] * (3 + len(rims)),
+        out_specs=VM,
+        scratch_shapes=[
+            pltpu.VMEM((3, RR, width + 2 * TILE, br), F32),
+            pltpu.VMEM((RR, TILE, br), BF16),
+        ],
+        compiler_params=params(16),
+        cost_estimate=cost(flops * RR, 4 * MIB),
+        name="conv_mid",
+    )(taps, partial, halo[0, True], *rims)
+    inner = sum(len(cols) for cols, _ in groups[1:]) * TILE
+    n_in = 1 + n_groups
     return pl.pallas_call(
-        functools.partial(conv_late, groups, cols_n, height),
+        functools.partial(conv_late, groups, height),
         out_shape=jax.ShapeDtypeStruct((height, width, br), BF16),
         in_specs=[VM] * n_in + [HBM],
         out_specs=HBM,
         input_output_aliases={n_in: 0},
         scratch_shapes=[
-            pltpu.VMEM((3, RR, width + 2 * TILE, br), F32),
+            pltpu.VMEM((3, RR, inner + 2 * TILE, br), F32),
             pltpu.VMEM((RR, width, br), BF16),
             pltpu.SemaphoreType.DMA((LATE,)),
         ],
         compiler_params=params(16),
         cost_estimate=cost(flops * RR, 4 * MIB),
         name="conv_late",
-    )(taps, partial, *pick(halo, True), *rims, out)
+    )(taps, partial, *pick(halo, True)[1:], out)
 
 
 def solution(mesh):

time: 42.8 us -> 42.4 us (level)
  waiting for transfers between devices: 8.91 us -> 8.35 us
    ppermute x4, waiting for transfers between devices: 8.9 us -> 7.34 us  [shards(): halo[i, near] = lax.ppermute(value, ('row', 'col'), swap(near))]
    ppermute x2, waiting for transfers between devices: 0.01 us -> 1.01 us  [trade(): return [lax.ppermute(picked[0], 'col', [(0, 1), (1, 0)])]]
    pallas_call x1 -> x2, Pallas kernels: 1.58 us -> 1.78 us  [the longest x1 1.23 us: shards(): pl.pallas_call(functools.partial(conv_late, groups, height), out_shape=ja...]
  transfers between devices with their start and end apart: 6 -> 6, of which waited for: 3 -> 4; matrix products, arithmetic and copies ran while one was open for 0% -> 0% of each run, Pallas kernels for 46% -> 48%
where the time goes in v9:
time: 42.4 us; the launch traced here: 42.3 us
  Pallas kernels  29.4 us (69%)
  waiting for transfers between devices  8.35 us (20%)
  starting transfers between devices  4.19 us (10%)
    pallas_call x3, Pallas kernels, shards(): pl.pallas_call(functools.partial(later_chunk, chunks[n], starts[n], heigh...  15.7 us
    pallas_call x1, Pallas kernels, shards(): pl.pallas_call(functools.partial(first_chunk, chunks, height), out_shape=...  7.99 us
    ppermute x4, waiting for transfers between devices, shards(): halo[i, near] = lax.ppermute(value, ('row', 'col'), swap(near))  7.34 us
    pallas_call x1, Pallas kernels, shards(): pl.pallas_call(functools.partial(conv_early, groups, rows_n, cols_n, heig...  3.95 us
    ppermute x2, starting transfers between devices, trade(): return [lax.ppermute(picked[0], 'col', [(0, 1), (1, 0)])]  2.67 us
    ppermute x4, starting transfers between devices, shards(): halo[i, near] = lax.ppermute(value, ('row', 'col'), swap(near))  1.52 us
    pallas_call x1, Pallas kernels, shards(): pl.pallas_call(functools.partial(conv_late, groups, height), out_shape=ja...  1.23 us
    ppermute x2, waiting for transfers between devices, trade(): return [lax.ppermute(picked[0], 'col', [(0, 1), (1, 0)])]  1.01 us
  transfers between devices with their start and end apart: 6, of which 4 were waited for; matrix products, arithmetic and copies ran while one was open for 0% of the time, Pallas kernels for 48%

profile of v9, /device:TPU:21, one launch (start us, length us, event | category | flops | bytes accessed | tf_op | source)
XLA Modules:
  0.0 42.3 jit_solution(6986410944238564608)
XLA Ops:
  0.0 0.0 copy-start.1
  0.0 8.0 %trunk_first.1 = (bf16[18,32,256]{2,1,0:T(8,128)(2,1)S(1)}, bf16[2048,1024]{1,0:T(8,128)(2,1)S(1)}, bf16[1024,512]{1,0:T(8,128)(2,1)S(1)}, bf16[512,2048]{1,0:T(...) custom-call(s32[2,4]{1,0:T(2,128)} %flags.5, bf16[2,4,256,1024]{3,2,1,0:T(8,128)(2,1)} %feats.1, ...), custom_call_target="tpu_custom_call" | custom-call | flops 4831838208 | bytes 12582912 | tf_op jit(solution)/shard_map/trunk_first/pallas_call | solution.py:379
  8.0 1.3 %collective-permute-start = (bf16[18,32,256]{2,1,0:T(8,128)(2,1)S(1)}, bf16[18,32,256]{2,1,0:T(8,128)(2,1)S(1)}, u32[]{:S(2)}, u32[]{:S(2)}) collective-permute-start(bf16[18,32,256]{2,1,0:T(8,128)(2,1)S(1)} %get-tuple-element.13.refs_0_), channel_id=1, source_target_pairs={{0,1},{1,0},{2,4},{3,5},{4,2},{5,3},{6,8},{7,9},{8,6},{9,7},{10,12... | collective-permute-start | bytes 884744 | tf_op jit(solution)/shard_map/ppermute | solution.py:431
  9.3 0.0 copy-done.1
  9.3 4.7 %shard_map.74.refs_1_.refs_2_ = bf16[18,32,256]{2,1,0:T(8,128)(2,1)S(1)} custom-call(s32[2,4]{1,0:T(2,128)S(1)} %copy-done.1, bf16[2048,1024]{1,0:T(8,128)(2,1)S(1)} %get-tuple-element.14.xs, bf16[1024,512]{1,0:T(8,128)(2,1)S(1)} %get-tuple-element.15.wr, bf16[512,2048]{1,0:T(8,128)(2,1)S(1)} %get-tuple-element.16.we, ...), custom_call_target="tpu_custom_call" | custom-call | flops 3758096384 | bytes 1048576 | tf_op jit(solution)/shard_map/pallas_call | solution.py:421
  14.1 0.1 collective-permute-start.3
  14.1 2.8 %collective-permute-done.refs_2_.refs_4_ = bf16[18,32,256]{2,1,0:T(8,128)(2,1)S(1)} collective-permute-done((bf16[18,32,256]{2,1,0:T(8,128)(2,1)S(1)}, bf16[18,32,256]{2,1,0:T(8,128)(2,1)S(1)}, u32[]{:S(2)}, u32[]{:S(2)}) %collective-permute-start) | collective-permute-done | bytes 294944 | tf_op jit(solution)/shard_map/ppermute | solution.py:431
  16.9 1.7 %collective-permute-start.2 = (bf16[54,16,256]{2,1,0:T(8,128)(2,1)S(1)}, bf16[54,16,256]{2,1,0:T(8,128)(2,1)S(1)}, u32[]{:S(2)}, u32[]{:S(2)}) collective-permute-start(bf16[54,16,256]{2,1,0:T(8,128)(2,1)S(1)} %shard_map.76), channel_id=1, source_target_pairs={{0,1},{1,0},{2,3},{3,2},{4,5},{5,4},{6,7},{7,6},{8,9},{9,8},{10,11... | collective-permute-start | bytes 1327112 | tf_op jit(solution)/shard_map/ppermute | solution.py:446
  18.6 6.0 %shard_map.73.refs_0_.refs_1_ = bf16[18,32,256]{2,1,0:T(8,128)(2,1)S(1)} custom-call(s32[2,4]{1,0:T(2,128)S(1)} %copy-done.1, bf16[2048,1024]{1,0:T(8,128)(2,1)S(1)} %get-tuple-element.14.xs, bf16[1024,512]{1,0:T(8,128)(2,1)S(1)} %get-tuple-element.15.wr, bf16[512,2048]{1,0:T(8,128)(2,1)S(1)} %get-tuple-element.16.we, ...), custom_call_target="tpu_custom_call" | custom-call | flops 4831838208 | bytes 1048576 | tf_op jit(solution)/shard_map/pallas_call | solution.py:421
  24.6 0.0 copy-start
  24.6 0.1 collective-permute-start.1
  24.7 5.0 %shard_map.75.refs_3_ = bf16[18,32,256]{2,1,0:T(8,128)(2,1)S(1)} custom-call(s32[2,4]{1,0:T(2,128)S(1)} %copy-done.1, bf16[2048,1024]{1,0:T(8,128)(2,1)S(1)} %get-tuple-element.14.xs, bf16[1024,512]{1,0:T(8,128)(2,1)S(1)} %get-tuple-element.15.wr, bf16[512,2048]{1,0:T(8,128)(2,1)S(1)} %get-tuple-element.16.we, bf16[1024,2048]{1,0:T(8,128)(2,1)S(1)} %get-tuple-element.17.ws, ...), custom_call_target="tpu_custom_call" | custom-call | flops 3758096384 | bytes 1048576 | tf_op jit(solution)/shard_map/pallas_call | solution.py:421
  29.6 0.1 collective-permute-start.5
  29.7 4.4 %collective-permute-done.1.refs_5_ = bf16[18,32,256]{2,1,0:T(8,128)(2,1)S(1)} collective-permute-done((bf16[18,32,256]{2,1,0:T(8,128)(2,1)S(1)}, bf16[18,32,256]{2,1,0:T(8,128)(2,1)S(1)}, u32[]{:S(2)}, u32[]{:S(2)}) %collective-permute-start.1) | collective-permute-done | bytes 294944 | tf_op jit(solution)/shard_map/ppermute | solution.py:431
  34.1 0.0 collective-permute-done.2.refs_6_
  34.1 0.0 copy-done
  34.1 3.9 %conv_early.1 = (bf16[32,64,256]{2,1,0:T(8,128)(2,1)}, f32[18,64,256]{2,1,0:T(8,128)S(1)}) custom-call(bf16[2304,256]{1,0:T(8,128)(2,1)S(1)} %bitcast.1, bf16[18,32,256]{2,1,0:T(8,128)(2,1)S(1)} %get-tuple-element.13.refs_0_, bf16[18,32,256]{2,1,0:T(8,128)(2,1)S(1)} %shard_map.73.refs_0_.refs_1_, bf16[18,32,256]{2,1,0:T(8,128)(2,1)S(1)} %shard_map.74.refs_1_.refs_2_, ...), custom_call_target="tpu_custom_call" | custom-call | flops 1962934272 | bytes 4194304 | tf_op jit(solution)/shard_map/conv_early/pallas_call | solution.py:458
  38.1 0.0 collective-permute-done.3.refs_0_.near
  38.1 1.0 %collective-permute-start.4 = (bf16[18,16,256]{2,1,0:T(8,128)(2,1)S(1)}, bf16[18,16,256]{2,1,0:T(8,128)(2,1)S(1)}, u32[]{:S(2)}, u32[]{:S(2)}) collective-permute-start(bf16[18,16,256]{2,1,0:T(8,128)(2,1)S(1)} %shard_map.77), channel_id=1, source_target_pairs={{0,1},{1,0},{2,3},{3,2},{4,5},{5,4},{6,7},{7,6},{8,9},{9,8},{10,11... | collective-permute-start | bytes 442376 | tf_op jit(solution)/shard_map/ppermute | solution.py:446
  39.1 1.0 %collective-permute-done.4.refs_0_ = bf16[18,16,256]{2,1,0:T(8,128)(2,1)S(1)} collective-permute-done((bf16[18,16,256]{2,1,0:T(8,128)(2,1)S(1)}, bf16[18,16,256]{2,1,0:T(8,128)(2,1)S(1)}, u32[]{:S(2)}, u32[]{:S(2)}) %collective-permute-start.4) | collective-permute-done | bytes 147488 | tf_op jit(solution)/shard_map/ppermute | solution.py:446
  40.1 0.6 %conv_mid.1.partial = f32[18,64,256]{2,1,0:T(8,128)S(1)} custom-call(bf16[2304,256]{1,0:T(8,128)(2,1)S(1)} %bitcast.2, f32[18,64,256]{2,1,0:T(8,128)S(1)} %get-tuple-element.19.refs_1_.partial, bf16[18,32,256]{2,1,0:T(8,128)(2,1)S(1)} %collective-permute-done.3.refs_0_.near, bf16[18,16,256]{2,1,0:T(8,128)(2,1)S(1)} %collective-permute-done.4.refs_0_), custom_call_target="tpu_custom_call" | custom-call | flops 452984832 | bytes 4194304 | tf_op jit(solution)/shard_map/conv_mid/pallas_call | solution.py:477
  40.7 0.2 collective-permute-done.5.refs_0_
  40.9 1.2 %conv_late.1 = bf16[32,64,256]{2,1,0:T(8,128)(2,1)} custom-call(bf16[2304,256]{1,0:T(8,128)(2,1)S(1)} %bitcast.3, f32[18,64,256]{2,1,0:T(8,128)S(1)} %conv_mid.1.partial, bf16[18,32,256]{2,1,0:T(8,128)(2,1)S(1)} %collective-permute-done.5.refs_0_, bf16[32,64,256]{2,1,0:T(8,128)(2,1)} %get-tuple-element.20.refs_1_), custom_call_target="tpu_custom_call", output_to_operand_aliasing={{}: (3, {})} | custom-call | flops 452984832 | bytes 4194304 | tf_op jit(solution)/shard_map/conv_late/pallas_call | solution.py:492
  (2 shorter events, 0.0 us)
Async XLA Ops:
  0.0 9.3 %copy-start.1 = (s32[2,4]{1,0:T(2,128)S(1)}, s32[2,4]{1,0:T(2,128)}, u32[]{:S(2)}) copy-start(s32[2,4]{1,0:T(2,128)} %flags.5) | copy-start | bytes 100
  8.0 8.9 %collective-permute-start = (bf16[18,32,256]{2,1,0:T(8,128)(2,1)S(1)}, bf16[18,32,256]{2,1,0:T(8,128)(2,1)S(1)}, u32[]{:S(2)}, u32[]{:S(2)}) collective-permute-start(bf16[18,32,256]{2,1,0:T(8,128)(2,1)S(1)} %get-tuple-element.13.refs_0_), channel_id=1, source_target_pairs={{0,1},{1,0},{2,4},{3,5},{4,2},{5,3},{6,8},{7,9},{8,6},{9,7},{10,12... | collective-permute-start | bytes 884744 | tf_op jit(solution)/shard_map/ppermute | solution.py:431
  14.1 24.0 %collective-permute-start.3 = (bf16[18,32,256]{2,1,0:T(8,128)(2,1)S(1)}, bf16[18,32,256]{2,1,0:T(8,128)(2,1)S(1)}, u32[]{:S(2)}, u32[]{:S(2)}) collective-permute-start(bf16[18,32,256]{2,1,0:T(8,128)(2,1)S(1)} %shard_map.74.refs_1_.refs_2_), channel_id=1, source_target_pairs={{0,2},{1,3},{2,0},{3,1},{4,6},{5,7},{6,4},{7,5},{8,10},{9,11},{10,... | collective-permute-start | bytes 884744 | tf_op jit(solution)/shard_map/ppermute | solution.py:431
  16.9 17.2 %collective-permute-start.2 = (bf16[54,16,256]{2,1,0:T(8,128)(2,1)S(1)}, bf16[54,16,256]{2,1,0:T(8,128)(2,1)S(1)}, u32[]{:S(2)}, u32[]{:S(2)}) collective-permute-start(bf16[54,16,256]{2,1,0:T(8,128)(2,1)S(1)} %shard_map.76), channel_id=1, source_target_pairs={{0,1},{1,0},{2,3},{3,2},{4,5},{5,4},{6,7},{7,6},{8,9},{9,8},{10,11... | collective-permute-start | bytes 1327112 | tf_op jit(solution)/shard_map/ppermute | solution.py:446
  24.6 9.5 %copy-start = (bf16[9,256,256]{2,1,0:T(8,128)(2,1)S(1)}, bf16[9,256,256]{2,1,0:T(8,128)(2,1)}, u32[]{:S(2)}) copy-start(bf16[9,256,256]{2,1,0:T(8,128)(2,1)} %param.13) | copy-start | bytes 3538948
  24.6 9.5 %collective-permute-start.1 = (bf16[18,32,256]{2,1,0:T(8,128)(2,1)S(1)}, bf16[18,32,256]{2,1,0:T(8,128)(2,1)S(1)}, u32[]{:S(2)}, u32[]{:S(2)}) collective-permute-start(bf16[18,32,256]{2,1,0:T(8,128)(2,1)S(1)} %shard_map.73.refs_0_.refs_1_), channel_id=1, source_target_pairs={{0,1},{1,0},{2,4},{3,5},{4,2},{5,3},{6,8},{7,9},{8,6},{9,7},{10,12... | collective-permute-start | bytes 884744 | tf_op jit(solution)/shard_map/ppermute | solution.py:431
  29.6 11.2 %collective-permute-start.5 = (bf16[18,32,256]{2,1,0:T(8,128)(2,1)S(1)}, bf16[18,32,256]{2,1,0:T(8,128)(2,1)S(1)}, u32[]{:S(2)}, u32[]{:S(2)}) collective-permute-start(bf16[18,32,256]{2,1,0:T(8,128)(2,1)S(1)} %shard_map.75.refs_3_), channel_id=1, source_target_pairs={{0,2},{1,3},{2,0},{3,1},{4,6},{5,7},{6,4},{7,5},{8,10},{9,11},{10,... | collective-permute-start | bytes 884744 | tf_op jit(solution)/shard_map/ppermute | solution.py:431
  38.1 2.0 %collective-permute-start.4 = (bf16[18,16,256]{2,1,0:T(8,128)(2,1)S(1)}, bf16[18,16,256]{2,1,0:T(8,128)(2,1)S(1)}, u32[]{:S(2)}, u32[]{:S(2)}) collective-permute-start(bf16[18,16,256]{2,1,0:T(8,128)(2,1)S(1)} %shard_map.77), channel_id=1, source_target_pairs={{0,1},{1,0},{2,3},{3,2},{4,5},{5,4},{6,7},{7,6},{8,9},{9,8},{10,11... | collective-permute-start | bytes 442376 | tf_op jit(solution)/shard_map/ppermute | solution.py:446

commit v10 on v9

--- a/solution.py
+++ b/solution.py
@@ -14,7 +14,7 @@
 BLOCK = 512
 DEPTH = 3
 WAITS = (1, 3)
-LATE = 2
+LATE = 1
 F32 = jnp.float32
 BF16 = jnp.bfloat16
 VM = pl.BlockSpec(memory_space=pltpu.VMEM)
@@ -356,7 +356,7 @@
 
 
 def plan(tile_cols):
-    groups = [([0, tile_cols - 1], False), (list(range(1, tile_cols - 1)), False)]
+    groups = [([0, tile_cols - 1], True), (list(range(1, tile_cols - 1)), False)]
     order = [(0, True), (0, False), (1, True), (1, False)]
     return groups, order
 
@@ -430,18 +430,18 @@
         near = one == groups[i][1]
         halo[i, near] = lax.ppermute(value, ("row", "col"), swap(near))
 
-    def trade(arrays, after=()):
+    def trade(arrays):
         used = len(arrays)
         side = jax.ShapeDtypeStruct((used * RR, TILE, br), BF16)
         n_out = 1 if cols_n == 2 else 2
         picked = pl.pallas_call(
             functools.partial(pick_kernel, cols_n, used),
             out_shape=[side] * n_out,
-            in_specs=[VM] * used + [pl.BlockSpec(memory_space=pl.ANY)] * len(after),
+            in_specs=[VM] * used,
             out_specs=[VM] * n_out,
             compiler_params=params(4),
             cost_estimate=cost(0, MIB),
-        )(*arrays, *after)
+        )(*arrays)
         if cols_n == 2:
             return [lax.ppermute(picked[0], "col", [(0, 1), (1, 0)])]
         return [
@@ -473,7 +473,7 @@
         cost_estimate=cost(flops * (3 * rest + 2 * RR), 4 * MIB),
         name="conv_early",
     )(taps, *pick(local, True), *pick(local, False), *pick(halo, False), *sides)
-    rims = trade([halo[0, True]], [partial])
+    rims = trade([halo[0, True]])
     partial = pl.pallas_call(
         functools.partial(conv_mid, groups, cols_n),
         out_shape=jax.ShapeDtypeStruct((RR, width, br), F32),

time: 42.4 us -> 47.3 us (1.12)
  the two profiles are of different devices: /device:TPU:21 before, /device:TPU:27 now
where the time goes in v10:
time: 47.3 us; the launch traced here: 47.1 us
  Pallas kernels  29.6 us (63%)
  waiting for transfers between devices  15.3 us (32%)
  starting transfers between devices  1.97 us (4%)
    pallas_call x3, Pallas kernels, shards(): pl.pallas_call(functools.partial(later_chunk, chunks[n], starts[n], heigh...  15.7 us
    ppermute x4, waiting for transfers between devices, shards(): halo[i, near] = lax.ppermute(value, ('row', 'col'), swap(near))  15.3 us
    pallas_call x1, Pallas kernels, shards(): pl.pallas_call(functools.partial(first_chunk, chunks, height), out_shape=...  7.99 us
    pallas_call x1, Pallas kernels, shards(): pl.pallas_call(functools.partial(conv_early, groups, rows_n, cols_n, heig...  3.94 us
    ppermute x2, starting transfers between devices, trade(): return [lax.ppermute(picked[0], 'col', [(0, 1), (1, 0)])]  1.69 us
    pallas_call x1, Pallas kernels, shards(): pl.pallas_call(functools.partial(conv_late, groups, height), out_shape=ja...  1.32 us
  transfers between devices with their start and end apart: 6, of which 3 were waited for; matrix products, arithmetic and copies ran while one was open for 0% of the time, Pallas kernels for 33%

profile of v10, /device:TPU:27, one launch (start us, length us, event | category | flops | bytes accessed | tf_op | source)
XLA Modules:
  0.0 47.1 jit_solution(9919775711379171369)
XLA Ops:
  0.0 0.0 copy-start.1
  0.0 8.0 %trunk_first.1 = (bf16[18,32,256]{2,1,0:T(8,128)(2,1)S(1)}, bf16[2048,1024]{1,0:T(8,128)(2,1)S(1)}, bf16[1024,512]{1,0:T(8,128)(2,1)S(1)}, bf16[512,2048]{1,0:T(...) custom-call(s32[2,4]{1,0:T(2,128)} %flags.5, bf16[2,4,256,1024]{3,2,1,0:T(8,128)(2,1)} %feats.1, ...), custom_call_target="tpu_custom_call" | custom-call | flops 4831838208 | bytes 12582912 | tf_op jit(solution)/shard_map/trunk_first/pallas_call | solution.py:379
  8.0 0.0 copy-done.1
  8.0 4.8 %shard_map.74.refs_1_.refs_2_ = bf16[18,32,256]{2,1,0:T(8,128)(2,1)S(1)} custom-call(s32[2,4]{1,0:T(2,128)S(1)} %copy-done.1, bf16[2048,1024]{1,0:T(8,128)(2,1)S(1)} %get-tuple-element.14.xs, bf16[1024,512]{1,0:T(8,128)(2,1)S(1)} %get-tuple-element.15.wr, bf16[512,2048]{1,0:T(8,128)(2,1)S(1)} %get-tuple-element.16.we, ...), custom_call_target="tpu_custom_call" | custom-call | flops 3758096384 | bytes 1048576 | tf_op jit(solution)/shard_map/pallas_call | solution.py:421
  12.8 0.1 collective-permute-start
  12.8 0.1 collective-permute-start.3
  12.9 8.8 %collective-permute-done.refs_2_.refs_4_ = bf16[18,32,256]{2,1,0:T(8,128)(2,1)S(1)} collective-permute-done((bf16[18,32,256]{2,1,0:T(8,128)(2,1)S(1)}, bf16[18,32,256]{2,1,0:T(8,128)(2,1)S(1)}, u32[]{:S(2)}, u32[]{:S(2)}) %collective-permute-start) | collective-permute-done | bytes 294944 | tf_op jit(solution)/shard_map/ppermute | solution.py:431
  21.7 1.6 %collective-permute-start.2 = (bf16[54,16,256]{2,1,0:T(8,128)(2,1)S(1)}, bf16[54,16,256]{2,1,0:T(8,128)(2,1)S(1)}, u32[]{:S(2)}, u32[]{:S(2)}) collective-permute-start(bf16[54,16,256]{2,1,0:T(8,128)(2,1)S(1)} %shard_map.76), channel_id=1, source_target_pairs={{0,1},{1,0},{2,3},{3,2},{4,5},{5,4},{6,7},{7,6},{8,9},{9,8},{10,11... | collective-permute-start | bytes 1327112 | tf_op jit(solution)/shard_map/ppermute | solution.py:446
  23.4 6.0 %shard_map.73.refs_0_.refs_1_ = bf16[18,32,256]{2,1,0:T(8,128)(2,1)S(1)} custom-call(s32[2,4]{1,0:T(2,128)S(1)} %copy-done.1, bf16[2048,1024]{1,0:T(8,128)(2,1)S(1)} %get-tuple-element.14.xs, bf16[1024,512]{1,0:T(8,128)(2,1)S(1)} %get-tuple-element.15.wr, bf16[512,2048]{1,0:T(8,128)(2,1)S(1)} %get-tuple-element.16.we, ...), custom_call_target="tpu_custom_call" | custom-call | flops 4831838208 | bytes 1048576 | tf_op jit(solution)/shard_map/pallas_call | solution.py:421
  29.4 0.0 copy-start
  29.4 0.1 collective-permute-start.1
  29.5 5.0 %shard_map.75.refs_3_ = bf16[18,32,256]{2,1,0:T(8,128)(2,1)S(1)} custom-call(s32[2,4]{1,0:T(2,128)S(1)} %copy-done.1, bf16[2048,1024]{1,0:T(8,128)(2,1)S(1)} %get-tuple-element.14.xs, bf16[1024,512]{1,0:T(8,128)(2,1)S(1)} %get-tuple-element.15.wr, bf16[512,2048]{1,0:T(8,128)(2,1)S(1)} %get-tuple-element.16.we, bf16[1024,2048]{1,0:T(8,128)(2,1)S(1)} %get-tuple-element.17.ws, ...), custom_call_target="tpu_custom_call" | custom-call | flops 3758096384 | bytes 1048576 | tf_op jit(solution)/shard_map/pallas_call | solution.py:421
  34.4 0.1 collective-permute-start.5
  34.5 0.0 collective-permute-done.3.refs_0_.near
  34.5 0.1 collective-permute-start.4
  34.6 4.3 %collective-permute-done.1.refs_5_ = bf16[18,32,256]{2,1,0:T(8,128)(2,1)S(1)} collective-permute-done((bf16[18,32,256]{2,1,0:T(8,128)(2,1)S(1)}, bf16[18,32,256]{2,1,0:T(8,128)(2,1)S(1)}, u32[]{:S(2)}, u32[]{:S(2)}) %collective-permute-start.1) | collective-permute-done | bytes 294944 | tf_op jit(solution)/shard_map/ppermute | solution.py:431
  38.9 0.0 collective-permute-done.2.refs_6_
  38.9 0.0 copy-done
  38.9 3.9 %conv_early.1 = (bf16[32,64,256]{2,1,0:T(8,128)(2,1)}, f32[18,64,256]{2,1,0:T(8,128)S(1)}) custom-call(bf16[2304,256]{1,0:T(8,128)(2,1)S(1)} %bitcast.1, bf16[18,32,256]{2,1,0:T(8,128)(2,1)S(1)} %get-tuple-element.13.refs_0_, bf16[18,32,256]{2,1,0:T(8,128)(2,1)S(1)} %shard_map.73.refs_0_.refs_1_, bf16[18,32,256]{2,1,0:T(8,128)(2,1)S(1)} %shard_map.74.refs_1_.refs_2_, ...), custom_call_target="tpu_custom_call" | custom-call | flops 1962934272 | bytes 4194304 | tf_op jit(solution)/shard_map/conv_early/pallas_call | solution.py:458
  42.9 0.0 collective-permute-done.4.refs_0_
  42.9 0.6 %conv_mid.1.partial = f32[18,64,256]{2,1,0:T(8,128)S(1)} custom-call(bf16[2304,256]{1,0:T(8,128)(2,1)S(1)} %bitcast.2, f32[18,64,256]{2,1,0:T(8,128)S(1)} %get-tuple-element.19.partial, bf16[18,32,256]{2,1,0:T(8,128)(2,1)S(1)} %collective-permute-done.3.refs_0_.near, bf16[18,16,256]{2,1,0:T(8,128)(2,1)S(1)} %collective-permute-done.4.refs_0_), custom_call_target="tpu_custom_call" | custom-call | flops 452984832 | bytes 4194304 | tf_op jit(solution)/shard_map/conv_mid/pallas_call | solution.py:477
  43.4 2.2 %collective-permute-done.5.refs_0_ = bf16[18,32,256]{2,1,0:T(8,128)(2,1)S(1)} collective-permute-done((bf16[18,32,256]{2,1,0:T(8,128)(2,1)S(1)}, bf16[18,32,256]{2,1,0:T(8,128)(2,1)S(1)}, u32[]{:S(2)}, u32[]{:S(2)}) %collective-permute-start.5) | collective-permute-done | bytes 294944 | tf_op jit(solution)/shard_map/ppermute | solution.py:431
  45.6 1.3 %conv_late.1 = bf16[32,64,256]{2,1,0:T(8,128)(2,1)} custom-call(bf16[2304,256]{1,0:T(8,128)(2,1)S(1)} %bitcast.3, f32[18,64,256]{2,1,0:T(8,128)S(1)} %conv_mid.1.partial, bf16[18,32,256]{2,1,0:T(8,128)(2,1)S(1)} %collective-permute-done.5.refs_0_, bf16[32,64,256]{2,1,0:T(8,128)(2,1)} %get-tuple-element.20.refs_1_), custom_call_target="tpu_custom_call", output_to_operand_aliasing={{}: (3, {})} | custom-call | flops 452984832 | bytes 4194304 | tf_op jit(solution)/shard_map/conv_late/pallas_call | solution.py:492
  (2 shorter events, 0.0 us)
Async XLA Ops:
  0.0 8.0 %copy-start.1 = (s32[2,4]{1,0:T(2,128)S(1)}, s32[2,4]{1,0:T(2,128)}, u32[]{:S(2)}) copy-start(s32[2,4]{1,0:T(2,128)} %flags.5) | copy-start | bytes 100
  12.8 8.9 %collective-permute-start = (bf16[18,32,256]{2,1,0:T(8,128)(2,1)S(1)}, bf16[18,32,256]{2,1,0:T(8,128)(2,1)S(1)}, u32[]{:S(2)}, u32[]{:S(2)}) collective-permute-start(bf16[18,32,256]{2,1,0:T(8,128)(2,1)S(1)} %shard_map.74.refs_1_.refs_2_), channel_id=1, source_target_pairs={{0,1},{1,0},{2,4},{3,5},{4,2},{5,3},{6,8},{7,9},{8,6},{9,7},{10,12... | collective-permute-start | bytes 884744 | tf_op jit(solution)/shard_map/ppermute | solution.py:431
  12.8 21.7 %collective-permute-start.3 = (bf16[18,32,256]{2,1,0:T(8,128)(2,1)S(1)}, bf16[18,32,256]{2,1,0:T(8,128)(2,1)S(1)}, u32[]{:S(2)}, u32[]{:S(2)}) collective-permute-start(bf16[18,32,256]{2,1,0:T(8,128)(2,1)S(1)} %get-tuple-element.13.refs_0_), channel_id=1, source_target_pairs={{0,2},{1,3},{2,0},{3,1},{4,6},{5,7},{6,4},{7,5},{8,10},{9,11},{10,... | collective-permute-start | bytes 884744 | tf_op jit(solution)/shard_map/ppermute | solution.py:431
  21.7 17.2 %collective-permute-start.2 = (bf16[54,16,256]{2,1,0:T(8,128)(2,1)S(1)}, bf16[54,16,256]{2,1,0:T(8,128)(2,1)S(1)}, u32[]{:S(2)}, u32[]{:S(2)}) collective-permute-start(bf16[54,16,256]{2,1,0:T(8,128)(2,1)S(1)} %shard_map.76), channel_id=1, source_target_pairs={{0,1},{1,0},{2,3},{3,2},{4,5},{5,4},{6,7},{7,6},{8,9},{9,8},{10,11... | collective-permute-start | bytes 1327112 | tf_op jit(solution)/shard_map/ppermute | solution.py:446
  29.4 9.6 %copy-start = (bf16[9,256,256]{2,1,0:T(8,128)(2,1)S(1)}, bf16[9,256,256]{2,1,0:T(8,128)(2,1)}, u32[]{:S(2)}) copy-start(bf16[9,256,256]{2,1,0:T(8,128)(2,1)} %param.13) | copy-start | bytes 3538948
  29.4 9.5 %collective-permute-start.1 = (bf16[18,32,256]{2,1,0:T(8,128)(2,1)S(1)}, bf16[18,32,256]{2,1,0:T(8,128)(2,1)S(1)}, u32[]{:S(2)}, u32[]{:S(2)}) collective-permute-start(bf16[18,32,256]{2,1,0:T(8,128)(2,1)S(1)} %shard_map.73.refs_0_.refs_1_), channel_id=1, source_target_pairs={{0,1},{1,0},{2,4},{3,5},{4,2},{5,3},{6,8},{7,9},{8,6},{9,7},{10,12... | collective-permute-start | bytes 884744 | tf_op jit(solution)/shard_map/ppermute | solution.py:431
  34.4 11.2 %collective-permute-start.5 = (bf16[18,32,256]{2,1,0:T(8,128)(2,1)S(1)}, bf16[18,32,256]{2,1,0:T(8,128)(2,1)S(1)}, u32[]{:S(2)}, u32[]{:S(2)}) collective-permute-start(bf16[18,32,256]{2,1,0:T(8,128)(2,1)S(1)} %shard_map.75.refs_3_), channel_id=1, source_target_pairs={{0,2},{1,3},{2,0},{3,1},{4,6},{5,7},{6,4},{7,5},{8,10},{9,11},{10,... | collective-permute-start | bytes 884744 | tf_op jit(solution)/shard_map/ppermute | solution.py:431
  34.5 8.3 %collective-permute-start.4 = (bf16[18,16,256]{2,1,0:T(8,128)(2,1)S(1)}, bf16[18,16,256]{2,1,0:T(8,128)(2,1)S(1)}, u32[]{:S(2)}, u32[]{:S(2)}) collective-permute-start(bf16[18,16,256]{2,1,0:T(8,128)(2,1)S(1)} %shard_map.77), channel_id=1, source_target_pairs={{0,1},{1,0},{2,3},{3,2},{4,5},{5,4},{6,7},{7,6},{8,9},{9,8},{10,11... | collective-permute-start | bytes 442376 | tf_op jit(solution)/shard_map/ppermute | solution.py:446
